TPU v7x, 32 devices: a whole 2x2x4 slice. The times are simulated.
32 devices in a mesh: groups: 16 (over z, y, x), batch: 2 (over core).
Axes of the slice: x: 2, y: 2, z: 4, core: 2. Of those that a mesh axis runs over, the one named last changes fastest.
Arguments:
- frames: bfloat16 [32, 1024, 1024], P(('groups', 'batch')), may hold values from -6 to 6
- time_embed: bfloat16 [32, 1024], P(('groups', 'batch')), may hold values from -6 to 6
- lengths: int32 [32], P(('groups', 'batch')), may hold values from 512 to 1024, as said below
- mod_weight: bfloat16 [1024, 6144], replicated, may hold values from -0.1875 to 0.1875
- mod_bias: bfloat16 [6144], replicated, may hold values from -3 to 3
- qkv_weight: bfloat16 [1024, 3072], replicated, may hold values from -0.1875 to 0.1875
- qkv_bias: bfloat16 [3072], replicated, may hold values from -2 to 2
- out_weight: bfloat16 [1024, 1024], replicated, may hold values from -1.5 to 1.5
- out_bias: bfloat16 [1024], replicated, may hold values from -2 to 2
- up_weight: bfloat16 [1024, 2048], replicated, may hold values from -0.1875 to 0.1875
- up_bias: bfloat16 [2048], replicated, may hold values from -2 to 2
- down_weight: bfloat16 [2048, 1024], replicated, may hold values from -0.125 to 0.125
- down_bias: bfloat16 [1024], replicated, may hold values from -2 to 2
- cotangent: bfloat16 [32, 1024, 1024], P(('groups', 'batch')), may hold values from -6 to 6
Outputs:
- frames_out: bfloat16 [32, 1024, 1024], P(('groups', 'batch'))
- frames_grad: float32 [32, 1024, 1024], P(('groups', 'batch'))
- time_grad: float32 [32, 1024], P(('groups', 'batch'))
- mod_weight_grad: float32 [1024, 6144], P('groups')
- mod_bias_grad: float32 [6144], P('groups')
- qkv_weight_grad: float32 [1024, 3072], P('groups')
- qkv_bias_grad: float32 [3072], P('groups')
- out_weight_grad: float32 [1024, 1024], P('groups')
- out_bias_grad: float32 [1024], P('groups')
- up_weight_grad: float32 [1024, 2048], P('groups')
- up_bias_grad: float32 [2048], P('groups')
- down_weight_grad: float32 [2048, 1024], P('groups')
- down_bias_grad: float32 [1024], P('groups')
Inputs may be any that keep to these rules, and one draw needn't show every extreme that they name: `lengths`: in every draw some clip has exactly 1024 frames and some other exactly 512; most clips are far shorter than 1024.
All inputs are finite; a program needn't handle non-finite values.
Results may differ from a plain program's by a relative error of at most 0.02.
The roundings to bfloat16 on the way count: a program that leaves them out, or rounds other values in their place, can miss the bound.
Values may be sent and summed in bfloat16 or wider, within the bound.
A program may use at most 320 MiB of HBM per device.

v0:
```python
from functools import partial

import jax
import jax.numpy as jnp
from jax import lax
from jax.sharding import PartitionSpec as P

HEADS = 16


norm_eps = 1e-06
neg_fill = -1e30


def norm_modulate(values, scale, shift):
    centred = values - jnp.mean(values, axis=-1, keepdims=True)
    spread = jnp.mean(centred * centred, axis=-1, keepdims=True)
    return centred * lax.rsqrt(spread + norm_eps) * (1.0 + scale) + shift


def rotary_tables(slots, head_size):
    positions = jnp.arange(slots).astype(jnp.float32)[:, None]
    pair_index = jnp.arange(head_size // 2).astype(jnp.float32)[None, :]
    angles = positions * jnp.power(10000.0, -2.0 * pair_index / head_size)
    return (jnp.cos(angles)[:, None, :], jnp.sin(angles)[:, None, :])


def rotate(values, cosine, sine):
    pairs = values.reshape(values.shape[:-1] + (values.shape[-1] // 2, 2))
    first = pairs[..., 0]
    second = pairs[..., 1]
    turned = jnp.stack([first * cosine - second * sine, second * cosine + first * sine], axis=-1)
    return turned.reshape(values.shape)


def contract_rows(left, right):
    return lax.dot_general(
        left, right, (((0,), (0,)), ((), ())), preferred_element_type=jnp.float32
    )


def contract_cols(left, right):
    return lax.dot_general(
        left, right, (((1,), (1,)), ((), ())), preferred_element_type=jnp.float32
    )


def block_scores(query_block, keys, length):
    slots = keys.shape[0]
    scores = jnp.einsum(
        "qhd,khd->hqk", query_block, keys, preferred_element_type=jnp.float32
    ) * keys.shape[-1] ** (-0.5)
    slot_valid = jnp.arange(slots) < length
    return jnp.where(slot_valid[None, None, :], scores, neg_fill)


def attend_forward(packed):
    queries, keys, values, length = packed
    slots, heads, head_size = queries.shape
    block = min(slots, 512)

    def one_block(query_block):
        scores = block_scores(query_block, keys, length)
        largest = jnp.max(scores, axis=-1, keepdims=True)
        expd = jnp.exp(scores - largest)
        total = jnp.sum(expd, axis=-1, keepdims=True)
        probs_low = (expd / total).astype(jnp.bfloat16)
        mixed = jnp.einsum("hqk,khd->qhd", probs_low, values, preferred_element_type=jnp.float32)
        return (mixed.astype(jnp.bfloat16), (largest + jnp.log(total))[..., 0])

    mixed, log_total = lax.map(one_block, queries.reshape(slots // block, block, heads, head_size))
    return (mixed.reshape(slots, heads, head_size), log_total)


def attend_backward(packed):
    queries, keys, values, length, mixed_grad, log_total = packed
    slots, heads, head_size = queries.shape
    block = min(slots, 512)
    scale = head_size ** (-0.5)

    def one_block(carry, inputs):
        key_acc, value_acc = carry
        query_block, grad_block, lse_block = inputs
        scores = block_scores(query_block, keys, length)
        probs = jnp.exp(scores - lse_block[..., None])
        value_acc = value_acc + jnp.einsum(
            "hqk,qhd->khd",
            probs.astype(jnp.bfloat16),
            grad_block,
            preferred_element_type=jnp.float32,
        )
        prob_grad = jnp.einsum(
            "qhd,khd->hqk", grad_block, values, preferred_element_type=jnp.float32
        )
        inner = jnp.sum(probs * prob_grad, axis=-1, keepdims=True)
        score_grad = (probs * (prob_grad - inner)).astype(jnp.bfloat16)
        query_grad = (
            jnp.einsum("hqk,khd->qhd", score_grad, keys, preferred_element_type=jnp.float32) * scale
        )
        key_acc = (
            key_acc
            + jnp.einsum(
                "hqk,qhd->khd", score_grad, query_block, preferred_element_type=jnp.float32
            )
            * scale
        )
        return ((key_acc, value_acc), query_grad)

    zeros_kv = jnp.zeros((slots, heads, head_size), jnp.float32)
    blocks = slots // block
    (key_grad, value_grad), query_grad = lax.scan(
        one_block,
        (zeros_kv, zeros_kv),
        (
            queries.reshape(blocks, block, heads, head_size),
            mixed_grad.reshape(blocks, block, heads, head_size),
            log_total,
        ),
    )
    return (query_grad.reshape(slots, heads, head_size), key_grad, value_grad)


def body(
    frames,
    time_embed,
    lengths,
    mod_weight,
    mod_bias,
    qkv_weight,
    qkv_bias,
    out_weight,
    out_bias,
    up_weight,
    up_bias,
    down_weight,
    down_bias,
    cotangent,
):
    items, slots, width = frames.shape
    heads = HEADS
    head_size = width // heads
    tokens = items * slots
    inputs = frames.astype(jnp.float32)
    embed_low = jax.nn.silu(time_embed.astype(jnp.float32)).astype(jnp.bfloat16)
    modulation = jnp.dot(
        embed_low, mod_weight, preferred_element_type=jnp.float32
    ) + mod_bias.astype(jnp.float32)
    shift_one = modulation[:, None, 0 * width : 1 * width]
    scale_one = modulation[:, None, 1 * width : 2 * width]
    gate_one = modulation[:, None, 2 * width : 3 * width]
    shift_two = modulation[:, None, 3 * width : 4 * width]
    scale_two = modulation[:, None, 4 * width : 5 * width]
    gate_two = modulation[:, None, 5 * width : 6 * width]
    hidden_one = (
        norm_modulate(inputs, scale_one, shift_one).astype(jnp.bfloat16).reshape(tokens, width)
    )
    qkv_all = jnp.dot(hidden_one, qkv_weight, preferred_element_type=jnp.float32) + qkv_bias.astype(
        jnp.float32
    )
    qkv_all = qkv_all.reshape(items, slots, 3, heads, head_size)
    cosine, sine = rotary_tables(slots, head_size)
    queries = rotate(qkv_all[:, :, 0], cosine, sine).astype(jnp.bfloat16)
    keys_rot = rotate(qkv_all[:, :, 1], cosine, sine).astype(jnp.bfloat16)
    values_low = qkv_all[:, :, 2].astype(jnp.bfloat16)
    mixed, log_total = lax.map(attend_forward, (queries, keys_rot, values_low, lengths))
    mixed_flat = mixed.reshape(tokens, width)
    row_valid = (jnp.arange(slots)[None, :] < lengths[:, None])[..., None]
    attn_full = (
        jnp.dot(mixed_flat, out_weight, preferred_element_type=jnp.float32)
        + out_bias.astype(jnp.float32)
    ).reshape(items, slots, width)
    attn_out = jnp.where(row_valid, attn_full, 0.0)
    middle = inputs + gate_one * attn_out
    hidden_two = (
        norm_modulate(middle, scale_two, shift_two).astype(jnp.bfloat16).reshape(tokens, width)
    )
    upper = jnp.dot(hidden_two, up_weight, preferred_element_type=jnp.float32) + up_bias.astype(
        jnp.float32
    )
    activ_low = jax.nn.gelu(upper, approximate=True).astype(jnp.bfloat16)
    branch = (
        jnp.dot(activ_low, down_weight, preferred_element_type=jnp.float32)
        + down_bias.astype(jnp.float32)
    ).reshape(items, slots, width)
    result = (middle + gate_two * branch).astype(jnp.bfloat16)
    out_grad = cotangent.astype(jnp.float32)
    gate_two_grad = jnp.sum(out_grad * branch, axis=1, keepdims=True)
    branch_grad = (gate_two * out_grad).astype(jnp.bfloat16).reshape(tokens, width)
    down_w_grad = contract_rows(activ_low, branch_grad)
    down_b_grad = jnp.sum(branch_grad.astype(jnp.float32), axis=0)
    activ_grad = contract_cols(branch_grad, down_weight)
    gelu_value, gelu_back = jax.vjp(partial(jax.nn.gelu, approximate=True), upper)
    upper_grad = gelu_back(activ_grad)[0].astype(jnp.bfloat16)
    up_w_grad = contract_rows(hidden_two, upper_grad)
    up_b_grad = jnp.sum(upper_grad.astype(jnp.float32), axis=0)
    hidden_two_grad = contract_cols(upper_grad, up_weight).reshape(items, slots, width)
    norm_two_value, norm_two_back = jax.vjp(norm_modulate, middle, scale_two, shift_two)
    middle_part, scale_two_grad, shift_two_grad = norm_two_back(hidden_two_grad)
    middle_grad = out_grad + middle_part
    gate_one_grad = jnp.sum(middle_grad * attn_out, axis=1, keepdims=True)
    attn_grad = (
        jnp.where(row_valid, gate_one * middle_grad, 0.0)
        .astype(jnp.bfloat16)
        .reshape(tokens, width)
    )
    out_w_grad = contract_rows(mixed_flat, attn_grad)
    out_b_grad = jnp.sum(attn_grad.astype(jnp.float32), axis=0)
    mixed_grad = (
        contract_cols(attn_grad, out_weight)
        .astype(jnp.bfloat16)
        .reshape(items, slots, heads, head_size)
    )
    early_part = (
        lax.psum_scatter(
            down_w_grad.astype(jnp.bfloat16), "groups", scatter_dimension=0, tiled=True
        ).astype(jnp.float32),
        lax.psum_scatter(
            up_w_grad.astype(jnp.bfloat16), "groups", scatter_dimension=0, tiled=True
        ).astype(jnp.float32),
        lax.psum_scatter(
            out_w_grad.astype(jnp.bfloat16), "groups", scatter_dimension=0, tiled=True
        ).astype(jnp.float32),
        lax.psum_scatter(
            down_b_grad.astype(jnp.bfloat16), "groups", scatter_dimension=0, tiled=True
        ).astype(jnp.float32),
        lax.psum_scatter(
            up_b_grad.astype(jnp.bfloat16), "groups", scatter_dimension=0, tiled=True
        ).astype(jnp.float32),
        lax.psum_scatter(
            out_b_grad.astype(jnp.bfloat16), "groups", scatter_dimension=0, tiled=True
        ).astype(jnp.float32),
    )
    down_w_sum, up_w_sum, out_w_sum, down_b_sum, up_b_sum, out_b_sum = (
        lax.psum(early_part[0].astype(jnp.bfloat16), "batch").astype(jnp.float32),
        lax.psum(early_part[1].astype(jnp.bfloat16), "batch").astype(jnp.float32),
        lax.psum(early_part[2].astype(jnp.bfloat16), "batch").astype(jnp.float32),
        lax.psum(early_part[3].astype(jnp.bfloat16), "batch").astype(jnp.float32),
        lax.psum(early_part[4].astype(jnp.bfloat16), "batch").astype(jnp.float32),
        lax.psum(early_part[5].astype(jnp.bfloat16), "batch").astype(jnp.float32),
    )
    query_grad, key_grad, value_grad = lax.map(
        attend_backward, (queries, keys_rot, values_low, lengths, mixed_grad, log_total)
    )
    qkv_grad = jnp.stack(
        [rotate(query_grad, cosine, -sine), rotate(key_grad, cosine, -sine), value_grad], axis=2
    )
    qkv_grad = qkv_grad.astype(jnp.bfloat16).reshape(tokens, 3 * width)
    qkv_w_grad = contract_rows(hidden_one, qkv_grad)
    qkv_b_grad = jnp.sum(qkv_grad.astype(jnp.float32), axis=0)
    hidden_one_grad = contract_cols(qkv_grad, qkv_weight).reshape(items, slots, width)
    norm_one_value, norm_one_back = jax.vjp(norm_modulate, inputs, scale_one, shift_one)
    input_part, scale_one_grad, shift_one_grad = norm_one_back(hidden_one_grad)
    frames_grad = middle_grad + input_part
    mod_grad = jnp.concatenate(
        [
            shift_one_grad,
            scale_one_grad,
            gate_one_grad,
            shift_two_grad,
            scale_two_grad,
            gate_two_grad,
        ],
        axis=-1,
    )[:, 0, :]
    mod_grad = mod_grad.astype(jnp.bfloat16)
    embed_grad = contract_cols(mod_grad, mod_weight)
    silu_value, silu_back = jax.vjp(jax.nn.silu, time_embed.astype(jnp.float32))
    time_grad = silu_back(embed_grad)[0]
    late_part = (
        lax.psum_scatter(
            qkv_w_grad.astype(jnp.bfloat16), "groups", scatter_dimension=0, tiled=True
        ).astype(jnp.float32),
        lax.psum_scatter(
            qkv_b_grad.astype(jnp.bfloat16), "groups", scatter_dimension=0, tiled=True
        ).astype(jnp.float32),
    )
    qkv_w_sum, qkv_b_sum = (
        lax.psum(late_part[0].astype(jnp.bfloat16), "batch").astype(jnp.float32),
        lax.psum(late_part[1].astype(jnp.bfloat16), "batch").astype(jnp.float32),
    )
    mod_w_grad = contract_rows(embed_low, mod_grad)
    mod_b_grad = jnp.sum(mod_grad.astype(jnp.float32), axis=0)
    mod_part = (
        lax.psum_scatter(
            mod_w_grad.astype(jnp.bfloat16), "groups", scatter_dimension=0, tiled=True
        ).astype(jnp.float32),
        lax.psum_scatter(
            mod_b_grad.astype(jnp.bfloat16), "groups", scatter_dimension=0, tiled=True
        ).astype(jnp.float32),
    )
    mod_w_sum, mod_b_sum = (
        lax.psum(mod_part[0].astype(jnp.bfloat16), "batch").astype(jnp.float32),
        lax.psum(mod_part[1].astype(jnp.bfloat16), "batch").astype(jnp.float32),
    )
    return (
        result,
        frames_grad,
        time_grad,
        mod_w_sum,
        mod_b_sum,
        qkv_w_sum,
        qkv_b_sum,
        out_w_sum,
        out_b_sum,
        up_w_sum,
        up_b_sum,
        down_w_sum,
        down_b_sum,
    )


def solution(mesh):
    return jax.shard_map(
        body,
        mesh=mesh,
        in_specs=(
            P(("groups", "batch"), None, None),
            P(("groups", "batch"), None),
            P(("groups", "batch")),
            P(),
            P(),
            P(),
            P(),
            P(),
            P(),
            P(),
            P(),
            P(),
            P(),
            P(("groups", "batch"), None, None),
        ),
        out_specs=(
            P(("groups", "batch"), None, None),
            P(("groups", "batch"), None, None),
            P(("groups", "batch"), None),
            P("groups", None),
            P("groups"),
            P("groups", None),
            P("groups"),
            P("groups", None),
            P("groups"),
            P("groups", None),
            P("groups"),
            P("groups", None),
            P("groups"),
        ),
        check_vma=False,
    )
```

profile of v0, /device:TPU:0, one launch (start us, length us, event | category | flops | bytes accessed | tf_op | source)
XLA Modules:
  0.0 1086.0 jit_solution(10350748045864637171)
XLA Ops:
  24.5 12.7 %broadcast_add_fusion = f32[1024,3072]{1,0:T(8,128)} fusion(f32[3072]{0:T(1024)S(1)} %convert_element_type.282, bf16[1024,3072]{1,0:T(8,128)(2,1)} %param.23, bf16[1,1024,1024]{1,2,0:T(8,128)(2,1)S(1)} %copy-done.5, f32[1024]{0:T(1024)S(1)} %bitcast.227, f32[1024]{0:T(1024)S(1)} %bitcast.216, f32[1024]{0:T(1024)S(1)} %fusion.87, ...), kind=kOutput, calls=%fused_computation.61 | convolution fusion | flops 6451888128 | bytes 21000192 | tf_op jit(solution)/shard_map/dot_general | solution.py:157
  37.2 12.6 %copy.66 = f32[1024,3072]{0,1:T(8,128)} copy(f32[1024,3072]{1,0:T(8,128)} %broadcast_add_fusion) | data formatting | bytes 25165824 | tf_op jit(solution)/shard_map/add | solution.py:157
  92.4 92.7 %while.47 = (s32[]{:T(128)}, bf16[2,512,16,64]{1,3,2,0:T(8,128)(2,1)}, f32[2,16,512]{2,1,0:T(8,128)S(1)}, s32[]{:T(128)}, bf16[2,512,16,64]{1,3,2,0:T(8,128)(2,1...) while((s32[]{:T(128)}, bf16[2,512,16,64]{1,3,2,0:T(8,128)(2,1)}, ...), condition=%wide.region_5.6_spmd, body=%wide.region_2.5_spmd.sunk | while | flops 2248664064 | bytes 132387000 | solution.py:71
  93.2 15.2 %fusion.147 = (f32[16,512]{1,0:T(8,128)S(1)}, f32[16,512,1024]{2,1,0:T(8,128)}) fusion(pred[1024]{0:T(1024)(128)(4,1)S(1)} %iota_compare_fusion.5, bf16[1024,16,64]{0,2,1:T(8,128)(2,1)} %get-tuple-element.512, bf16[2,512,16,64]{1,3,2,0:T(8,128)(2,1)} %get-tuple-element.511, s32[]{:T(128)S(6)} %copy.116), kind=kOutput, calls=%fused_computation.3.clone.1 | convolution fusion | flops 1098899456 | bytes 36733956 | tf_op jit(solution)/shard_map/while/body/eval_jaxpr/while/body/eval_jaxpr/qhd,khd->hqk/dot_general | solution.py:50
  108.4 15.0 %fusion.148 = f32[16,512]{1,0:T(8,128)S(1)} fusion(f32[16,512,1024]{2,1,0:T(8,128)} %get-tuple-element.477, f32[16,512]{1,0:T(8,128)S(1)} %get-tuple-element.478, pred[1024]{0:T(1024)(128)(4,1)S(1)} %iota_compare_fusion.5), kind=kLoop, calls=%fused_computation.4.clone.1 | loop fusion | flops 33546240 | bytes 33620992 | tf_op jit(solution)/shard_map/while/body/eval_jaxpr/while/body/eval_jaxpr/reduce_sum | solution.py:66
  123.5 13.7 %fusion.149 = bf16[2,512,16,64]{1,3,2,0:T(8,128)(2,1)S(1)} fusion(bf16[2,512,16,64]{1,3,2,0:T(8,128)(2,1)S(1)} %copy-done.22, s32[]{:T(128)S(6)} %copy.116, bf16[1024,16,64]{0,2,1:T(8,128)(2,1)S(1)} %copy-done.4, f32[16,512,1024]{2,1,0:T(8,128)} %get-tuple-element.477, f32[16,512]{1,0:T(8,128)S(1)} %fusion.148, ...), kind=kOutput, calls=%fused_computation.8.clone.1 | convolution fusion | flops 1116209152 | bytes 36766724 | tf_op jit(solution)/shard_map/while/body/eval_jaxpr/while/body/eval_jaxpr/hqk,khd->qhd/dot_general | solution.py:68
  139.3 15.2 %fusion.147 = (f32[16,512]{1,0:T(8,128)S(1)}, f32[16,512,1024]{2,1,0:T(8,128)}) fusion(pred[1024]{0:T(1024)(128)(4,1)S(1)} %iota_compare_fusion.5, bf16[1024,16,64]{0,2,1:T(8,128)(2,1)} %get-tuple-element.512, bf16[2,512,16,64]{1,3,2,0:T(8,128)(2,1)} %get-tuple-element.511, s32[]{:T(128)S(6)} %copy.116), kind=kOutput, calls=%fused_computation.3.clone.1 | convolution fusion | flops 1098899456 | bytes 36733956 | tf_op jit(solution)/shard_map/while/body/eval_jaxpr/while/body/eval_jaxpr/qhd,khd->hqk/dot_general | solution.py:50
  154.5 15.0 %fusion.148 = f32[16,512]{1,0:T(8,128)S(1)} fusion(f32[16,512,1024]{2,1,0:T(8,128)} %get-tuple-element.477, f32[16,512]{1,0:T(8,128)S(1)} %get-tuple-element.478, pred[1024]{0:T(1024)(128)(4,1)S(1)} %iota_compare_fusion.5), kind=kLoop, calls=%fused_computation.4.clone.1 | loop fusion | flops 33546240 | bytes 33620992 | tf_op jit(solution)/shard_map/while/body/eval_jaxpr/while/body/eval_jaxpr/reduce_sum | solution.py:66
  169.5 13.7 %fusion.149 = bf16[2,512,16,64]{1,3,2,0:T(8,128)(2,1)S(1)} fusion(bf16[2,512,16,64]{1,3,2,0:T(8,128)(2,1)S(1)} %copy-done.22, s32[]{:T(128)S(6)} %copy.116, bf16[1024,16,64]{0,2,1:T(8,128)(2,1)S(1)} %copy-done.4, f32[16,512,1024]{2,1,0:T(8,128)} %get-tuple-element.477, f32[16,512]{1,0:T(8,128)S(1)} %fusion.148, ...), kind=kOutput, calls=%fused_computation.8.clone.1 | convolution fusion | flops 1116209152 | bytes 36766724 | tf_op jit(solution)/shard_map/while/body/eval_jaxpr/while/body/eval_jaxpr/hqk,khd->qhd/dot_general | solution.py:68
  203.6 12.6 %fusion.106 = (bf16[2048]{0:T(1024)(128)(2,1)}, bf16[1024,2048]{1,0:T(8,128)(2,1)}) fusion(f32[1024,2048]{1,0:T(8,128)S(1)} %fusion.95, f32[2048]{0:T(1024)S(1)} %copy-done.50, bf16[2048,1024]{1,0:T(8,128)(2,1)S(1)} %copy-done.64, bf16[1,1024,1024]{1,2,0:T(8,128)(2,1)S(1)} %copy-done.15, f32[1024]{0:T(1024)S(1)} %bitcast.221), kind=kOutput, calls=%fused_computation.173 | convolution fusion | flops 4344248320 | bytes 18890752 | tf_op jit(solution)/shard_map/dot_general | solution.py:43
  246.4 12.0 %convolution_convert_fusion.1 = bf16[2048,1024]{1,0:T(8,128)(2,1)} fusion(bf16[1,1024,1024]{1,2,0:T(8,128)(2,1)} %copy.73, f32[1024]{0:T(1024)S(1)} %bitcast.223, f32[1024,2048]{1,0:T(8,128)} %copy-done.66, f32[2048]{0:T(1024)S(1)} %copy-done.50), kind=kOutput, calls=%fused_computation.95 | convolution fusion | flops 4321181696 | bytes 14692352 | tf_op jit(solution)/shard_map/dot_general | solution.py:37
  258.5 10.2 convolution_convert_fusion.2
  286.1 296.4 %while.48 = (s32[]{:T(128)}, f32[1024,16,64]{0,2,1:T(8,128)}, f32[1024,16,64]{0,2,1:T(8,128)}, f32[2,512,16,64]{1,0,2,3:T(2,128)}, bf16[2,512,16,64]{1,3,2,0:T(8...) while((s32[]{:T(128)}, f32[1024,16,64]{0,2,1:T(8,128)}, ...), condition=%wide.region_12.13_spmd.clone, body=%wide.region_10.12_spmd.clone.sunk | while | flops 5500298240 | bytes 298029216 | solution.py:111
  287.0 14.5 %fusion.159 = f32[16,512,1024]{2,1,0:T(8,128)} fusion(bf16[1024,16,64]{0,2,1:T(8,128)(2,1)S(1)} %get-tuple-element.545, bf16[2,512,16,64]{1,3,2,0:T(8,128)(2,1)} %get-tuple-element.543, s32[]{:T(128)S(6)} %copy.126), kind=kOutput, calls=%fused_computation.30.clone.1 | convolution fusion | flops 1073741824 | bytes 36700164 | tf_op jit(solution)/shard_map/while/body/eval_jaxpr/while/body/eval_jaxpr/qhd,khd->hqk/dot_general | solution.py:50
  301.4 17.0 %bitcast_add_fusion.6 = f32[1024,16,64]{0,2,1:T(8,128)} fusion(f32[1024,16,64]{0,2,1:T(8,128)} %get-tuple-element.529, f32[16,512,1024]{2,1,0:T(8,128)} %fusion.159, f32[16,512]{1,0:T(8,128)S(1)} %dynamic-slice_bitcast_fusion.2, pred[1024]{0:T(1024)(128)(4,1)S(1)} %iota_compare_fusion.6, pred[]{:T(512)S(6)} %compare.3, ...), kind=kOutput, calls=%fused_computation.23.clone.1 | convolution fusion | flops 1109393408 | bytes 43025412 | tf_op jit(solution)/shard_map/while/body/eval_jaxpr/while/body/eval_jaxpr/hqk,qhd->khd/dot_general | solution.py:86
  318.4 25.3 %multiply_reduce_fusion.3 = (f32[16,512]{1,0:T(8,128)S(1)}, f32[16,512,1024]{2,1,0:T(8,128)}) fusion(f32[16,512,1024]{2,1,0:T(8,128)} %fusion.159, f32[16,512]{1,0:T(8,128)S(1)} %dynamic-slice_bitcast_fusion.2, pred[1024]{0:T(1024)(128)(4,1)S(1)} %iota_compare_fusion.6, bf16[1024,16,64]{0,2,1:T(8,128)(2,1)} %get-tuple-element.548, ...), kind=kOutput, calls=%fused_computation.18.clone.1 | convolution fusion | flops 1115676672 | bytes 70321152 | tf_op jit(solution)/shard_map/while/body/eval_jaxpr/while/body/eval_jaxpr/qhd,khd->hqk/dot_general | solution.py:92
  343.7 28.3 %multiply_convert_fusion.6 = bf16[16,512,1024]{2,1,0:T(8,128)(2,1)} fusion(f32[16,512,1024]{2,1,0:T(8,128)} %get-tuple-element.489, f32[16,512,1024]{2,1,0:T(8,128)} %fusion.159, f32[16,512]{1,0:T(8,128)S(1)} %get-tuple-element.490, f32[16,512]{1,0:T(8,128)S(1)} %dynamic-slice_bitcast_fusion.2, pred[1024]{0:T(1024)(128)(4,1)S(1)} %iota_compare_fusion.6), kind=kLoop, calls=%fused_computation.17.clone.1 | loop fusion | flops 50331648 | bytes 83952640 | tf_op jit(solution)/shard_map/while/body/eval_jaxpr/while/body/eval_jaxpr/convert_element_type | solution.py:96
  372.0 8.9 multiply_bitcast_fusion.2
  380.9 10.9 %bitcast_add_fusion.5 = f32[1024,16,64]{0,2,1:T(8,128)} fusion(f32[1024,16,64]{0,2,1:T(8,128)} %get-tuple-element.528, bf16[16,512,1024]{2,1,0:T(8,128)(2,1)} %multiply_convert_fusion.6, pred[]{:T(512)S(6)} %compare.3, bf16[2,512,16,64]{1,3,2,0:T(8,128)(2,1)S(1)} %copy-done.3, s32[]{:T(128)S(6)} %copy.126), kind=kOutput, calls=%fused_computation.24.clone.1 | convolution fusion | flops 1076887552 | bytes 26214404 | tf_op jit(solution)/shard_map/while/body/eval_jaxpr/while/body/eval_jaxpr/hqk,qhd->khd/dot_general | solution.py:102
  395.4 37.6 %dynamic_update_slice.33 = f32[2,512,16,64]{1,0,2,3:T(2,128)} dynamic-update-slice(f32[2,512,16,64]{1,0,2,3:T(2,128)} %get-tuple-element.530, f32[1,512,16,64]{1,0,2,3:T(1,128)} %copy.109, s32[]{:T(128)S(6)} %copy.126, s32[]{:T(128)} %constant.110.clone.1..sunk, s32[]{:T(128)} %constant.110.clone.1..sunk, s32[]{:T(128)} %constant.110.clone.1..sunk) | dynamic-update-slice | bytes 4194308 | tf_op jit(solution)/shard_map/while/body/eval_jaxpr/while/body/jit(dynamic_update_index_in_dim)/dynamic_update_slice | solution.py:111
  433.7 14.6 %fusion.159 = f32[16,512,1024]{2,1,0:T(8,128)} fusion(bf16[1024,16,64]{0,2,1:T(8,128)(2,1)S(1)} %get-tuple-element.545, bf16[2,512,16,64]{1,3,2,0:T(8,128)(2,1)} %get-tuple-element.543, s32[]{:T(128)S(6)} %copy.126), kind=kOutput, calls=%fused_computation.30.clone.1 | convolution fusion | flops 1073741824 | bytes 36700164 | tf_op jit(solution)/shard_map/while/body/eval_jaxpr/while/body/eval_jaxpr/qhd,khd->hqk/dot_general | solution.py:50
  448.3 18.3 %bitcast_add_fusion.6 = f32[1024,16,64]{0,2,1:T(8,128)} fusion(f32[1024,16,64]{0,2,1:T(8,128)} %get-tuple-element.529, f32[16,512,1024]{2,1,0:T(8,128)} %fusion.159, f32[16,512]{1,0:T(8,128)S(1)} %dynamic-slice_bitcast_fusion.2, pred[1024]{0:T(1024)(128)(4,1)S(1)} %iota_compare_fusion.6, pred[]{:T(512)S(6)} %compare.3, ...), kind=kOutput, calls=%fused_computation.23.clone.1 | convolution fusion | flops 1109393408 | bytes 43025412 | tf_op jit(solution)/shard_map/while/body/eval_jaxpr/while/body/eval_jaxpr/hqk,qhd->khd/dot_general | solution.py:86
  466.5 25.3 %multiply_reduce_fusion.3 = (f32[16,512]{1,0:T(8,128)S(1)}, f32[16,512,1024]{2,1,0:T(8,128)}) fusion(f32[16,512,1024]{2,1,0:T(8,128)} %fusion.159, f32[16,512]{1,0:T(8,128)S(1)} %dynamic-slice_bitcast_fusion.2, pred[1024]{0:T(1024)(128)(4,1)S(1)} %iota_compare_fusion.6, bf16[1024,16,64]{0,2,1:T(8,128)(2,1)} %get-tuple-element.548, ...), kind=kOutput, calls=%fused_computation.18.clone.1 | convolution fusion | flops 1115676672 | bytes 70321152 | tf_op jit(solution)/shard_map/while/body/eval_jaxpr/while/body/eval_jaxpr/qhd,khd->hqk/dot_general | solution.py:92
  491.8 28.2 %multiply_convert_fusion.6 = bf16[16,512,1024]{2,1,0:T(8,128)(2,1)} fusion(f32[16,512,1024]{2,1,0:T(8,128)} %get-tuple-element.489, f32[16,512,1024]{2,1,0:T(8,128)} %fusion.159, f32[16,512]{1,0:T(8,128)S(1)} %get-tuple-element.490, f32[16,512]{1,0:T(8,128)S(1)} %dynamic-slice_bitcast_fusion.2, pred[1024]{0:T(1024)(128)(4,1)S(1)} %iota_compare_fusion.6), kind=kLoop, calls=%fused_computation.17.clone.1 | loop fusion | flops 50331648 | bytes 83952640 | tf_op jit(solution)/shard_map/while/body/eval_jaxpr/while/body/eval_jaxpr/convert_element_type | solution.py:96
  520.1 8.9 multiply_bitcast_fusion.2
  529.0 12.0 %bitcast_add_fusion.5 = f32[1024,16,64]{0,2,1:T(8,128)} fusion(f32[1024,16,64]{0,2,1:T(8,128)} %get-tuple-element.528, bf16[16,512,1024]{2,1,0:T(8,128)(2,1)} %multiply_convert_fusion.6, pred[]{:T(512)S(6)} %compare.3, bf16[2,512,16,64]{1,3,2,0:T(8,128)(2,1)S(1)} %copy-done.3, s32[]{:T(128)S(6)} %copy.126), kind=kOutput, calls=%fused_computation.24.clone.1 | convolution fusion | flops 1076887552 | bytes 26214404 | tf_op jit(solution)/shard_map/while/body/eval_jaxpr/while/body/eval_jaxpr/hqk,qhd->khd/dot_general | solution.py:102
  544.5 37.6 %dynamic_update_slice.33 = f32[2,512,16,64]{1,0,2,3:T(2,128)} dynamic-update-slice(f32[2,512,16,64]{1,0,2,3:T(2,128)} %get-tuple-element.530, f32[1,512,16,64]{1,0,2,3:T(1,128)} %copy.109, s32[]{:T(128)S(6)} %copy.126, s32[]{:T(128)} %constant.110.clone.1..sunk, s32[]{:T(128)} %constant.110.clone.1..sunk, s32[]{:T(128)} %constant.110.clone.1..sunk) | dynamic-update-slice | bytes 4194308 | tf_op jit(solution)/shard_map/while/body/eval_jaxpr/while/body/jit(dynamic_update_index_in_dim)/dynamic_update_slice | solution.py:111
  612.4 12.3 %fusion.104 = (bf16[1024]{0:T(1024)(128)(2,1)S(1)}, f32[1024,1024]{1,0:T(8,128)}) fusion(bf16[1024,3072]{0,1:T(8,128)(2,1)} %bitcast.206, bf16[1024,3072]{1,0:T(8,128)(2,1)} %param.23), kind=kOutput, calls=%fused_computation.171 | convolution fusion | flops 6443498496 | bytes 16779264 | tf_op jit(solution)/shard_map/dot_general | solution.py:43
  635.8 17.8 %fusion.53 = (bf16[1024]{0:T(1024)(128)(2,1)S(1)}, bf16[1024]{0:T(1024)(128)(2,1)S(1)}, f32[1,1024,1024]{1,2,0:T(8,128)}, bf16[1,1024,1024]{1,2,0:T(8,128)(2,1)}) fusion(bf16[1,1024,1024]{1,2,0:T(8,128)(2,1)} %copy.73, f32[1024]{0:T(1024)S(1)} %convert_element_type.292, f32[1024,1024]{0,1:T(8,128)} %get-tuple-element.370, f32[1024]{0:T(1024)S(1)} %copy-done.57, ...), kind=kOutput, calls=%fused_computation.78 | convolution fusion | flops 4339005440 | bytes 39896064 | tf_op jit(solution)/shard_map/dot_general | solution.py:182
  661.3 100.6 %reduce-scatter.8.cloned.1.call-done = bf16[64,3072]{1,0:T(8,128)(2,1)} async-done(((bf16[1024,3072]{1,0:T(8,128)(2,1)}), bf16[64,3072]{1,0:T(8,128)(2,1)}) %reduce-scatter.8.cloned.1.call-update) | async-done | bytes 393232 | tf_op jit(solution)/shard_map/reduce_scatter | solution.py:270
  761.9 207.3 %reduce-scatter.6.cloned.1.call-done = bf16[64,6144]{1,0:T(8,128)(2,1)} async-done(((bf16[1024,6144]{1,0:T(8,128)(2,1)}), bf16[64,6144]{1,0:T(8,128)(2,1)}) %reduce-scatter.6.cloned.1.call-update) | async-done | bytes 786448 | tf_op jit(solution)/shard_map/reduce_scatter | solution.py:284
  978.2 75.4 %all-reduce.5 = (bf16[6144]{0:T(1024)(128)(2,1)S(1)}, bf16[3072]{0:T(1024)(128)(2,1)S(1)}, bf16[1024]{0:T(1024)(128)(2,1)S(1)}, bf16[2048]{0:T(1024)(128)(2,1)S(1)}, bf16[1024]{0:T(1024)(128)(2,1)S(1)}) all-reduce(bf16[6144]{0:T(1024)(128)(2,1)S(1)} %reduce.24, ...), channel_id=3, replica_groups=mesh['groups'=16,'batch'=2] {'groups'}, use_global_device_ids=true, to_apply=%region_23.24.clone | all-reduce | flops 13312 | bytes 53248
  (269 shorter events, 217.5 us)
Async XLA Ops:
  7.2 182.4 %copy-start = (bf16[1024,1024]{1,0:T(8,128)(2,1)S(1)}, bf16[1024,1024]{1,0:T(8,128)(2,1)}, u32[]{:S(2)}) copy-start(bf16[1024,1024]{1,0:T(8,128)(2,1)} %param.25) | copy-start | bytes 6291460
  7.2 654.1 %reduce-scatter.10.cloned.1.call-start = ((), (), s32[]{:S(2)}) async-start(), calls=%async_computation.7 | async-start | bytes 2228224 | tf_op jit(solution)/shard_map/reduce_scatter | solution.py:220
  8.1 6.3 copy-start.46
  15.1 8.8 copy-start.38
  15.1 8.9 copy-start.53
  19.0 5.5 copy-start.5
  53.7 9.7 copy-start.59
  53.8 10.3 copy-start.52
  108.4 15.1 %copy-start.4 = (bf16[1024,16,64]{0,2,1:T(8,128)(2,1)S(1)}, bf16[1024,16,64]{0,2,1:T(8,128)(2,1)}, u32[]{:S(2)}) copy-start(bf16[1024,16,64]{0,2,1:T(8,128)(2,1)} %get-tuple-element.513) | copy-start | bytes 6291460 | tf_op jit(solution)/shard_map/while/body/eval_jaxpr/while
  108.4 15.1 %copy-start.22 = (bf16[2,512,16,64]{1,3,2,0:T(8,128)(2,1)S(1)}, bf16[2,512,16,64]{1,3,2,0:T(8,128)(2,1)}, u32[]{:S(2)}) copy-start(bf16[2,512,16,64]{1,3,2,0:T(8,128)(2,1)} %get-tuple-element.500) | copy-start | bytes 6291460 | tf_op jit(solution)/shard_map/while/body/eval_jaxpr/while
  154.5 15.1 %copy-start.4 = (bf16[1024,16,64]{0,2,1:T(8,128)(2,1)S(1)}, bf16[1024,16,64]{0,2,1:T(8,128)(2,1)}, u32[]{:S(2)}) copy-start(bf16[1024,16,64]{0,2,1:T(8,128)(2,1)} %get-tuple-element.513) | copy-start | bytes 6291460 | tf_op jit(solution)/shard_map/while/body/eval_jaxpr/while
  154.5 15.1 %copy-start.22 = (bf16[2,512,16,64]{1,3,2,0:T(8,128)(2,1)S(1)}, bf16[2,512,16,64]{1,3,2,0:T(8,128)(2,1)}, u32[]{:S(2)}) copy-start(bf16[2,512,16,64]{1,3,2,0:T(8,128)(2,1)} %get-tuple-element.500) | copy-start | bytes 6291460 | tf_op jit(solution)/shard_map/while/body/eval_jaxpr/while
  194.7 8.8 copy-start.8
  203.6 12.6 %copy-start.66 = (f32[1024,2048]{1,0:T(8,128)}, f32[1024,2048]{1,0:T(8,128)S(1)}, u32[]{:S(2)}) copy-start(f32[1024,2048]{1,0:T(8,128)S(1)} %fusion.95) | copy-start | bytes 25165828
  230.5 5.9 copy-start.10
  246.3 415.0 %reduce-scatter.14.cloned.1.call-start = ((), (), s32[]{:S(2)}) async-start(), calls=%async_computation.9 | async-start | bytes 4456448 | tf_op jit(solution)/shard_map/reduce_scatter | solution.py:214
  258.4 402.9 %reduce-scatter.12.cloned.1.call-start = ((), (), s32[]{:S(2)}) async-start(), calls=%async_computation.8 | async-start | bytes 4456448 | tf_op jit(solution)/shard_map/reduce_scatter | solution.py:217
  268.7 493.2 %reduce-scatter.8.cloned.1.call-start = ((), (), s32[]{:S(2)}) async-start(), calls=%async_computation.6 | async-start | bytes 6684672 | tf_op jit(solution)/shard_map/reduce_scatter | solution.py:270
  280.5 5.6 copy-start.2
  372.0 8.9 copy-start.3
  520.1 8.9 copy-start.3
  611.7 357.5 %reduce-scatter.6.cloned.1.call-start = ((), (), s32[]{:S(2)}) async-start(), calls=%async_computation.5 | async-start | bytes 13369344 | tf_op jit(solution)/shard_map/reduce_scatter | solution.py:284
  635.8 17.8 %copy-start.49 = (bf16[1024]{0:T(1024)(128)(2,1)S(1)}, bf16[1024]{0:T(1024)(128)(2,1)}, u32[]{:S(2)}) copy-start(bf16[1024]{0:T(1024)(128)(2,1)} %get-tuple-element.373) | copy-start | bytes 6148
  635.8 17.8 %copy-start.40 = (bf16[1024]{0:T(1024)(128)(2,1)S(1)}, bf16[1024]{0:T(1024)(128)(2,1)}, u32[]{:S(2)}) copy-start(bf16[1024]{0:T(1024)(128)(2,1)} %get-tuple-element.277) | copy-start | bytes 6148
  661.2 308.1 %copy-start.65 = (u32[32]{0:T(128)S(1)}, u32[32]{0:T(128)}, u32[]{:S(2)}) copy-start(u32[32]{0:T(128)} %constant.129) | copy-start | bytes 388
  661.2 409.1 %all-reduce.10.cloned.1.call-start = ((), (), s32[]{:S(2)}) async-start(), calls=%async_computation.10 | async-start | bytes 3670016 | tf_op jit(solution)/shard_map/psum | solution.py:292
  972.5 5.7 copy-start.47
  972.5 5.7 copy-start.48
  972.6 5.7 copy-start.58
  972.6 86.6 %copy-start.21 = (bf16[1,1024,1024]{1,2,0:T(8,128)(2,1)S(1)}, bf16[1,1024,1024]{1,2,0:T(8,128)(2,1)}, u32[]{:S(2)}) copy-start(bf16[1,1024,1024]{1,2,0:T(8,128)(2,1)} %get-tuple-element.355) | copy-start | bytes 6291460
  1061.7 17.2 %copy-start.1 = (bf16[1024,1024]{1,0:T(8,128)(2,1)S(1)}, bf16[1024,1024]{1,0:T(8,128)(2,1)}, u32[]{:S(2)}) copy-start(bf16[1024,1024]{1,0:T(8,128)(2,1)} %param.25) | copy-start | bytes 6291460
  1070.4 7.6 copy-start.29
  (45 other events, 146.1 us)
Sparse Core Ops, SparseCore 0:
  246.5 84.0 reduce-scatter.9
  332.9 91.9 reduce-scatter.13
  427.2 94.7 reduce-scatter.11
  611.8 150.0 reduce-scatter.7
  767.4 201.7 reduce-scatter.5
  971.8 20.7 all-reduce.9
where the time goes:
time: 1100 us; the launch traced here: 1090 us
  matrix products  343 us (31%)
  waiting for transfers between devices  308 us (28%)
  local copies, waits for them, and re-layouts  198 us (18%)
  other arithmetic  139 us (13%)
  blocking collectives  77.8 us (7%)
  between operations  18.4 us (2%)
    reduce_scatter x1, waiting for transfers between devices, body(): lax.psum_scatter(mod_w_grad.astype(jnp.bfloat16), 'groups', scatter_dimen...  207 us
    reduce_scatter x1, waiting for transfers between devices, body(): lax.psum_scatter(qkv_w_grad.astype(jnp.bfloat16), 'groups', scatter_dimen...  101 us
    dynamic_update_slice x4, local copies, waits for them, and re-layouts, attend_backward(): lax.scan(one_block, (zeros_kv, zeros_kv), (queries.reshape(blocks, block,...  82.2 us
    unnamed x1, blocking collectives  75.4 us
    dot_general x4, matrix products, block_scores(): jnp.einsum('qhd,khd->hqk', query_block, keys, preferred_element_type=jnp....  59.5 us
    convert_element_type x2, other arithmetic, one_block(): score_grad = (probs * (prob_grad - inner)).astype(jnp.bfloat16)  56.5 us
    dot_general x2, matrix products, one_block(): jnp.einsum('qhd,khd->hqk', grad_block, values, preferred_element_type=jnp...  50.6 us
    dot_general x5, matrix products, contract_cols(): lax.dot_general(left, right, (((1,), (1,)), ((), ())), preferred_element_...  47.8 us
  transfers between devices with their start and end apart: 6, of which 2 were waited for; matrix products, arithmetic and copies ran while one was open for 40% of the time, Pallas kernels for 0%

commit v1 on v0

v1 whole, which is shorter than its diff:
```python
import jax, jax.numpy as jnp
import numpy as np
from jax import lax
from jax.experimental import pallas as pl
from jax.experimental.pallas import tpu as pltpu
from jax.sharding import PartitionSpec as P

f32 = jnp.float32
bf16 = jnp.bfloat16
HEADS = 16
LOG2E = 1.4426950408889634
EPS = 1e-6
NN = ((1,), (0,))
NT = ((1,), (1,))
TN = ((0,), (0,))
VMEM_LIMIT = 62 * 2**20


def mm(a, b, dims):
    return lax.dot_general(a, b, (dims, ((), ())), preferred_element_type=f32)


def params(**kw):
    return pltpu.CompilerParams(vmem_limit_bytes=VMEM_LIMIT, **kw)


def rot_tables(slots, size):
    pos = np.arange(slots, dtype=np.float64)[:, None]
    pair = np.arange(size // 2, dtype=np.float64)[None, :]
    ang = pos * np.power(10000.0, -2.0 * pair / size)
    cos = np.repeat(np.cos(ang), 2, axis=1)
    sin = np.repeat(np.sin(ang), 2, axis=1) * np.where(np.arange(size) % 2 == 0, -1.0, 1.0)
    return np.tile(cos, (1, 2)).astype(np.float32), np.tile(sin, (1, 2)).astype(np.float32)


def turn(x, cos, sin, even):
    swapped = jnp.where(even, pltpu.roll(x, 127, 1), pltpu.roll(x, 1, 1))
    return x * cos + swapped * sin


def even_lanes(rows):
    return lax.broadcasted_iota(jnp.int32, (rows, 128), 1) % 2 == 0


def full(shape):
    return pl.BlockSpec(shape, lambda *_: (0,) * len(shape), pipeline_mode=pl.Buffered(1))


def mod_kernel(te_ref, w_ref, b_ref, out_ref):
    t = te_ref[...].astype(f32)
    embed = (t * jax.nn.sigmoid(t)).astype(bf16)
    embed = jnp.broadcast_to(embed, (8, embed.shape[1]))
    out_ref[...] = mm(embed, w_ref[...], NN)[:1] + b_ref[...].astype(f32)


def modulation(te, w, b):
    d, n = w.shape
    blk = d
    return pl.pallas_call(
        mod_kernel,
        grid=(n // blk,),
        in_specs=[full((1, d)), pl.BlockSpec((d, blk), lambda i: (0, i)), pl.BlockSpec((1, blk), lambda i: (0, i))],
        out_specs=pl.BlockSpec((1, blk), lambda i: (0, i)),
        out_shape=jax.ShapeDtypeStruct((1, n), f32),
        compiler_params=params(),
        name="modulation",
    )(te, w, b)


def qkv_kernel(x_ref, mod_ref, w_ref, b_ref, cos_ref, sin_ref, h_ref, qkv_ref):
    d = x_ref.shape[1]
    x = x_ref[...].astype(f32)
    c = x - jnp.mean(x, axis=1, keepdims=True)
    r = lax.rsqrt(jnp.mean(c * c, axis=1, keepdims=True) + EPS)
    h = (c * r * (1.0 + mod_ref[:, d : 2 * d]) + mod_ref[:, :d]).astype(bf16)
    h_ref[...] = h
    cos, sin = cos_ref[...], sin_ref[...]
    even = even_lanes(x.shape[0])
    step = 512
    for n in range(0, 3 * d, step):
        y = mm(h, w_ref[:, n : n + step], NN) + b_ref[:, n : n + step].astype(f32)
        for t in range(0, step, 128):
            col = n + t
            z = y[:, t : t + 128]
            if col < 2 * d:
                z = turn(z, cos, sin, even)
            if col < d:
                z = z * 0.125
            qkv_ref[:, col : col + 128] = z.astype(bf16)


def project_qkv(x, mod, w, b, cos, sin, tile=256):
    slots, d = x.shape
    row = lambda n: pl.BlockSpec((tile, n), lambda i: (i, 0))
    return pl.pallas_call(
        qkv_kernel,
        grid=(slots // tile,),
        in_specs=[row(d), full(mod.shape), full(w.shape), full(b.shape), row(128), row(128)],
        out_specs=[row(d), row(3 * d)],
        out_shape=[jax.ShapeDtypeStruct((slots, d), bf16), jax.ShapeDtypeStruct((slots, 3 * d), bf16)],
        compiler_params=params(),
        name="project_qkv",
    )(x, mod, w, b, cos, sin)


def attend_kernel(len_ref, q_ref, k_ref, v_ref, o_ref, e_ref, linv_ref, *, rows_at_once):
    slots = q_ref.shape[0]
    lane = lax.broadcasted_iota(jnp.int32, (1, 128), 1)
    ones = jnp.where(lax.broadcasted_iota(jnp.int32, (slots, 128), 1) == 0, 1.0, 0.0).astype(bf16)
    k = k_ref[...]
    v = jnp.concatenate([v_ref[...], ones], axis=1)
    valid = lax.broadcasted_iota(jnp.int32, (1, slots), 1) < len_ref[0]
    for at in range(0, slots, rows_at_once):
        rows = pl.ds(at, rows_at_once)
        q = q_ref[rows, :]
        outs, invs = [], []
        for h in range(2):
            qh = jnp.where(lane < 64 if h == 0 else lane >= 64, q, jnp.zeros_like(q))
            s = jnp.where(valid, mm(qh, k, NT), -1e30)
            m = jnp.max(s, axis=1, keepdims=True)
            e = jnp.exp2((s - m) * LOG2E).astype(bf16)
            e_ref[h, rows, :] = e
            r = mm(e, v, NN)
            inv = 1.0 / r[:, 128:129]
            outs.append(r[:, :128] * inv)
            invs.append(inv)
        o_ref[rows, :] = jnp.where(lane < 64, outs[0], outs[1]).astype(bf16)
        linv_ref[rows, :] = jnp.where(lane < 64, invs[0], invs[1])


def attend(length, qkv, rows_at_once=128):
    slots, d = qkv.shape[0], qkv.shape[1] // 3
    pairs = d // 128
    col = lambda off: pl.BlockSpec((slots, 128), lambda i, n: (0, off + i))
    return pl.pallas_call(
        lambda *a: attend_kernel(*a, rows_at_once=rows_at_once),
        grid_spec=pltpu.PrefetchScalarGridSpec(
            num_scalar_prefetch=1,
            grid=(pairs,),
            in_specs=[col(0), col(pairs), col(2 * pairs)],
            out_specs=[col(0), pl.BlockSpec((2, slots, slots), lambda i, n: (i, 0, 0)), col(0)],
        ),
        out_shape=[
            jax.ShapeDtypeStruct((slots, d), bf16),
            jax.ShapeDtypeStruct((2 * pairs, slots, slots), bf16),
            jax.ShapeDtypeStruct((slots, d), f32),
        ],
        compiler_params=params(),
        name="attend",
    )(length, qkv, qkv, qkv)


def middle_kernel(
    len_ref, mixed_ref, x_ref, cot_ref, mod_ref, linv_ref, ow_ref, ob_ref, uw_ref, ub_ref, dw_ref, db_ref,
    out_ref, h2_ref, act_ref, dbr_ref, dup_ref, dat_ref, dmix_ref, dmid_ref, dmod_ref,
):
    i = pl.program_id(0)
    tile, d = x_ref.shape
    mod = lambda k: mod_ref[:, k * d : (k + 1) * d]
    gate1, shift2, scale2, gate2 = mod(2), mod(3), mod(4), mod(5)
    slot = lax.broadcasted_iota(jnp.int32, (tile, 1), 0) + i * tile
    valid = slot < len_ref[0]
    attn = jnp.where(valid, mm(mixed_ref[...], ow_ref[...], NN) + ob_ref[...].astype(f32), 0.0)
    mid = x_ref[...].astype(f32) + gate1 * attn
    c = mid - jnp.mean(mid, axis=1, keepdims=True)
    r2 = lax.rsqrt(jnp.mean(c * c, axis=1, keepdims=True) + EPS)
    n2 = c * r2
    h2 = (n2 * (1.0 + scale2) + shift2).astype(bf16)
    h2_ref[...] = h2
    cot = cot_ref[...].astype(f32)
    dbr = (gate2 * cot).astype(bf16)
    dbr_ref[...] = dbr
    ff = uw_ref.shape[1]
    step = 512
    for n in range(0, ff, step):
        u = mm(h2, uw_ref[:, n : n + step], NN) + ub_ref[:, n : n + step].astype(f32)
        c0 = 0.7978845608028654
        th = jnp.tanh(c0 * (u + 0.044715 * u * u * u))
        half = 0.5 * (1.0 + th)
        act_ref[:, n : n + step] = (u * half).astype(bf16)
        grad = half + 0.5 * u * (1.0 - th * th) * (c0 * (1.0 + 3.0 * 0.044715 * u * u))
        da = mm(dbr, dw_ref[n : n + step, :], NT)
        dup_ref[:, n : n + step] = (da * grad).astype(bf16)
    branch = mm(act_ref[...], dw_ref[...], NN) + db_ref[...].astype(f32)
    out_ref[...] = (mid + gate2 * branch).astype(bf16)
    dgate2 = jnp.sum(cot * branch, axis=0, keepdims=True)
    dh2 = mm(dup_ref[...], uw_ref[...], NT)
    dscale2 = jnp.sum(dh2 * n2, axis=0, keepdims=True)
    dshift2 = jnp.sum(dh2, axis=0, keepdims=True)
    dn2 = dh2 * (1.0 + scale2)
    dmid = cot + r2 * (
        dn2 - jnp.mean(dn2, axis=1, keepdims=True) - n2 * jnp.mean(dn2 * n2, axis=1, keepdims=True)
    )
    dmid_ref[...] = dmid
    dgate1 = jnp.sum(dmid * attn, axis=0, keepdims=True)
    dat = jnp.where(valid, gate1 * dmid, 0.0).astype(bf16)
    dat_ref[...] = dat
    dmix_ref[...] = (mm(dat, ow_ref[...], NT) * linv_ref[...]).astype(bf16)
    part = jnp.concatenate([dgate1, dshift2, dscale2, dgate2], axis=1)

    @pl.when(i == 0)
    def _():
        dmod_ref[...] = part

    @pl.when(i > 0)
    def _():
        dmod_ref[...] += part


def middle_part(length, mixed, x, cot, mod, linv, ow, ob, uw, ub, dw, db, tile=256):
    slots, d = x.shape
    ff = uw.shape[1]
    row = lambda n: pl.BlockSpec((tile, n), lambda i, n_: (i, 0))
    S = jax.ShapeDtypeStruct
    return pl.pallas_call(
        middle_kernel,
        grid_spec=pltpu.PrefetchScalarGridSpec(
            num_scalar_prefetch=1,
            grid=(slots // tile,),
            in_specs=[row(d), row(d), row(d), full(mod.shape), row(d), full(ow.shape), full(ob.shape),
                      full(uw.shape), full(ub.shape), full(dw.shape), full(db.shape)],
            out_specs=[row(d), row(d), row(ff), row(d), row(ff), row(d), row(d), row(d),
                       pl.BlockSpec((1, 4 * d), lambda i, n_: (0, 0))],
        ),
        out_shape=[S((slots, d), bf16), S((slots, d), bf16), S((slots, ff), bf16), S((slots, d), bf16),
                   S((slots, ff), bf16), S((slots, d), bf16), S((slots, d), bf16), S((slots, d), f32),
                   S((1, 4 * d), f32)],
        compiler_params=params(),
        name="middle_part",
    )(length, mixed, x, cot, mod, linv, ow, ob, uw, ub, dw, db)


def wgrad_kernel(l_ref, r_ref, w_ref, b_ref):
    w_ref[...] = mm(l_ref[...], r_ref[...], TN).astype(bf16)

    @pl.when(pl.program_id(0) == 0)
    def _():
        b_ref[...] = jnp.sum(r_ref[...].astype(f32), axis=0, keepdims=True)


def wgrad(left, right, tile=256):
    slots, m = left.shape
    n = right.shape[1]
    return pl.pallas_call(
        wgrad_kernel,
        grid=(m // tile,),
        in_specs=[pl.BlockSpec((slots, tile), lambda i: (0, i)), full((slots, n))],
        out_specs=[pl.BlockSpec((tile, n), lambda i: (i, 0)), pl.BlockSpec((1, n), lambda i: (0, 0))],
        out_shape=[jax.ShapeDtypeStruct((m, n), bf16), jax.ShapeDtypeStruct((1, n), f32)],
        compiler_params=params(),
        name="wgrad",
    )(left, right)


def attend_back_kernel(q_ref, k_ref, v_ref, o_ref, do_ref, e_ref, cos_ref, sin_ref, dq_ref, dk_ref, dv_ref, ds_ref, *, rows_at_once):
    slots = q_ref.shape[0]
    lane = lax.broadcasted_iota(jnp.int32, (1, 128), 1)
    q, k, v, do = q_ref[...], k_ref[...], v_ref[...], do_ref[...]
    dqs = []
    for h in range(2):
        mine = lane < 64 if h == 0 else lane >= 64
        parts = []
        for at in range(0, slots, rows_at_once):
            rows = pl.ds(at, rows_at_once)
            d = do_ref[rows, :]
            d = jnp.where(mine, d, jnp.zeros_like(d))
            inner = jnp.sum(d.astype(f32) * o_ref[rows, :].astype(f32), axis=1, keepdims=True)
            ds = (e_ref[h, rows, :].astype(f32) * (mm(d, v, NT) - inner)).astype(bf16)
            ds_ref[h, rows, :] = ds
            parts.append(mm(ds, k, NN))
        dqs.append(jnp.concatenate(parts, axis=0))
    do_t, q_t = do.T, q.T
    dv = jnp.concatenate([mm(do_t[h * 64 : h * 64 + 64], e_ref[h], NN) for h in range(2)], axis=0)
    dk = jnp.concatenate([mm(q_t[h * 64 : h * 64 + 64], ds_ref[h], NN) for h in range(2)], axis=0)
    cos, sin = cos_ref[...], -sin_ref[...]
    even = even_lanes(slots)
    dq = jnp.where(lane < 64, dqs[0], dqs[1]) * 0.125
    dq_ref[...] = turn(dq, cos, sin, even).astype(bf16)
    dk_ref[...] = turn(dk.T, cos, sin, even).astype(bf16)
    dv_ref[...] = dv.T.astype(bf16)


def attend_back(qkv, mixed, dmix, e, cos, sin, rows_at_once=256):
    slots, d = mixed.shape
    pairs = d // 128
    col = lambda off: pl.BlockSpec((slots, 128), lambda i: (0, off + i))
    return pl.pallas_call(
        lambda *a: attend_back_kernel(*a, rows_at_once=rows_at_once),
        grid=(pairs,),
        in_specs=[col(0), col(pairs), col(2 * pairs), col(0), col(0),
                  pl.BlockSpec((2, slots, slots), lambda i: (i, 0, 0)), full((slots, 128)), full((slots, 128))],
        out_specs=[col(0)] * 3,
        out_shape=[jax.ShapeDtypeStruct((slots, d), bf16)] * 3,
        scratch_shapes=[pltpu.VMEM((2, slots, slots), bf16)],
        compiler_params=params(),
        name="attend_back",
    )(qkv, qkv, qkv, mixed, dmix, e, cos, sin)


def front_kernel(dq_ref, dk_ref, dv_ref, w_ref, x_ref, dmid_ref, mod_ref, out_ref, dmod_ref):
    i = pl.program_id(0)
    d = x_ref.shape[1]
    dh = mm(dq_ref[...], w_ref[:, :d], NT) + mm(dk_ref[...], w_ref[:, d : 2 * d], NT) + mm(dv_ref[...], w_ref[:, 2 * d :], NT)
    x = x_ref[...].astype(f32)
    c = x - jnp.mean(x, axis=1, keepdims=True)
    r = lax.rsqrt(jnp.mean(c * c, axis=1, keepdims=True) + EPS)
    n1 = c * r
    dscale = jnp.sum(dh * n1, axis=0, keepdims=True)
    dshift = jnp.sum(dh, axis=0, keepdims=True)
    dn = dh * (1.0 + mod_ref[:, d : 2 * d])
    out_ref[...] = dmid_ref[...] + r * (
        dn - jnp.mean(dn, axis=1, keepdims=True) - n1 * jnp.mean(dn * n1, axis=1, keepdims=True)
    )
    part = jnp.concatenate([dshift, dscale], axis=1)

    @pl.when(i == 0)
    def _():
        dmod_ref[...] = part

    @pl.when(i > 0)
    def _():
        dmod_ref[...] += part


def front_grad(dq, dk, dv, w, x, dmid, mod, tile=256):
    slots, d = x.shape
    row = pl.BlockSpec((tile, d), lambda i: (i, 0))
    return pl.pallas_call(
        front_kernel,
        grid=(slots // tile,),
        in_specs=[row, row, row, full(w.shape), row, row, full(mod.shape)],
        out_specs=[row, pl.BlockSpec((1, 2 * d), lambda i: (0, 0))],
        out_shape=[jax.ShapeDtypeStruct((slots, d), f32), jax.ShapeDtypeStruct((1, 2 * d), f32)],
        compiler_params=params(),
        name="front_grad",
    )(dq, dk, dv, w, x, dmid, mod)


MESH = pl.DeviceIdType.MESH
SMALL = (16, 512)


class Exchange:
    def __init__(self, groups, batch, own, s, sems):
        self.G, self.B, self.H = groups, batch, groups // 4
        self.own = own
        self.s = s
        self.send, self.recv = sems
        g, c = lax.axis_index("groups"), lax.axis_index("batch")
        self.c, self.x, self.y, self.z = c, g % 2, (g // 2) % 2, g // 4
        x, y, z, H, B = self.x, self.y, self.z, self.H, self.B
        pos = lambda z_, y_, x_: z_ * 4 + y_ * 2 + x_
        self.cores = [(g, (c + k) % B) for k in range(1, B)]
        self.across_x = (pos(z, y, 1 - x), c)
        self.across_y = (pos(z, 1 - y, x), c)
        self.across_z = [(pos((z + k) % H, y, x), c) for k in range(1, H)]
        self.n_sems = 2 * (B - 1) + 4 + (H - 1)

    @staticmethod
    def sems_per_chunk(groups, batch):
        return 2 * (batch - 1) + 4 + (groups // 4 - 1)

    def barrier(self):
        sem = pltpu.get_barrier_semaphore()
        peers = self.cores + [self.across_x, self.across_y] + self.across_z
        for p in peers:
            pl.semaphore_signal(sem, inc=1, device_id=p, device_id_type=MESH)
        pl.semaphore_wait(sem, len(peers))

    def copy(self, j, n, src, dst, peer):
        return pltpu.make_async_remote_copy(
            src_ref=src, dst_ref=dst, send_sem=self.send.at[j, n], recv_sem=self.recv.at[j, n],
            device_id=peer, device_id_type=MESH,
        )

    def copies(self, j, phase):
        B, H, x, y, z = self.B, self.H, self.x, self.y, self.z
        s = self.s
        rows, width = s["r0"].shape[-2:]
        half = rows // 2
        if phase == 0:
            out = []
            for k, p in enumerate(self.cores):
                cols = pl.ds(pl.multiple_of(p[1] * width, width), width)
                out.append(self.copy(j, k, self.own(j).at[:, :, :, :, cols], s["r0"].at[j, k], p))
            return out
        n = B - 1
        if phase == 1:
            total = s["r0"].at[j, 0]
            return [
                self.copy(j, n, total.at[:, :, 1 - x, :half], s["r1"].at[j, 0], self.across_x),
                self.copy(j, n + 1, total.at[:, 1 - y, :, half:], s["r1"].at[j, 1], self.across_y),
            ]
        if phase == 2:
            return [
                self.copy(j, n + 2, s["r1"].at[j, 0, :, 1 - y], s["r2"].at[j, :, :half], self.across_y),
                self.copy(j, n + 3, s["r1"].at[j, 1, :, 1 - x], s["r2"].at[j, :, half:], self.across_x),
            ]
        n += 4
        if phase == 3:
            return [
                self.copy(j, n + k, s["r2"].at[j, p[0] // 4], s["r3"].at[j, k], p)
                for k, p in enumerate(self.across_z)
            ]
        n += H - 1
        cols = pl.ds(pl.multiple_of(self.c * width, width), width)
        place = s["out"].at[j, :, cols]
        return [self.copy(j, n + k, place, place, p) for k, p in enumerate(self.cores)]

    def start(self, j, phase):
        for d in self.copies(j, phase):
            d.start()

    def wait(self, j, phase):
        for d in self.copies(j, phase):
            d.wait()

    def finish(self, j, phase):
        self.wait(j, phase)
        s, x, y, z, H = self.s, self.x, self.y, self.z, self.H
        rows, width = s["r0"].shape[-2:]
        half = rows // 2
        cols = pl.ds(pl.multiple_of(self.c * width, width), width)
        if phase == 0:
            own = self.own(j)

            def add(i, _):
                h, b = i // 4, i % 4
                t = own[h, b // 2, b % 2, :, cols].astype(f32)
                for k in range(self.B - 1):
                    t = t + s["r0"][j, k, h, b // 2, b % 2].astype(f32)
                s["r0"][j, 0, h, b // 2, b % 2] = t.astype(bf16)
                return _

            lax.fori_loop(0, 4 * H, add, 0)
        elif phase == 1:

            def add(h, _):
                for i in range(2):
                    a = s["r1"][j, 0, h, i].astype(f32) + s["r0"][j, 0, h, i, x, :half].astype(f32)
                    s["r1"][j, 0, h, i] = a.astype(bf16)
                    b = s["r1"][j, 1, h, i].astype(f32) + s["r0"][j, 0, h, y, i, half:].astype(f32)
                    s["r1"][j, 1, h, i] = b.astype(bf16)
                return _

            lax.fori_loop(0, H, add, 0)
        elif phase == 2:

            def add(h, _):
                a = s["r2"][j, h, :half].astype(f32) + s["r1"][j, 0, h, y].astype(f32)
                s["r2"][j, h, :half] = a.astype(bf16)
                b = s["r2"][j, h, half:].astype(f32) + s["r1"][j, 1, h, x].astype(f32)
                s["r2"][j, h, half:] = b.astype(bf16)
                return _

            lax.fori_loop(0, H, add, 0)
        elif phase == 3:
            t = s["r2"][j, z].astype(f32)
            for k in range(H - 1):
                t = t + s["r3"][j, k].astype(f32)
            s["out"][j, :, cols] = t

    @staticmethod
    def scratch(groups, batch, chunks, rows, cols):
        H, w = groups // 4, cols // batch
        return dict(
            r0=pltpu.VMEM((chunks, batch - 1, H, 2, 2, rows, w), bf16),
            r1=pltpu.VMEM((chunks, 2, H, 2, rows // 2, w), bf16),
            r2=pltpu.VMEM((chunks, H, rows, w), bf16),
            r3=pltpu.VMEM((chunks, H - 1, rows, w), bf16),
            out=pltpu.VMEM((chunks, rows, cols), f32),
        )

    def advance(self, step, chunks):
        for phase in range(4, 0, -1):
            j = step - phase
            if 0 <= j < chunks:
                self.finish(j, phase - 1)
                self.start(j, phase)
        if 0 <= step < chunks:
            self.start(step, 0)


class Small:
    def __init__(self, ex, bias, seen, mine, sems):
        self.ex, self.bias, self.seen, self.mine = ex, bias, seen, mine
        self.send, self.recv = sems

    @staticmethod
    def count(groups, batch):
        return 2 * (batch - 1 + 2 + groups // 4 - 1)

    @staticmethod
    def scratch(groups, batch):
        n = batch - 1 + 2 + groups // 4 - 1
        return dict(
            bias=pltpu.VMEM((n,) + SMALL, f32),
            seen=pltpu.VMEM((groups // 4, 2, 2, batch) + SMALL, bf16),
        )

    def pairs(self, phase):
        ex = self.ex
        B, H, x, y, z, c = ex.B, ex.H, ex.x, ex.y, ex.z, ex.c
        seen = self.seen
        peers = [ex.cores, [ex.across_x], [ex.across_y], ex.across_z][phase]
        first = [0, B - 1, B, B + 1][phase]
        block = [seen.at[z, y, x, c], seen.at[z, y, x], seen.at[z, y], seen.at[z]][phase]
        out = []
        for k, p in enumerate(peers):
            n = 2 * (first + k)
            mk = lambda m, src, dst: pltpu.make_async_remote_copy(
                src_ref=src, dst_ref=dst, send_sem=self.send.at[m], recv_sem=self.recv.at[m],
                device_id=p, device_id_type=MESH)
            out.append(mk(n, self.mine.at[phase], self.bias.at[first + k]))
            out.append(mk(n + 1, block, block))
        return out

    def start(self, phase):
        for d in self.pairs(phase):
            d.start()

    def finish(self, phase):
        for d in self.pairs(phase):
            d.wait()
        ex = self.ex
        n = [ex.B - 1, 1, 1, ex.H - 1][phase]
        first = [0, ex.B - 1, ex.B, ex.B + 1][phase]
        t = self.mine[phase]
        for k in range(n):
            t = t + self.bias[first + k]
        self.mine[phase + 1] = t


def reduce_kernel(groups, batch, chunks, dw_ref, uw_ref, ow_ref, qw_ref, bias_ref, row_ref,
                  dwo_ref, uwo_ref, owo_ref, qwo_ref, bias_out, seen_out,
                  own, r0, r1, r2, r3, out, sbias, seen, mine, send, recv, ssend, srecv, load, store):
    cols = own.shape[-1]
    ex = Exchange(groups, batch, lambda j: own.at[j], dict(r0=r0, r1=r1, r2=r2, r3=r3, out=out), (send, recv))
    sm = Small(ex, sbias, seen, mine, (ssend, srecv))
    src = [dw_ref.at[:, :, :, 0], dw_ref.at[:, :, :, 1]]
    src += [uw_ref.at[:, :, :, :, k * cols : (k + 1) * cols] for k in range(2)]
    src += [ow_ref]
    src += [qw_ref.at[k] for k in range(3)]
    loads = [pltpu.make_async_copy(a, own.at[j], load.at[j]) for j, a in enumerate(src)]
    for d in loads:
        d.start()
    z, y, x, c = ex.z, ex.y, ex.x, ex.c
    mine[0] = bias_ref[...]
    seen[z, y, x, c] = row_ref[...]
    ex.barrier()
    sm.start(0)
    for step in range(chunks + 5):
        if step < chunks:
            loads[step].wait()
        ex.advance(step, chunks)
        if step < 4:
            sm.finish(step)
            if step < 3:
                sm.start(step + 1)
        if 0 <= step - 5 < chunks:
            ex.wait(step - 5, 4)
    bias_out[...] = mine[4]
    dst = [dwo_ref.at[0], dwo_ref.at[1]]
    dst += [uwo_ref.at[:, k * cols : (k + 1) * cols] for k in range(2)]
    dst += [owo_ref]
    dst += [qwo_ref.at[:, k * cols : (k + 1) * cols] for k in range(3)]
    stores = [pltpu.make_async_copy(out.at[j], a, store.at[j]) for j, a in enumerate(dst)]
    stores.append(pltpu.make_async_copy(seen, seen_out, store.at[chunks]))
    for d in stores:
        d.start()
    for d in stores:
        d.wait()


def reduce_all(groups, batch, down, up, outw, qkv3, bias, row):
    d = outw.shape[0]
    H, rows = groups // 4, d // groups
    chunks = 8
    S = jax.ShapeDtypeStruct
    hbm = pl.BlockSpec(memory_space=pl.ANY)
    vm = pl.BlockSpec(memory_space=pltpu.VMEM)
    sc = Exchange.scratch(groups, batch, chunks, rows, d)
    ss = Small.scratch(groups, batch)
    ns, nsm = Exchange.sems_per_chunk(groups, batch), Small.count(groups, batch)
    dma = pltpu.SemaphoreType.DMA
    return pl.pallas_call(
        lambda *a: reduce_kernel(groups, batch, chunks, *a),
        in_specs=[hbm] * 4 + [vm] * 2,
        out_specs=[hbm] * 4 + [vm, hbm],
        out_shape=[S((2, rows, d), f32), S((rows, 2 * d), f32), S((rows, d), f32), S((rows, 3 * d), f32),
                   S(SMALL, f32), S((H, 2, 2, batch) + SMALL, bf16)],
        scratch_shapes=[pltpu.VMEM((chunks, H, 2, 2, rows, d), bf16), sc["r0"], sc["r1"], sc["r2"], sc["r3"], sc["out"],
                        ss["bias"], ss["seen"], pltpu.VMEM((5,) + SMALL, f32),
                        dma((chunks, ns)), dma((chunks, ns)), dma((nsm,)), dma((nsm,)), dma((chunks,)), dma((chunks + 1,))],
        compiler_params=params(collective_id=0, has_side_effects=True),
        name="reduce_all",
    )(down.reshape(H, 2, 2, 2, rows, d), up.reshape(H, 2, 2, rows, 2 * d), outw.reshape(H, 2, 2, rows, d),
      qkv3, bias, row)


def solution(mesh):
    groups, batch = mesh.shape["groups"], mesh.shape["batch"]

    def body(frames, te, lengths, mod_w, mod_b, qkv_w, qkv_b, out_w, out_b, up_w, up_b, down_w, down_b, cot):
        x, ct = frames[0], cot[0]
        slots, d = x.shape
        cos, sin = rot_tables(slots, d // HEADS)
        row = lambda b: b.reshape(1, -1)
        mod = modulation(te, mod_w, row(mod_b))
        h1, qkv = project_qkv(x, mod, qkv_w, row(qkv_b), cos, sin)
        mixed, e, linv = attend(lengths, qkv)
        out, h2, act, dbr, dup, dat, dmix, dmid, dmod_b = middle_part(
            lengths, mixed, x, ct, mod, linv, out_w, row(out_b), up_w, row(up_b), down_w, row(down_b)
        )
        down_g, down_bg = wgrad(act, dbr)
        up_g, up_bg = wgrad(h2, dup)
        out_g, out_bg = wgrad(mixed, dat)
        dq, dk, dv = attend_back(qkv, mixed, dmix, e, cos, sin)
        parts = [wgrad(h1, t) for t in (dq, dk, dv)]
        fg, dmod_a = front_grad(dq, dk, dv, qkv_w, x, dmid, mod)
        dmod = jnp.concatenate([dmod_a, dmod_b], axis=1).astype(bf16)
        embed = jax.nn.silu(te.astype(f32)).astype(bf16)
        pad = jnp.zeros((1, 1024), bf16)
        small = jnp.concatenate([dmod, embed, pad], axis=1).reshape(SMALL)
        bias = jnp.concatenate([p[1] for p in parts] + [out_bg, up_bg, down_bg, pad.astype(f32)], axis=1).reshape(SMALL)
        H, rows = groups // 4, d // groups
        qkv3 = jnp.stack([p[0].reshape(H, 2, 2, rows, d) for p in parts])
        dws, uws, ows, qws, bs, seen = reduce_all(groups, batch, down_g, up_g, out_g, qkv3, bias, small)
        seen = seen.reshape(groups * batch, 8192)
        g = lax.axis_index("groups")
        dm_all, em_all = seen[:, : 6 * d], seen[:, 6 * d : 7 * d]
        em = lax.dynamic_slice_in_dim(em_all, g * rows, rows, 1)
        mod_wg = mm(em, dm_all, TN)
        mod_bg = lax.dynamic_slice_in_dim(jnp.sum(dm_all.astype(f32), axis=0), g * 6 * rows, 6 * rows)
        bs = bs.reshape(8192)
        cut = lambda off, n: lax.dynamic_slice_in_dim(bs, off + g * n, n)
        silu_value, silu_back = jax.vjp(jax.nn.silu, te.astype(f32))
        time_grad = silu_back(mm(dmod, mod_w, NT))[0]
        return (out[None], fg[None], time_grad, mod_wg, mod_bg, qws, cut(0, 3 * rows), ows, cut(3 * d, rows),
                uws, cut(4 * d, 2 * rows), dws.reshape(2 * rows, d), cut(6 * d, 2 * rows // 2))

    split = P(("groups", "batch"))
    own = P("groups")
    return jax.shard_map(
        body, mesh=mesh,
        in_specs=(split,) * 3 + (P(),) * 10 + (split,),
        out_specs=(split,) * 3 + (own,) * 10,
        check_vma=False,
    )
```

time: 1100 us -> 325 us (0.30); the launches traced: 1090 us -> 324 us
  matrix products: 343 us -> 10.3 us
  waiting for transfers between devices: 308 us -> 0 us
  Pallas kernels: 0 us -> 287 us
  local copies, waits for them, and re-layouts: 198 us -> 17.5 us
  other arithmetic: 139 us -> 7.95 us
  blocking collectives: 77.8 us -> 0 us
  between operations: 18.4 us -> 1.49 us
    dot_general x28 -> x2, matrix products: 343 us -> 10.3 us  [mm(): return lax.dot_general(a, b, (dims, ((), ())), preferred_element_type=f32)]
    reduce_scatter x5 -> x0, waiting for transfers between devices: 308 us -> none  [the longest x1 207 us: body(): lax.psum_scatter(mod_w_grad.astype(jnp.bfloat16), 'groups', scatter_dimen...]
    pallas_call x0 -> x13, Pallas kernels: none -> 287 us  [the longest x1 100 us: reduce_all(): pl.pallas_call(lambda *a: reduce_kernel(groups, batch, chunks, *a), in_sp...]
    dynamic_update_slice x4 -> x0, local copies, waits for them, and re-layouts: 82.2 us -> none  [attend_backward(): lax.scan(one_block, (zeros_kv, zeros_kv), (queries.reshape(blocks, block,...]
    convert_element_type x19 -> x1, other arithmetic: 77.3 us -> 0.02 us  [body(): embed = jax.nn.silu(te.astype(f32)).astype(bf16)]
    unnamed x1 -> x0, blocking collectives: 75.4 us -> none
    reduce_sum x11 -> x1, other arithmetic: 50.9 us -> 0.09 us  [body(): jnp.sum(dm_all.astype(f32), axis=0)]
    unnamed x148 -> x34, local copies, waits for them, and re-layouts: 34.7 us -> 9.49 us
  transfers between devices with their start and end apart: 6 -> 0, of which waited for: 2 -> 0; matrix products, arithmetic and copies ran while one was open for 40% -> 0% of each run, Pallas kernels for 0% -> 0%
where the time goes in v1:
time: 325 us; the launch traced here: 324 us
  Pallas kernels  287 us (88%)
  local copies, waits for them, and re-layouts  17.5 us (5%)
  matrix products  10.3 us (3%)
  other arithmetic  7.95 us (2%)
    pallas_call x1, Pallas kernels, reduce_all(): pl.pallas_call(lambda *a: reduce_kernel(groups, batch, chunks, *a), in_sp...  100 us
    pallas_call x6, Pallas kernels, wgrad(): pl.pallas_call(wgrad_kernel, grid=(m // tile,), in_specs=[pl.BlockSpec((s...  46.1 us
    pallas_call x1, Pallas kernels, middle_part(): pl.pallas_call(middle_kernel, grid_spec=pltpu.PrefetchScalarGridSpec(num_...  38.8 us
    pallas_call x1, Pallas kernels, attend_back(): pl.pallas_call(lambda *a: attend_back_kernel(*a, rows_at_once=rows_at_onc...  38.6 us
    pallas_call x1, Pallas kernels, attend(): pl.pallas_call(lambda *a: attend_kernel(*a, rows_at_once=rows_at_once), g...  27.7 us
    pallas_call x1, Pallas kernels, front_grad(): pl.pallas_call(front_kernel, grid=(slots // tile,), in_specs=[row, row, r...  14.8 us
    pallas_call x1, Pallas kernels, project_qkv(): pl.pallas_call(qkv_kernel, grid=(slots // tile,), in_specs=[row(d), full(...  12.7 us
    dot_general x2, matrix products, mm(): return lax.dot_general(a, b, (dims, ((), ())), preferred_element_type=f32)  10.3 us

profile of v1, /device:TPU:0, one launch (start us, length us, event | category | flops | bytes accessed | tf_op | source)
XLA Modules:
  0.0 323.8 jit_solution(12063081432673034944)
XLA Ops:
  0.6 1.3 reshape.101.b_ref
  2.0 7.6 %modulation.1.mod_ref = f32[1,6144]{1,0:T(1,128)} custom-call(bf16[1,1024]{1,0:T(2,128)(2,1)} %te_ref.1, bf16[1024,6144]{1,0:T(8,128)(2,1)} %w_ref.3, bf16[1,6144]{1,0:T(2,128)(2,1)} %reshape.101.b_ref), custom_call_target="tpu_custom_call" | custom-call | tf_op jit(solution)/shard_map/modulation/pallas_call | solution.py:59
  10.2 12.7 %project_qkv.1 = (bf16[1024,1024]{1,0:T(8,128)(2,1)}, bf16[1024,3072]{1,0:T(8,128)(2,1)}) custom-call(bf16[1024,1024]{1,0:T(8,128)(2,1)} %bitcast.19, f32[1,6144]{1,0:T(1,128)} %modulation.1.mod_ref, bf16[1024,3072]{1,0:T(8,128)(2,1)} %w_ref.5, bf16[1,3072]{1,0:T(2,128)(2,1)} %reshape.102.b_ref, f32[1024,128]{1,0:T(8,128)} %constant.47.clone.cos_ref.a_6_, ...), custom_call_target="tpu_custom_call" | custom-call | tf_op jit(solution)/shard_map/project_qkv/pallas_call | solution.py:95
  23.5 27.7 %attend.1 = (bf16[1024,1024]{1,0:T(8,128)(2,1)}, bf16[16,1024,1024]{2,1,0:T(8,128)(2,1)}, f32[1024,1024]{1,0:T(8,128)}) custom-call(s32[1]{0:T(128)S(6)} %copy.41.a_0_.len_ref, bf16[1024,3072]{1,0:T(8,128)(2,1)} %get-tuple-element.50.a_1_.a_2_.a_3_.a_0_, bf16[1024,3072]{1,0:T(8,128)(2,1)} %get-tuple-element.50.a_1_.a_2_.a_3_.a_0_, ...), custom_call_target="tpu_custom_call" | custom-call | tf_op jit(solution)/shard_map/attend/pallas_call | solution.py:135
  53.0 38.8 %middle_part.1 = (bf16[1024,1024]{1,0:T(8,128)(2,1)}, bf16[1024,1024]{1,0:T(8,128)(2,1)}, bf16[1024,2048]{1,0:T(8,128)(2,1)}, bf16[1024,1024]{1,0:T(8,128)(2,1)}...) custom-call(s32[1]{0:T(128)S(6)} %copy.41.a_0_.len_ref, ...), custom_call_target="tpu_custom_call" | custom-call | tf_op jit(solution)/shard_map/middle_part/pallas_call | solution.py:215
  91.8 38.6 %attend_back.1 = (bf16[1024,1024]{1,0:T(8,128)(2,1)}, bf16[1024,1024]{1,0:T(8,128)(2,1)}, bf16[1024,1024]{1,0:T(8,128)(2,1)}) custom-call(bf16[1024,3072]{1,0:T(8,128)(2,1)} %get-tuple-element.50.a_1_.a_2_.a_3_.a_0_, bf16[1024,3072]{1,0:T(8,128)(2,1)} %get-tuple-element.50.a_1_.a_2_.a_3_.a_0_, bf16[1024,3072]{1,0:T(8,128)(2,1)} %get-tuple-element.50.a_1_.a_2_.a_3_.a_0_, ...), custom_call_target="tpu_custom_call" | custom-call | tf_op jit(solution)/shard_map/attend_back/pallas_call | solution.py:287
  130.5 14.8 %front_grad.1 = (f32[1024,1024]{1,0:T(8,128)}, f32[1,2048]{1,0:T(1,128)}) custom-call(bf16[1024,1024]{1,0:T(8,128)(2,1)} %get-tuple-element.56.dq_ref.r_ref, bf16[1024,1024]{1,0:T(8,128)(2,1)} %get-tuple-element.57.dk_ref.r_ref, bf16[1024,1024]{1,0:T(8,128)(2,1)} %get-tuple-element.58.dv_ref.r_ref, bf16[1024,3072]{1,0:T(8,128)(2,1)} %w_ref.5, ...), custom_call_target="tpu_custom_call" | custom-call | tf_op jit(solution)/shard_map/front_grad/pallas_call | solution.py:328
  145.3 0.7 convert.10
  146.9 6.5 %wgrad.9 = (bf16[1024,1024]{1,0:T(8,128)(2,1)}, f32[1,1024]{1,0:T(1,128)}) custom-call(bf16[1024,1024]{1,0:T(8,128)(2,1)} %get-tuple-element.71.l_ref, bf16[1024,1024]{1,0:T(8,128)(2,1)} %get-tuple-element.56.dq_ref.r_ref), custom_call_target="tpu_custom_call" | custom-call | tf_op jit(solution)/shard_map/wgrad/pallas_call | solution.py:244
  153.4 0.7 constant_dynamic-update-slice_fusion.6
  154.1 6.5 %wgrad.10 = (bf16[1024,1024]{1,0:T(8,128)(2,1)}, f32[1,1024]{1,0:T(1,128)}) custom-call(bf16[1024,1024]{1,0:T(8,128)(2,1)} %get-tuple-element.71.l_ref, bf16[1024,1024]{1,0:T(8,128)(2,1)} %get-tuple-element.57.dk_ref.r_ref), custom_call_target="tpu_custom_call" | custom-call | tf_op jit(solution)/shard_map/wgrad/pallas_call | solution.py:244
  160.6 0.7 constant_dynamic-update-slice_fusion.5
  161.3 6.5 %wgrad.11 = (bf16[1024,1024]{1,0:T(8,128)(2,1)}, f32[1,1024]{1,0:T(1,128)}) custom-call(bf16[1024,1024]{1,0:T(8,128)(2,1)} %get-tuple-element.71.l_ref, bf16[1024,1024]{1,0:T(8,128)(2,1)} %get-tuple-element.58.dv_ref.r_ref), custom_call_target="tpu_custom_call" | custom-call | tf_op jit(solution)/shard_map/wgrad/pallas_call | solution.py:244
  167.8 0.7 constant_dynamic-update-slice_fusion.4
  168.5 6.5 %wgrad.8 = (bf16[1024,1024]{1,0:T(8,128)(2,1)}, f32[1,1024]{1,0:T(1,128)}) custom-call(bf16[1024,1024]{1,0:T(8,128)(2,1)} %get-tuple-element.51.mixed_ref.a_3_.l_ref, bf16[1024,1024]{1,0:T(8,128)(2,1)} %get-tuple-element.69.r_ref), custom_call_target="tpu_custom_call" | custom-call | tf_op jit(solution)/shard_map/wgrad/pallas_call | solution.py:244
  175.0 0.7 constant_dynamic-update-slice_fusion.3
  175.7 9.5 %wgrad.7 = (bf16[1024,2048]{1,0:T(8,128)(2,1)}, f32[1,2048]{1,0:T(1,128)}) custom-call(bf16[1024,1024]{1,0:T(8,128)(2,1)} %get-tuple-element.66.l_ref, bf16[1024,2048]{1,0:T(8,128)(2,1)} %get-tuple-element.67.r_ref), custom_call_target="tpu_custom_call" | custom-call | tf_op jit(solution)/shard_map/wgrad/pallas_call | solution.py:244
  185.2 0.7 constant_dynamic-update-slice_fusion.2
  185.9 10.6 %wgrad.6 = (bf16[2048,1024]{1,0:T(8,128)(2,1)}, f32[1,1024]{1,0:T(1,128)}) custom-call(bf16[1024,2048]{1,0:T(8,128)(2,1)} %get-tuple-element.63.l_ref, bf16[1024,1024]{1,0:T(8,128)(2,1)} %get-tuple-element.64.r_ref), custom_call_target="tpu_custom_call" | custom-call | tf_op jit(solution)/shard_map/wgrad/pallas_call | solution.py:244
  196.5 0.7 constant_dynamic-update-slice_fusion.1
  197.7 0.7 reduce.9
  199.0 6.2 %pad_maximum_fusion.a_3_ = bf16[3,4,2,2,64,1024]{5,4,3,2,1,0:T(8,128)(2,1)} fusion(bf16[1,4,2,2,64,1024]{5,4,3,2,1,0:T(8,128)(2,1)} %bitcast.30, bf16[1,4,2,2,64,1024]{5,4,3,2,1,0:T(8,128)(2,1)} %bitcast.29, bf16[1,4,2,2,64,1024]{5,4,3,2,1,0:T(8,128)(2,1)} %bitcast.28), kind=kLoop, calls=%fused_computation | loop fusion | flops 6291456 | bytes 12582912 | tf_op jit(solution)/shard_map/stack | solution.py:627
  205.2 100.3 %reduce_all.1 = (f32[2,64,1024]{2,1,0:T(8,128)}, f32[64,2048]{1,0:T(8,128)}, f32[64,1024]{1,0:T(8,128)}, f32[64,3072]{1,0:T(8,128)}, f32[16,512]{1,0:T(8,128)}, /*index=5*/bf16[4,2,2,2,16,512]{5,4,3,2,1,0:T(8,128)(2,1)}) custom-call(bf16[4,2,2,2,64,1024]{5,4,3,2,1,0:T(8,128)(2,1)} %bitcast.23, bf16[4,2,2,64,2048]{4,3,2,1,0:T(8,128)(2,1)} %bitcast.22, ...), custom_call_target="tpu_custom_call" | custom-call | tf_op jit(solution)/shard_map/reduce_all/pallas_call | solution.py:586
  305.5 1.3 copy.29
  306.9 1.6 fusion
  308.6 0.7 dynamic_slice.19
  309.2 0.8 copy.30
  312.0 8.7 %fusion.5 = f32[1,1024]{1,0:T(1,128)} fusion(f32[1,1024]{1,0:T(1,128)S(1)} %get-tuple-element.88, bf16[1,1024]{1,0:T(2,128)(2,1)S(1)} %copy-done.5, bf16[6144,1]{0,1:T(2,128)(2,1)S(1)} %reshape.114, bf16[1024,6144]{1,0:T(8,128)(2,1)} %w_ref.3), kind=kOutput, calls=%fused_computation.17 | convolution fusion | flops 12590080 | bytes 12605440 | tf_op jit(solution)/shard_map/dot_general | solution.py:20
  320.6 0.9 copy.42
  321.5 0.7 copy.43
  322.2 0.8 copy.44
  323.0 0.8 copy.45
  (44 shorter events, 6.4 us)
Async XLA Ops:
  2.0 7.6 %copy-start.7 = (bf16[3072]{0:T(1024)(128)(2,1)S(1)}, bf16[3072]{0:T(1024)(128)(2,1)}, u32[]{:S(2)}) copy-start(bf16[3072]{0:T(1024)(128)(2,1)} %param.22) | copy-start | bytes 18436
  23.5 27.7 %copy-start.8 = (bf16[2048]{0:T(1024)(128)(2,1)S(1)}, bf16[2048]{0:T(1024)(128)(2,1)}, u32[]{:S(2)}) copy-start(bf16[2048]{0:T(1024)(128)(2,1)} %param.26) | copy-start | bytes 12292
  23.5 28.3 %copy-start.9 = (bf16[1024]{0:T(1024)(128)(2,1)S(1)}, bf16[1024]{0:T(1024)(128)(2,1)}, u32[]{:S(2)}) copy-start(bf16[1024]{0:T(1024)(128)(2,1)} %param.24) | copy-start | bytes 6148
  23.5 28.9 %copy-start.10 = (bf16[1024]{0:T(1024)(128)(2,1)S(1)}, bf16[1024]{0:T(1024)(128)(2,1)}, u32[]{:S(2)}) copy-start(bf16[1024]{0:T(1024)(128)(2,1)} %param.28) | copy-start | bytes 6148
  130.5 15.5 %copy-start.4 = (f32[1,4096]{1,0:T(1,128)S(1)}, f32[1,4096]{1,0:T(1,128)}, u32[]{:S(2)}) copy-start(f32[1,4096]{1,0:T(1,128)} %get-tuple-element.62) | copy-start | bytes 49156
  130.5 15.5 %copy-start.5 = (bf16[1,1024]{1,0:T(2,128)(2,1)S(1)}, bf16[1,1024]{1,0:T(2,128)(2,1)}, u32[]{:S(2)}) copy-start(bf16[1,1024]{1,0:T(2,128)(2,1)} %te_ref.1) | copy-start | bytes 6148
  205.2 106.6 %copy-start.6 = (f32[1,2048]{1,0:T(1,128)S(1)}, f32[1,2048]{1,0:T(1,128)}, u32[]{:S(2)}) copy-start(f32[1,2048]{1,0:T(1,128)} %get-tuple-element.61) | copy-start | bytes 24580
  311.9 8.7 %copy-start = (f32[64,3072]{1,0:T(8,128)S(1)}, f32[64,3072]{1,0:T(8,128)}, u32[]{:S(2)}) copy-start(f32[64,3072]{1,0:T(8,128)} %get-tuple-element.109) | copy-start | bytes 2359300
  311.9 9.6 %copy-start.3 = (f32[64,1024]{1,0:T(8,128)S(1)}, f32[64,1024]{1,0:T(8,128)}, u32[]{:S(2)}) copy-start(f32[64,1024]{1,0:T(8,128)} %get-tuple-element.111) | copy-start | bytes 786436
  312.0 10.3 %copy-start.2 = (f32[64,2048]{1,0:T(8,128)S(1)}, f32[64,2048]{1,0:T(8,128)}, u32[]{:S(2)}) copy-start(f32[64,2048]{1,0:T(8,128)} %get-tuple-element.113) | copy-start | bytes 1572868
  312.0 11.1 %copy-start.1 = (f32[2,64,1024]{2,1,0:T(8,128)S(1)}, f32[2,64,1024]{2,1,0:T(8,128)}, u32[]{:S(2)}) copy-start(f32[2,64,1024]{2,1,0:T(8,128)} %get-tuple-element.86) | copy-start | bytes 1572868

commit v2 on v1

v2 whole, which is shorter than its diff:
```python
import jax, jax.numpy as jnp
import numpy as np
from jax import lax
from jax.experimental import pallas as pl
from jax.experimental.pallas import tpu as pltpu
from jax.sharding import PartitionSpec as P

f32 = jnp.float32
bf16 = jnp.bfloat16
HEADS = 16
LOG2E = 1.4426950408889634
EPS = 1e-6
NN = ((1,), (0,))
NT = ((1,), (1,))
TN = ((0,), (0,))
VMEM_LIMIT = 62 * 2**20


def mm(a, b, dims):
    return lax.dot_general(a, b, (dims, ((), ())), preferred_element_type=f32)


def params(**kw):
    return pltpu.CompilerParams(vmem_limit_bytes=VMEM_LIMIT, **kw)


def rot_tables(slots, size):
    pos = np.arange(slots, dtype=np.float64)[:, None]
    pair = np.arange(size // 2, dtype=np.float64)[None, :]
    ang = pos * np.power(10000.0, -2.0 * pair / size)
    cos = np.repeat(np.cos(ang), 2, axis=1)
    sin = np.repeat(np.sin(ang), 2, axis=1) * np.where(np.arange(size) % 2 == 0, -1.0, 1.0)
    return np.tile(cos, (1, 2)).astype(np.float32), np.tile(sin, (1, 2)).astype(np.float32)


def turn(x, cos, sin, even):
    swapped = jnp.where(even, pltpu.roll(x, 127, 1), pltpu.roll(x, 1, 1))
    return x * cos + swapped * sin


def even_lanes(rows):
    return lax.broadcasted_iota(jnp.int32, (rows, 128), 1) % 2 == 0


def full(shape):
    return pl.BlockSpec(shape, lambda *_: (0,) * len(shape), pipeline_mode=pl.Buffered(1))


def mod_kernel(te_ref, w_ref, b_ref, out_ref):
    t = te_ref[...].astype(f32)
    embed = (t * jax.nn.sigmoid(t)).astype(bf16)
    embed = jnp.broadcast_to(embed, (8, embed.shape[1]))
    out_ref[...] = mm(embed, w_ref[...], NN)[:1] + b_ref[...].astype(f32)


def modulation(te, w, b):
    d, n = w.shape
    blk = d
    return pl.pallas_call(
        mod_kernel,
        grid=(n // blk,),
        in_specs=[full((1, d)), pl.BlockSpec((d, blk), lambda i: (0, i)), pl.BlockSpec((1, blk), lambda i: (0, i))],
        out_specs=pl.BlockSpec((1, blk), lambda i: (0, i)),
        out_shape=jax.ShapeDtypeStruct((1, n), f32),
        compiler_params=params(),
        name="modulation",
    )(te, w, b)


def qkv_kernel(x_ref, mod_ref, w_ref, b_ref, cos_ref, sin_ref, h_ref, qkv_ref):
    d = x_ref.shape[1]
    x = x_ref[...].astype(f32)
    c = x - jnp.mean(x, axis=1, keepdims=True)
    r = lax.rsqrt(jnp.mean(c * c, axis=1, keepdims=True) + EPS)
    h = (c * r * (1.0 + mod_ref[:, d : 2 * d]) + mod_ref[:, :d]).astype(bf16)
    h_ref[...] = h
    cos, sin = cos_ref[...], sin_ref[...]
    even = even_lanes(x.shape[0])
    step = 512
    for n in range(0, 3 * d, step):
        y = mm(h, w_ref[:, n : n + step], NN) + b_ref[:, n : n + step].astype(f32)
        for t in range(0, step, 128):
            col = n + t
            z = y[:, t : t + 128]
            if col < 2 * d:
                z = turn(z, cos, sin, even)
            if col < d:
                z = z * 0.125
            qkv_ref[:, col : col + 128] = z.astype(bf16)


def project_qkv(x, mod, w, b, cos, sin, tile=256):
    slots, d = x.shape
    row = lambda n: pl.BlockSpec((tile, n), lambda i: (i, 0))
    return pl.pallas_call(
        qkv_kernel,
        grid=(slots // tile,),
        in_specs=[row(d), full(mod.shape), full(w.shape), full(b.shape), row(128), row(128)],
        out_specs=[row(d), row(3 * d)],
        out_shape=[jax.ShapeDtypeStruct((slots, d), bf16), jax.ShapeDtypeStruct((slots, 3 * d), bf16)],
        compiler_params=params(),
        name="project_qkv",
    )(x, mod, w, b, cos, sin)


def attend_kernel(len_ref, q_ref, k_ref, v_ref, o_ref, e_ref, linv_ref, *, rows_at_once):
    slots = q_ref.shape[0]
    lane = lax.broadcasted_iota(jnp.int32, (1, 128), 1)
    ones = jnp.where(lax.broadcasted_iota(jnp.int32, (slots, 128), 1) == 0, 1.0, 0.0).astype(bf16)
    k = k_ref[...]
    v = jnp.concatenate([v_ref[...], ones], axis=1)
    valid = lax.broadcasted_iota(jnp.int32, (1, slots), 1) < len_ref[0]
    for at in range(0, slots, rows_at_once):
        rows = pl.ds(at, rows_at_once)
        q = q_ref[rows, :]
        outs, invs = [], []
        for h in range(2):
            qh = jnp.where(lane < 64 if h == 0 else lane >= 64, q, jnp.zeros_like(q))
            s = jnp.where(valid, mm(qh, k, NT), -1e30)
            m = jnp.max(s, axis=1, keepdims=True)
            e = jnp.exp2((s - m) * LOG2E).astype(bf16)
            e_ref[h, rows, :] = e
            r = mm(e, v, NN)
            inv = 1.0 / r[:, 128:129]
            outs.append(r[:, :128] * inv)
            invs.append(inv)
        o_ref[rows, :] = jnp.where(lane < 64, outs[0], outs[1]).astype(bf16)
        linv_ref[rows, :] = jnp.where(lane < 64, invs[0], invs[1])


def attend(length, qkv, rows_at_once=128):
    slots, d = qkv.shape[0], qkv.shape[1] // 3
    pairs = d // 128
    col = lambda off: pl.BlockSpec((slots, 128), lambda i, n: (0, off + i))
    return pl.pallas_call(
        lambda *a: attend_kernel(*a, rows_at_once=rows_at_once),
        grid_spec=pltpu.PrefetchScalarGridSpec(
            num_scalar_prefetch=1,
            grid=(pairs,),
            in_specs=[col(0), col(pairs), col(2 * pairs)],
            out_specs=[col(0), pl.BlockSpec((2, slots, slots), lambda i, n: (i, 0, 0)), col(0)],
        ),
        out_shape=[
            jax.ShapeDtypeStruct((slots, d), bf16),
            jax.ShapeDtypeStruct((2 * pairs, slots, slots), bf16),
            jax.ShapeDtypeStruct((slots, d), f32),
        ],
        compiler_params=params(),
        name="attend",
    )(length, qkv, qkv, qkv)


def middle_kernel(
    len_ref, mixed_ref, x_ref, cot_ref, mod_ref, linv_ref, ow_ref, ob_ref, uw_ref, ub_ref, dw_ref, db_ref,
    out_ref, h2_ref, act_ref, dbr_ref, dup_ref, dat_ref, dmix_ref, dmid_ref, dmod_ref,
):
    i = pl.program_id(0)
    tile, d = x_ref.shape
    mod = lambda k: mod_ref[:, k * d : (k + 1) * d]
    gate1, shift2, scale2, gate2 = mod(2), mod(3), mod(4), mod(5)
    slot = lax.broadcasted_iota(jnp.int32, (tile, 1), 0) + i * tile
    valid = slot < len_ref[0]
    attn = jnp.where(valid, mm(mixed_ref[...], ow_ref[...], NN) + ob_ref[...].astype(f32), 0.0)
    mid = x_ref[...].astype(f32) + gate1 * attn
    c = mid - jnp.mean(mid, axis=1, keepdims=True)
    r2 = lax.rsqrt(jnp.mean(c * c, axis=1, keepdims=True) + EPS)
    n2 = c * r2
    h2 = (n2 * (1.0 + scale2) + shift2).astype(bf16)
    h2_ref[...] = h2
    cot = cot_ref[...].astype(f32)
    dbr = (gate2 * cot).astype(bf16)
    dbr_ref[...] = dbr
    ff = uw_ref.shape[1]
    step = 512
    for n in range(0, ff, step):
        u = mm(h2, uw_ref[:, n : n + step], NN) + ub_ref[:, n : n + step].astype(f32)
        c0 = 0.7978845608028654
        th = jnp.tanh(c0 * (u + 0.044715 * u * u * u))
        half = 0.5 * (1.0 + th)
        act_ref[:, n : n + step] = (u * half).astype(bf16)
        grad = half + 0.5 * u * (1.0 - th * th) * (c0 * (1.0 + 3.0 * 0.044715 * u * u))
        da = mm(dbr, dw_ref[n : n + step, :], NT)
        dup_ref[:, n : n + step] = (da * grad).astype(bf16)
    branch = mm(act_ref[...], dw_ref[...], NN) + db_ref[...].astype(f32)
    out_ref[...] = (mid + gate2 * branch).astype(bf16)
    dgate2 = jnp.sum(cot * branch, axis=0, keepdims=True)
    dh2 = mm(dup_ref[...], uw_ref[...], NT)
    dscale2 = jnp.sum(dh2 * n2, axis=0, keepdims=True)
    dshift2 = jnp.sum(dh2, axis=0, keepdims=True)
    dn2 = dh2 * (1.0 + scale2)
    dmid = cot + r2 * (
        dn2 - jnp.mean(dn2, axis=1, keepdims=True) - n2 * jnp.mean(dn2 * n2, axis=1, keepdims=True)
    )
    dmid_ref[...] = dmid
    dgate1 = jnp.sum(dmid * attn, axis=0, keepdims=True)
    dat = jnp.where(valid, gate1 * dmid, 0.0).astype(bf16)
    dat_ref[...] = dat
    dmix_ref[...] = (mm(dat, ow_ref[...], NT) * linv_ref[...]).astype(bf16)
    part = jnp.concatenate([dgate1, dshift2, dscale2, dgate2], axis=1)

    @pl.when(i == 0)
    def _():
        dmod_ref[...] = part

    @pl.when(i > 0)
    def _():
        dmod_ref[...] += part


def middle_part(length, mixed, x, cot, mod, linv, ow, ob, uw, ub, dw, db, tile=256):
    slots, d = x.shape
    ff = uw.shape[1]
    row = lambda n: pl.BlockSpec((tile, n), lambda i, n_: (i, 0))
    S = jax.ShapeDtypeStruct
    return pl.pallas_call(
        middle_kernel,
        grid_spec=pltpu.PrefetchScalarGridSpec(
            num_scalar_prefetch=1,
            grid=(slots // tile,),
            in_specs=[row(d), row(d), row(d), full(mod.shape), row(d), full(ow.shape), full(ob.shape),
                      full(uw.shape), full(ub.shape), full(dw.shape), full(db.shape)],
            out_specs=[row(d), row(d), row(ff), row(d), row(ff), row(d), row(d), row(d),
                       pl.BlockSpec((1, 4 * d), lambda i, n_: (0, 0))],
        ),
        out_shape=[S((slots, d), bf16), S((slots, d), bf16), S((slots, ff), bf16), S((slots, d), bf16),
                   S((slots, ff), bf16), S((slots, d), bf16), S((slots, d), bf16), S((slots, d), f32),
                   S((1, 4 * d), f32)],
        compiler_params=params(),
        name="middle_part",
    )(length, mixed, x, cot, mod, linv, ow, ob, uw, ub, dw, db)


MESH = pl.DeviceIdType.MESH
STRIP = 512
RING = 4


class Exchange:
    def __init__(self, groups, batch, own, s, sems, chunks):
        self.G, self.B, self.H, self.chunks = groups, batch, groups // 4, chunks
        self.own = own
        self.s = s
        self.send, self.recv = sems
        g, c = lax.axis_index("groups"), lax.axis_index("batch")
        self.c, self.x, self.y, self.z = c, g % 2, (g // 2) % 2, g // 4
        x, y, z, H, B = self.x, self.y, self.z, self.H, self.B
        pos = lambda z_, y_, x_: z_ * 4 + y_ * 2 + x_
        self.cores = [(g, (c + k) % B) for k in range(1, B)]
        self.across_x = (pos(z, y, 1 - x), c)
        self.across_y = (pos(z, 1 - y, x), c)
        self.across_z = [(pos((z + k) % H, y, x), c) for k in range(1, H)]

    @staticmethod
    def sems_per_chunk(groups, batch):
        return 2 * (batch - 1) + 4 + (groups // 4 - 1)

    def barrier(self):
        sem = pltpu.get_barrier_semaphore()
        peers = self.cores + [self.across_x, self.across_y] + self.across_z
        for p in peers:
            pl.semaphore_signal(sem, inc=1, device_id=p, device_id_type=MESH)
        pl.semaphore_wait(sem, len(peers))

    def copy(self, j, n, src, dst, peer):
        return pltpu.make_async_remote_copy(
            src_ref=src, dst_ref=dst, send_sem=self.send.at[j, n], recv_sem=self.recv.at[j, n],
            device_id=peer, device_id_type=MESH,
        )

    def copies(self, j, phase):
        B, H, x, y = self.B, self.H, self.x, self.y
        s = self.s
        rows, width = s["r0"].shape[-2:]
        half = rows // 2
        q = j % RING
        if phase == 0:
            out = []
            for k, p in enumerate(self.cores):
                cols = pl.ds(pl.multiple_of(p[1] * width, width), width)
                out.append(self.copy(j, k, self.own(j).at[:, :, :, :, cols], s["r0"].at[q, k], p))
            return out
        n = B - 1
        if phase == 1:
            total = s["r0"].at[q, 0]
            return [
                self.copy(j, n, total.at[:, :, 1 - x, :half], s["r1"].at[q, 0], self.across_x),
                self.copy(j, n + 1, total.at[:, 1 - y, :, half:], s["r1"].at[q, 1], self.across_y),
            ]
        if phase == 2:
            return [
                self.copy(j, n + 2, s["r1"].at[q, 0, :, 1 - y], s["r2"].at[q, :, :half], self.across_y),
                self.copy(j, n + 3, s["r1"].at[q, 1, :, 1 - x], s["r2"].at[q, :, half:], self.across_x),
            ]
        n += 4
        if phase == 3:
            return [
                self.copy(j, n + k, s["r2"].at[q, p[0] // 4], s["r3"].at[q, k], p)
                for k, p in enumerate(self.across_z)
            ]
        n += H - 1
        cols = pl.ds(pl.multiple_of(self.c * width, width), width)
        place = s["out"].at[j, :, cols]
        return [self.copy(j, n + k, place, place, p) for k, p in enumerate(self.cores)]

    def start(self, j, phase):
        for d in self.copies(j, phase):
            d.start()

    def finish(self, j, phase):
        for d in self.copies(j, phase):
            d.wait()
        s, x, y, z, H = self.s, self.x, self.y, self.z, self.H
        rows, width = s["r0"].shape[-2:]
        half = rows // 2
        q = j % RING
        cols = pl.ds(pl.multiple_of(self.c * width, width), width)
        if phase == 0:
            own = self.own(j)

            def add(i, _):
                h, b = i // 4, i % 4
                t = own[h, b // 2, b % 2, :, cols].astype(f32)
                for k in range(self.B - 1):
                    t = t + s["r0"][q, k, h, b // 2, b % 2].astype(f32)
                s["r0"][q, 0, h, b // 2, b % 2] = t.astype(bf16)
                return _

            lax.fori_loop(0, 4 * H, add, 0)
        elif phase == 1:

            def add(h, _):
                for i in range(2):
                    a = s["r1"][q, 0, h, i].astype(f32) + s["r0"][q, 0, h, i, x, :half].astype(f32)
                    s["r1"][q, 0, h, i] = a.astype(bf16)
                    b = s["r1"][q, 1, h, i].astype(f32) + s["r0"][q, 0, h, y, i, half:].astype(f32)
                    s["r1"][q, 1, h, i] = b.astype(bf16)
                return _

            lax.fori_loop(0, H, add, 0)
        elif phase == 2:

            def add(h, _):
                a = s["r2"][q, h, :half].astype(f32) + s["r1"][q, 0, h, y].astype(f32)
                s["r2"][q, h, :half] = a.astype(bf16)
                b = s["r2"][q, h, half:].astype(f32) + s["r1"][q, 1, h, x].astype(f32)
                s["r2"][q, h, half:] = b.astype(bf16)
                return _

            lax.fori_loop(0, H, add, 0)
        elif phase == 3:
            t = s["r2"][q, z].astype(f32)
            for k in range(H - 1):
                t = t + s["r3"][q, k].astype(f32)
            s["out"][j, :, cols] = t

    @staticmethod
    def scratch(groups, batch, chunks, rows, cols):
        H, w = groups // 4, cols // batch
        return dict(
            r0=pltpu.VMEM((RING, batch - 1, H, 2, 2, rows, w), bf16),
            r1=pltpu.VMEM((RING, 2, H, 2, rows // 2, w), bf16),
            r2=pltpu.VMEM((RING, H, rows, w), bf16),
            r3=pltpu.VMEM((RING, H - 1, rows, w), bf16),
            out=pltpu.VMEM((chunks, rows, cols), f32),
        )

    def advance(self, step):
        static = isinstance(step, int)
        for phase in range(5, -1, -1):
            j = step - phase
            if static and not 0 <= j < self.chunks:
                continue
            if phase > 0:
                self.finish(j, phase - 1)
            if phase < 5:
                self.start(j, phase)


class Small:
    def __init__(self, ex, sems, total=None, mine=None, seen=None):
        self.ex, self.total, self.mine, self.seen = ex, total, mine, seen
        self.send, self.recv = sems

    @staticmethod
    def count(groups, batch):
        return batch - 1 + 2 + groups // 4 - 1

    def copies(self, phase):
        ex = self.ex
        peers = [ex.cores, [ex.across_x], [ex.across_y], ex.across_z][phase]
        first = [0, ex.B - 1, ex.B, ex.B + 1][phase]
        out = []
        for k, p in enumerate(peers):
            n = first + k
            if self.seen is None:
                src, dst = self.mine.at[phase], self.total.at[n]
            else:
                at = (ex.z, ex.y, ex.x, ex.c)[: 4 - phase]
                src = dst = self.seen.at[at]
            out.append(pltpu.make_async_remote_copy(
                src_ref=src, dst_ref=dst, send_sem=self.send.at[n], recv_sem=self.recv.at[n],
                device_id=p, device_id_type=MESH))
        return out

    def start(self, phase):
        for d in self.copies(phase):
            d.start()

    def finish(self, phase):
        for d in self.copies(phase):
            d.wait()
        if self.seen is None:
            ex = self.ex
            n = [ex.B - 1, 1, 1, ex.H - 1][phase]
            first = [0, ex.B - 1, ex.B, ex.B + 1][phase]
            t = self.mine[phase]
            for k in range(n):
                t = t + self.total[first + k]
            self.mine[phase + 1] = t


def back_kernel(groups, batch, per, n_chunks, *refs):
    (act_hbm, dbr_hbm, h2_hbm, dup_hbm, mixed_hbm, dat_hbm, dmix_hbm, qkv_hbm, e_hbm, h1_hbm, w_hbm, x_hbm, dmid_hbm,
     cos_ref, sin_ref, mod_ref, dmodb_ref, te_ref,
     dwo, uwo, owo, qwo, bias_out, early_out, late_out, fg_hbm, dmoda_ref,
     own, r0, r1, r2, r3, out, total, mine, early, late, etmp, ltmp,
     ebuf, dsb, qkv, mixed, dmix, dbr, h2, dat, dmid, fg,
     send, recv, ssum, rsum, sear, rear, slat, rlat, ld, eld, dld, fst, ost) = refs
    slots, d = mixed.shape
    H, rows = groups // 4, d // groups
    chunk = lambda strip: strip // per
    n_own = own.shape[0]
    ex = Exchange(groups, batch, lambda j: own.at[j % n_own], dict(r0=r0, r1=r1, r2=r2, r3=r3, out=out), (send, recv), n_chunks)
    sums = Small(ex, (ssum, rsum), total=total, mine=mine)
    gather_early = Small(ex, (sear, rear), seen=early)
    gather_late = Small(ex, (slat, rlat), seen=late)

    load = lambda k, src, dst: pltpu.make_async_copy(src, dst, ld.at[k])
    half = lambda ref, k: ref.at[:, k * d : (k + 1) * d]
    loads = [
        load(0, half(act_hbm, 0), ebuf.at[1, 0]), load(1, half(act_hbm, 1), ebuf.at[1, 1]), load(2, dbr_hbm, dbr),
        load(3, h2_hbm, h2), load(4, half(dup_hbm, 0), dsb.at[0]), load(5, half(dup_hbm, 1), dsb.at[1]),
        load(6, mixed_hbm, mixed), load(7, dat_hbm, dat), load(8, qkv_hbm, qkv), load(9, dmix_hbm, dmix),
    ]
    load_h1 = load(10, h1_hbm, h2)
    load_w = [load(11 + k, half(w_hbm, k), ebuf.at[k // 2, k % 2]) for k in range(3)]
    load_x = load(14, x_hbm, dat)
    load_e = lambda p, slot: pltpu.make_async_copy(e_hbm.at[pl.ds(2 * p, 2)], ebuf.at[slot], eld.at[slot])
    for t in loads:
        t.start()
    load_e(0, 0).start()

    for k in range(4 * d // STRIP):
        etmp[k : k + 1, :] = dmodb_ref[:, k * STRIP : (k + 1) * STRIP]
    t = te_ref[...].astype(f32)
    t = t * jax.nn.sigmoid(t)
    at = 4 * d // STRIP
    for k in range(d // STRIP):
        etmp[at + k : at + k + 1, :] = t[:, k * STRIP : (k + 1) * STRIP]
    at += d // STRIP
    etmp[at:, :] = jnp.zeros((etmp.shape[0] - at, STRIP), f32)
    early[ex.z, ex.y, ex.x, ex.c] = etmp[...].astype(bf16)
    mine[0] = jnp.zeros(mine.shape[1:], f32)
    ex.barrier()
    gather_early.start(0)

    done = [0]

    def service(ready, most):
        n = max(0, min(ready - done[0], most))
        for _ in range(n):
            ex.advance(done[0])
            done[0] += 1

    def column_sums(value, row, k):
        mine[0, row + k : row + k + 1, :] = jnp.sum(value.astype(f32), axis=0, keepdims=True)

    def wgrad_into(left, block_rows, rights, place, zs):
        parts = block_rows // rows

        def body(i, _):
            n = zs * 4 * block_rows
            lt = left(i * n, n).T
            for k, right in enumerate(rights):
                r = mm(lt, right(), NN).astype(bf16)
                for b in range(4 * zs):
                    for part in range(parts):
                        strip = place(k, part)
                        lo = b * block_rows + part * rows
                        off = (strip % per) * STRIP
                        own[chunk(strip) % n_own, i * zs + b // 4, (b // 2) % 2, b % 2, :, off : off + STRIP] = r[lo : lo + rows]
            return _

        lax.fori_loop(0, H // zs, body, 0)

    for k in (0, 1, 2):
        loads[k].wait()
    wide = lambda ref: lambda lo, n: ref[lo // d, :, pl.ds(pl.multiple_of(lo % d, 128), n)]
    flat = lambda ref: lambda lo, n: ref[:, pl.ds(pl.multiple_of(lo, 128), n)]
    cut = lambda ref, k: lambda: ref[:, k * STRIP : (k + 1) * STRIP]
    wgrad_into(wide(ebuf.at[1]), 2 * rows, [cut(dbr, k) for k in range(2)], lambda k, part: 2 * k + part, 2)
    for k in range(2):
        column_sums(cut(dbr, k)(), 12, k)
    gather_early.finish(0)
    gather_early.start(1)
    service(4 // per, 1)
    for k in (3, 4, 5):
        loads[k].wait()
    for h in range(2):
        wgrad_into(flat(h2), rows, [cut(dsb.at[h], k) for k in range(2)], lambda k, part: 4 + 2 * h + k, 2)
        for k in range(2):
            column_sums(cut(dsb.at[h], k)(), 8 + 2 * h, k)
        if h == 0:
            gather_early.finish(1)
            gather_early.start(2)
        service((6 + 2 * h) // per, 1)
    load_h1.start()
    for k in (6, 7):
        loads[k].wait()
    wgrad_into(flat(mixed), rows, [cut(dat, k) for k in range(2)], lambda k, part: 8 + k, 2)
    for k in range(2):
        column_sums(cut(dat, k)(), 6, k)
    gather_early.finish(2)
    gather_early.start(3)
    load_x.start()
    service(10 // per, 2)
    for k in (8, 9):
        loads[k].wait()
    gather_early.finish(3)
    lane = lax.broadcasted_iota(jnp.int32, (1, 128), 1)
    even = even_lanes(slots)
    pairs = d // 128
    at_once = 256

    def attention(p, slot):
        col = lambda off: pl.ds(pl.multiple_of(off + p * 128, 128), 128)
        qc, kc, vc = col(0), col(d), col(2 * d)
        q, k, v, do = qkv[:, qc], qkv[:, kc], qkv[:, vc], dmix[:, qc]
        dqs = []
        for h in range(2):
            own_lanes = lane < 64 if h == 0 else lane >= 64
            parts = []
            for a in range(0, slots, at_once):
                rws = pl.ds(a, at_once)
                t = dmix[rws, qc]
                t = jnp.where(own_lanes, t, jnp.zeros_like(t))
                inner = jnp.sum(t.astype(f32) * mixed[rws, qc].astype(f32), axis=1, keepdims=True)
                ds = (ebuf[slot, h, rws, :].astype(f32) * (mm(t, v, NT) - inner)).astype(bf16)
                dsb[h, rws, :] = ds
                parts.append(mm(ds, k, NN))
            dqs.append(jnp.concatenate(parts, axis=0))
        do_t, q_t = do.T, q.T
        dv = jnp.concatenate([mm(do_t[h * 64 : h * 64 + 64], ebuf[slot, h], NN) for h in range(2)], axis=0)
        dk = jnp.concatenate([mm(q_t[h * 64 : h * 64 + 64], dsb[h], NN) for h in range(2)], axis=0)
        cos, sin = cos_ref[...], -sin_ref[...]
        dq = jnp.where(lane < 64, dqs[0], dqs[1]) * 0.125
        qkv[:, qc] = turn(dq, cos, sin, even).astype(bf16)
        qkv[:, kc] = turn(dk.T, cos, sin, even).astype(bf16)
        qkv[:, vc] = dv.T.astype(bf16)

    for part in range(2):
        base = done[0]
        assert base >= 5
        ready = (10 if part == 0 else 13) // per
        n_half = pairs // 2
        n_serve = max(0, min(ready - base, n_half))

        def body(i, carry):
            p = part * n_half + i
            slot = p % 2
            load_e(p, slot).wait()

            @pl.when(p + 1 < pairs)
            def _():
                load_e(p + 1, 1 - slot).start()

            attention(p, slot)
            if n_serve:

                @pl.when(i < n_serve)
                def _():
                    ex.advance(base + i)

            return carry

        lax.fori_loop(0, n_half, body, 0)
        done[0] += n_serve
        if part == 0:
            load_h1.wait()
        else:
            for t in load_w:
                t.start()
        order = (0, 1, 2) if part == 0 else (2, 0, 1)
        rights = [cut(qkv, 2 * k + part) for k in order]
        wgrad_into(flat(h2), rows, rights, lambda k, _: 10 + 3 * part + k, 2)
        for k, r in zip(order, rights):
            column_sums(r(), 2 * k + part, 0)
        service((13 if part == 0 else 16) // per, 1)
    sums.start(0)
    tile = dmid.shape[1]
    tiles = slots // tile
    load_d = lambda i, slot: pltpu.make_async_copy(dmid_hbm.at[pl.ds(i * tile, tile)], dmid.at[slot], dld.at[slot])
    store_f = lambda i, slot: pltpu.make_async_copy(fg.at[slot], fg_hbm.at[pl.ds(i * tile, tile)], fst.at[slot])
    load_d(0, 0).start()
    load_x.wait()
    for t in load_w:
        t.wait()
    for i in range(tiles):
        slot = i % 2
        if i + 1 < tiles:
            load_d(i + 1, 1 - slot).start()
        rws = pl.ds(i * tile, tile)
        dh = (
            mm(qkv[rws, :d], ebuf[0, 0], NT) + mm(qkv[rws, d : 2 * d], ebuf[0, 1], NT) + mm(qkv[rws, 2 * d :], ebuf[1, 0], NT)
        )
        x = dat[rws, :].astype(f32)
        cen = x - jnp.mean(x, axis=1, keepdims=True)
        r = lax.rsqrt(jnp.mean(cen * cen, axis=1, keepdims=True) + EPS)
        n1 = cen * r
        psc = jnp.sum(dh * n1, axis=0, keepdims=True)
        psh = jnp.sum(dh, axis=0, keepdims=True)
        if i == 0:
            dmoda_ref[:, :d] = psh
            dmoda_ref[:, d:] = psc
        else:
            dmoda_ref[:, :d] += psh
            dmoda_ref[:, d:] += psc
        dn = dh * (1.0 + mod_ref[:, d : 2 * d])
        load_d(i, slot).wait()
        if i >= 2:
            store_f(i - 2, slot).wait()
        fg[slot] = dmid[slot] + r * (
            dn - jnp.mean(dn, axis=1, keepdims=True) - n1 * jnp.mean(dn * n1, axis=1, keepdims=True)
        )
        store_f(i, slot).start()
        if i < 3:
            sums.finish(i)
            sums.start(i + 1)
        service(n_chunks + 5, 1)
    for k in range(2 * d // 128):
        ltmp[k : k + 1, :] = dmoda_ref[:, k * 128 : (k + 1) * 128]
    late[ex.z, ex.y, ex.x, ex.c] = ltmp[...].astype(bf16)
    gather_late.start(0)
    sums.finish(3)
    for phase in range(4):
        service(n_chunks + 5, 1)
        gather_late.finish(phase)
        if phase < 3:
            gather_late.start(phase + 1)
    bias_out[...] = mine[4]
    for i in range(max(0, tiles - 2), tiles):
        store_f(i, i % 2).wait()
    service(n_chunks + 5, n_chunks + 5)
    dst = [dwo.at[part, :, k * STRIP : (k + 1) * STRIP] for k in range(2) for part in range(2)]
    dst += [uwo.at[:, k * STRIP : (k + 1) * STRIP] for k in range(4)]
    dst += [owo.at[:, k * STRIP : (k + 1) * STRIP] for k in range(2)]
    dst += [qwo.at[:, k * STRIP : (k + 1) * STRIP] for k in (0, 2, 4, 5, 1, 3)]
    stores = []
    for strip, a in enumerate(dst):
        off = (strip % per) * STRIP
        stores.append(pltpu.make_async_copy(out.at[chunk(strip), :, off : off + STRIP], a, ost.at[strip]))
    stores.append(pltpu.make_async_copy(early, early_out, ost.at[16]))
    stores.append(pltpu.make_async_copy(late, late_out, ost.at[17]))
    for t in stores:
        t.start()
    for t in stores:
        t.wait()


def backward(groups, batch, act, dbr, h2, dup, mixed, dat, dmix, qkv, e, h1, w, x, dmid, cos, sin, mod, dmodb, te):
    slots, d = mixed.shape
    H, rows = groups // 4, d // groups
    per = max(1, 128 * batch // STRIP)
    n_chunks = 16 // per
    S = jax.ShapeDtypeStruct
    hbm = pl.BlockSpec(memory_space=pl.ANY)
    vm = pl.BlockSpec(memory_space=pltpu.VMEM)
    V = pltpu.VMEM
    sc = Exchange.scratch(groups, batch, n_chunks, rows, per * STRIP)
    ns, nsm = Exchange.sems_per_chunk(groups, batch), Small.count(groups, batch)
    dma = pltpu.SemaphoreType.DMA
    tile = 256
    seen = (H, 2, 2, batch)
    return pl.pallas_call(
        lambda *a: back_kernel(groups, batch, per, n_chunks, *a),
        in_specs=[hbm] * 13 + [vm] * 5,
        out_specs=[hbm] * 4 + [vm, hbm, hbm, hbm, vm],
        out_shape=[S((2, rows, d), f32), S((rows, 2 * d), f32), S((rows, d), f32), S((rows, 3 * d), f32),
                   S((16, STRIP), f32), S(seen + (16, STRIP), bf16), S(seen + (16, 128), bf16),
                   S((slots, d), f32), S((1, 2 * d), f32)],
        scratch_shapes=[V((-(-10 // per), H, 2, 2, rows, per * STRIP), bf16),
                        sc["r0"], sc["r1"], sc["r2"], sc["r3"], sc["out"],
                        V((nsm, 16, STRIP), f32), V((5, 16, STRIP), f32), V(seen + (16, STRIP), bf16), V(seen + (16, 128), bf16),
                        V((16, STRIP), f32), V((16, 128), f32),
                        V((2, 2, slots, slots), bf16), V((2, slots, slots), bf16), V((slots, 3 * d), bf16), V((slots, d), bf16),
                        V((slots, d), bf16), V((slots, d), bf16), V((slots, d), bf16), V((slots, d), bf16),
                        V((2, tile, d), f32), V((2, tile, d), f32),
                        dma((n_chunks, ns)), dma((n_chunks, ns)), dma((nsm,)), dma((nsm,)), dma((nsm,)), dma((nsm,)),
                        dma((nsm,)), dma((nsm,)), dma((15,)), dma((2,)), dma((2,)), dma((2,)), dma((18,))],
        compiler_params=pltpu.CompilerParams(vmem_limit_bytes=67_000_000, collective_id=0, has_side_effects=True),
        name="backward",
    )(act, dbr, h2, dup, mixed, dat, dmix, qkv, e, h1, w, x, dmid, cos, sin, mod, dmodb, te)


def mods_kernel(em_ref, dm_ref, own_ref, w_ref, te_ref, wg_ref, bg_ref, tg_ref):
    i = pl.program_id(0)
    dm = dm_ref[...]
    wg_ref[...] = mm(em_ref[...], dm, TN)
    bg_ref[...] = jnp.sum(dm.astype(f32), axis=0, keepdims=True)
    part = mm(jnp.broadcast_to(own_ref[...], (8, own_ref.shape[1])), w_ref[...], NT)[:1]

    @pl.when(i == 0)
    def _():
        tg_ref[...] = part

    @pl.when(i > 0)
    def _():
        tg_ref[...] += part

    @pl.when(i == pl.num_programs(0) - 1)
    def _():
        t = te_ref[...].astype(f32)
        s = jax.nn.sigmoid(t)
        tg_ref[...] = tg_ref[...] * (s * (1.0 + t * (1.0 - s)))


def mods(em, dm, own, w, te):
    n, rows = em.shape
    d, wide = w.shape
    col = lambda r: pl.BlockSpec((r, d), lambda i: (0, i))
    S = jax.ShapeDtypeStruct
    return pl.pallas_call(
        mods_kernel,
        grid=(wide // d,),
        in_specs=[full((n, rows)), col(n), col(1), col(d), full((1, d))],
        out_specs=[col(rows), col(1), pl.BlockSpec((1, d), lambda i: (0, 0))],
        out_shape=[S((rows, wide), f32), S((1, wide), f32), S((1, d), f32)],
        compiler_params=params(),
        name="mods",
    )(em, dm, own, w, te)


def solution(mesh):
    groups, batch = mesh.shape["groups"], mesh.shape["batch"]

    def body(frames, te, lengths, mod_w, mod_b, qkv_w, qkv_b, out_w, out_b, up_w, up_b, down_w, down_b, cot):
        x, ct = frames[0], cot[0]
        slots, d = x.shape
        cos, sin = rot_tables(slots, d // HEADS)
        row = lambda b: b.reshape(1, -1)
        mod = modulation(te, mod_w, row(mod_b))
        h1, qkv = project_qkv(x, mod, qkv_w, row(qkv_b), cos, sin)
        mixed, e, linv = attend(lengths, qkv)
        out, h2, act, dbr, dup, dat, dmix, dmid, dmod_b = middle_part(
            lengths, mixed, x, ct, mod, linv, out_w, row(out_b), up_w, row(up_b), down_w, row(down_b)
        )
        dws, uws, ows, qws, bs, early, late, fg, dmod_a = backward(
            groups, batch, act, dbr, h2, dup, mixed, dat, dmix, qkv, e, h1, qkv_w, x, dmid, cos, sin, mod, dmod_b, te
        )
        rows, n = d // groups, groups * batch
        early, late = early.reshape(n, 16 * STRIP), late.reshape(n, 2 * d)
        g = lax.axis_index("groups")
        em = lax.dynamic_slice_in_dim(early, 4 * d + g * rows, rows, 1)
        dm = jnp.concatenate([late, early[:, : 4 * d]], axis=1)
        own = jnp.concatenate([dmod_a, dmod_b], axis=1).astype(bf16)
        mod_wg, mod_bg, time_grad = mods(em, dm, own, mod_w, te)
        bs = bs.reshape(16 * STRIP)
        cut = lambda v, off, n: lax.dynamic_slice_in_dim(v, off + g * n, n)
        return (out[None], fg[None], time_grad, mod_wg, cut(mod_bg[0], 0, 6 * rows), qws, cut(bs, 0, 3 * rows),
                ows, cut(bs, 3 * d, rows), uws, cut(bs, 4 * d, 2 * rows), dws.reshape(2 * rows, d), cut(bs, 6 * d, rows))

    split = P(("groups", "batch"))
    own = P("groups")
    return jax.shard_map(
        body, mesh=mesh,
        in_specs=(split,) * 3 + (P(),) * 10 + (split,),
        out_specs=(split,) * 3 + (own,) * 10,
        check_vma=False,
    )
```

time: 325 us -> 257 us (0.79); the launches traced: 324 us -> 252 us
  Pallas kernels: 287 us -> 230 us
  matrix products: 10.3 us -> 0 us
  other arithmetic: 7.95 us -> 2.13 us
    pallas_call x9 -> x2, Pallas kernels: 200 us -> 143 us  [the longest x1 134 us: backward(): pl.pallas_call(lambda *a: back_kernel(groups, batch, per, n_chunks, *a),...]
    dot_general x2 -> x0, matrix products: 10.3 us -> none  [mm(): return lax.dot_general(a, b, (dims, ((), ())), preferred_element_type=f32)]
    another operation x5 -> x2, other arithmetic: 7 us -> 0.72 us  [the longest x1 6.2 us: body(): qkv3 = jnp.stack([p[0].reshape(H, 2, 2, rows, d) for p in parts])]
    unnamed x34 -> x28, local copies, waits for them, and re-layouts: 9.49 us -> 10.4 us
where the time goes in v2:
time: 257 us; the launch traced here: 252 us
  Pallas kernels  230 us (89%)
  local copies, waits for them, and re-layouts  17.9 us (7%)
    pallas_call x1, Pallas kernels, backward(): pl.pallas_call(lambda *a: back_kernel(groups, batch, per, n_chunks, *a),...  134 us
    pallas_call x1, Pallas kernels, middle_part(): pl.pallas_call(middle_kernel, grid_spec=pltpu.PrefetchScalarGridSpec(num_...  38.8 us
    pallas_call x1, Pallas kernels, attend(): pl.pallas_call(lambda *a: attend_kernel(*a, rows_at_once=rows_at_once), g...  27.7 us
    pallas_call x1, Pallas kernels, project_qkv(): pl.pallas_call(qkv_kernel, grid=(slots // tile,), in_specs=[row(d), full(...  12.7 us
    unnamed x28, local copies, waits for them, and re-layouts  10.4 us
    pallas_call x1, Pallas kernels, mods(): pl.pallas_call(mods_kernel, grid=(wide // d,), in_specs=[full((n, rows)),...  9.16 us
    pallas_call x1, Pallas kernels, modulation(): pl.pallas_call(mod_kernel, grid=(n // blk,), in_specs=[full((1, d)), pl.B...  7.56 us

profile of v2, /device:TPU:0, one launch (start us, length us, event | category | flops | bytes accessed | tf_op | source)
XLA Modules:
  0.0 251.7 jit_solution(15233815965631494845)
XLA Ops:
  1.3 1.3 reshape.82.b_ref
  2.6 7.6 %modulation.1.mod_ref.a_15_ = f32[1,6144]{1,0:T(1,128)} custom-call(bf16[1,1024]{1,0:T(2,128)(2,1)} %te_ref.3, bf16[1024,6144]{1,0:T(8,128)(2,1)} %w_ref.5, bf16[1,6144]{1,0:T(2,128)(2,1)} %reshape.82.b_ref), custom_call_target="tpu_custom_call" | custom-call | tf_op jit(solution)/shard_map/modulation/pallas_call | solution.py:59
  10.2 0.6 reshape.83.b_ref
  10.8 12.7 %project_qkv.1 = (bf16[1024,1024]{1,0:T(8,128)(2,1)}, bf16[1024,3072]{1,0:T(8,128)(2,1)}) custom-call(bf16[1024,1024]{1,0:T(8,128)(2,1)} %bitcast.15, f32[1,6144]{1,0:T(1,128)} %modulation.1.mod_ref.a_15_, bf16[1024,3072]{1,0:T(8,128)(2,1)} %a_10_.1, bf16[1,3072]{1,0:T(2,128)(2,1)} %reshape.83.b_ref, f32[1024,128]{1,0:T(8,128)} %constant.36.clone.cos_ref.a_13_, ...), custom_call_target="tpu_custom_call" | custom-call | tf_op jit(solution)/shard_map/project_qkv/pallas_call | solution.py:95
  23.5 0.0 copy-start.9
  23.5 27.7 %attend.1 = (bf16[1024,1024]{1,0:T(8,128)(2,1)}, bf16[16,1024,1024]{2,1,0:T(8,128)(2,1)}, f32[1024,1024]{1,0:T(8,128)}) custom-call(s32[1]{0:T(128)S(6)} %copy.39.a_0_.len_ref, bf16[1024,3072]{1,0:T(8,128)(2,1)} %get-tuple-element.39.a_1_.a_2_.a_3_.a_7_, bf16[1024,3072]{1,0:T(8,128)(2,1)} %get-tuple-element.39.a_1_.a_2_.a_3_.a_7_, ...), custom_call_target="tpu_custom_call" | custom-call | tf_op jit(solution)/shard_map/attend/pallas_call | solution.py:135
  51.2 0.0 copy-done.8
  51.2 0.6 reshape.84.ob_ref
  51.8 0.6 reshape.85.ub_ref
  52.4 0.0 copy-done.9
  52.4 0.6 reshape.86.db_ref
  53.0 38.8 %middle_part.1 = (bf16[1024,1024]{1,0:T(8,128)(2,1)}, bf16[1024,1024]{1,0:T(8,128)(2,1)}, bf16[1024,2048]{1,0:T(8,128)(2,1)}, bf16[1024,1024]{1,0:T(8,128)(2,1)}...) custom-call(s32[1]{0:T(128)S(6)} %copy.39.a_0_.len_ref, ...), custom_call_target="tpu_custom_call" | custom-call | tf_op jit(solution)/shard_map/middle_part/pallas_call | solution.py:215
  91.8 0.0 copy-start.4
  91.8 133.9 %backward.1 = (f32[2,64,1024]{2,1,0:T(8,128)}, f32[64,2048]{1,0:T(8,128)}, f32[64,1024]{1,0:T(8,128)}, f32[64,3072]{1,0:T(8,128)}, f32[16,512]{1,0:T(8,128)}, /*...) custom-call(bf16[1024,2048]{1,0:T(8,128)(2,1)} %get-tuple-element.43, ...), custom_call_target="tpu_custom_call" | custom-call | tf_op jit(solution)/shard_map/backward/pallas_call | solution.py:684
  225.7 1.3 copy.29
  227.1 0.7 constant_dynamic-slice_fusion.em_ref
  227.8 0.9 copy.33
  228.7 0.8 pad_maximum_fusion.dm_ref
  229.5 0.7 convert.6
  230.2 0.6 pad_maximum_fusion.1.own_ref
  230.9 9.2 %mods.1 = (f32[64,6144]{1,0:T(8,128)}, f32[1,6144]{1,0:T(1,128)}, f32[1,1024]{1,0:T(1,128)}) custom-call(bf16[32,64]{1,0:T(8,128)(2,1)} %constant_dynamic-slice_fusion.em_ref, bf16[32,6144]{1,0:T(8,128)(2,1)} %pad_maximum_fusion.dm_ref, bf16[1,6144]{1,0:T(2,128)(2,1)} %pad_maximum_fusion.1.own_ref, bf16[1024,6144]{1,0:T(8,128)(2,1)} %w_ref.5, ...), custom_call_target="tpu_custom_call" | custom-call | tf_op jit(solution)/shard_map/mods/pallas_call | solution.py:732
  240.0 1.3 dynamic-slice_reduce_fusion
  241.3 0.0 copy-done.5
  241.3 0.6 dynamic_slice.23
  242.0 0.6 fusion
  242.5 0.6 dynamic_slice.25
  243.1 4.9 %copy.40 = f32[1,1024,1024]{2,1,0:T(8,128)} copy(f32[1,1024,1024]{2,1,0:T(8,128)} %bitcast.18) | data formatting | bytes 8388608
  248.1 0.0 copy-done
  248.1 0.9 copy.41
  249.0 0.7 copy.42
  249.7 0.8 copy.43
  250.5 0.8 copy.44
  (17 shorter events, 0.1 us)
Async XLA Ops:
  2.6 7.6 %copy-start.6 = (bf16[3072]{0:T(1024)(128)(2,1)S(1)}, bf16[3072]{0:T(1024)(128)(2,1)}, u32[]{:S(2)}) copy-start(bf16[3072]{0:T(1024)(128)(2,1)} %param.22) | copy-start | bytes 18436
  23.5 27.7 %copy-start.8 = (bf16[1024]{0:T(1024)(128)(2,1)S(1)}, bf16[1024]{0:T(1024)(128)(2,1)}, u32[]{:S(2)}) copy-start(bf16[1024]{0:T(1024)(128)(2,1)} %param.24) | copy-start | bytes 6148
  23.5 28.3 %copy-start.7 = (bf16[2048]{0:T(1024)(128)(2,1)S(1)}, bf16[2048]{0:T(1024)(128)(2,1)}, u32[]{:S(2)}) copy-start(bf16[2048]{0:T(1024)(128)(2,1)} %param.26) | copy-start | bytes 12292
  23.5 28.9 %copy-start.9 = (bf16[1024]{0:T(1024)(128)(2,1)S(1)}, bf16[1024]{0:T(1024)(128)(2,1)}, u32[]{:S(2)}) copy-start(bf16[1024]{0:T(1024)(128)(2,1)} %param.28) | copy-start | bytes 6148
  91.8 137.7 %copy-start.4 = (f32[1,4096]{1,0:T(1,128)S(1)}, f32[1,4096]{1,0:T(1,128)}, u32[]{:S(2)}) copy-start(f32[1,4096]{1,0:T(1,128)} %get-tuple-element.52.a_16_) | copy-start | bytes 49156
  230.9 10.4 %copy-start.5 = (f32[16,512]{1,0:T(8,128)S(1)}, f32[16,512]{1,0:T(8,128)}, u32[]{:S(2)}) copy-start(f32[16,512]{1,0:T(8,128)} %get-tuple-element.61) | copy-start | bytes 98308
  243.1 4.9 %copy-start = (f32[64,3072]{1,0:T(8,128)S(1)}, f32[64,3072]{1,0:T(8,128)}, u32[]{:S(2)}) copy-start(f32[64,3072]{1,0:T(8,128)} %get-tuple-element.85) | copy-start | bytes 2359300
  243.1 5.8 %copy-start.3 = (f32[64,1024]{1,0:T(8,128)S(1)}, f32[64,1024]{1,0:T(8,128)}, u32[]{:S(2)}) copy-start(f32[64,1024]{1,0:T(8,128)} %get-tuple-element.87) | copy-start | bytes 786436
  243.1 6.5 %copy-start.2 = (f32[64,2048]{1,0:T(8,128)S(1)}, f32[64,2048]{1,0:T(8,128)}, u32[]{:S(2)}) copy-start(f32[64,2048]{1,0:T(8,128)} %get-tuple-element.89) | copy-start | bytes 1572868
  243.1 7.3 %copy-start.1 = (f32[2,64,1024]{2,1,0:T(8,128)S(1)}, f32[2,64,1024]{2,1,0:T(8,128)}, u32[]{:S(2)}) copy-start(f32[2,64,1024]{2,1,0:T(8,128)} %get-tuple-element.64) | copy-start | bytes 1572868

commit v3 on v2

--- a/solution.py
+++ b/solution.py
@@ -24,13 +24,19 @@
     return pltpu.CompilerParams(vmem_limit_bytes=VMEM_LIMIT, **kw)
 
 
+BLOCK = 32
+
+
 def rot_tables(slots, size):
-    pos = np.arange(slots, dtype=np.float64)[:, None]
     pair = np.arange(size // 2, dtype=np.float64)[None, :]
-    ang = pos * np.power(10000.0, -2.0 * pair / size)
-    cos = np.repeat(np.cos(ang), 2, axis=1)
-    sin = np.repeat(np.sin(ang), 2, axis=1) * np.where(np.arange(size) % 2 == 0, -1.0, 1.0)
-    return np.tile(cos, (1, 2)).astype(np.float32), np.tile(sin, (1, 2)).astype(np.float32)
+    sign = np.where(np.arange(size) % 2 == 0, -1.0, 1.0)
+    out = []
+    for pos in (np.arange(0, slots, BLOCK), np.arange(BLOCK)):
+        ang = pos.astype(np.float64)[:, None] * np.power(10000.0, -2.0 * pair / size)
+        cos = np.repeat(np.cos(ang), 2, axis=1)
+        sin = np.repeat(np.sin(ang), 2, axis=1) * sign
+        out += [np.tile(cos, (1, 2)).astype(np.float32), np.tile(sin, (1, 2)).astype(np.float32)]
+    return out
 
 
 def turn(x, cos, sin, even):
@@ -67,13 +73,18 @@
     )(te, w, b)
 
 
-def qkv_kernel(x_ref, mod_ref, w_ref, b_ref, cos_ref, sin_ref, h_ref, qkv_ref):
+def qkv_kernel(x_ref, mod_ref, w_ref, b_ref, cosa_ref, sina_ref, cosb_ref, sinb_ref, h_ref, qkv_ref, cos_ref, sin_ref):
     d = x_ref.shape[1]
     x = x_ref[...].astype(f32)
     c = x - jnp.mean(x, axis=1, keepdims=True)
     r = lax.rsqrt(jnp.mean(c * c, axis=1, keepdims=True) + EPS)
     h = (c * r * (1.0 + mod_ref[:, d : 2 * d]) + mod_ref[:, :d]).astype(bf16)
     h_ref[...] = h
+    cosb, sinb = cosb_ref[...], sinb_ref[...]
+    for k in range(x.shape[0] // BLOCK):
+        cosa, sina = cosa_ref[k : k + 1, :], sina_ref[k : k + 1, :]
+        cos_ref[k * BLOCK : (k + 1) * BLOCK, :] = cosa * cosb - sina * sinb
+        sin_ref[k * BLOCK : (k + 1) * BLOCK, :] = sina * cosb + cosa * sinb
     cos, sin = cos_ref[...], sin_ref[...]
     even = even_lanes(x.shape[0])
     step = 512
@@ -89,18 +100,20 @@
             qkv_ref[:, col : col + 128] = z.astype(bf16)
 
 
-def project_qkv(x, mod, w, b, cos, sin, tile=256):
+def project_qkv(x, mod, w, b, tables, tile=256):
     slots, d = x.shape
     row = lambda n: pl.BlockSpec((tile, n), lambda i: (i, 0))
     return pl.pallas_call(
         qkv_kernel,
         grid=(slots // tile,),
-        in_specs=[row(d), full(mod.shape), full(w.shape), full(b.shape), row(128), row(128)],
-        out_specs=[row(d), row(3 * d)],
-        out_shape=[jax.ShapeDtypeStruct((slots, d), bf16), jax.ShapeDtypeStruct((slots, 3 * d), bf16)],
+        in_specs=[row(d), full(mod.shape), full(w.shape), full(b.shape)]
+        + [pl.BlockSpec((tile // BLOCK, 128), lambda i: (i, 0))] * 2 + [full((BLOCK, 128))] * 2,
+        out_specs=[row(d), row(3 * d), row(128), row(128)],
+        out_shape=[jax.ShapeDtypeStruct((slots, d), bf16), jax.ShapeDtypeStruct((slots, 3 * d), bf16),
+                   jax.ShapeDtypeStruct((slots, 128), f32), jax.ShapeDtypeStruct((slots, 128), f32)],
         compiler_params=params(),
         name="project_qkv",
-    )(x, mod, w, b, cos, sin)
+    )(x, mod, w, b, *tables)
 
 
 def attend_kernel(len_ref, q_ref, k_ref, v_ref, o_ref, e_ref, linv_ref, *, rows_at_once):
@@ -232,12 +245,19 @@
 
 MESH = pl.DeviceIdType.MESH
 STRIP = 512
-RING = 4
+RINGS = dict(r0=4, r1=6, r2=6, r3=4)
+DELAYS = (0, 1, 3, 5, 7, 8)
 
 
 class Exchange:
-    def __init__(self, groups, batch, own, s, sems, chunks):
+    def __init__(self, groups, batch, own, s, sems, ready, chunks):
         self.G, self.B, self.H, self.chunks = groups, batch, groups // 4, chunks
+        self.plan = []
+        while len(self.plan) - self.plan.count(None) < chunks:
+            n = len(self.plan) - self.plan.count(None)
+            self.plan.append(n if len(self.plan) >= len(ready) or n < ready[len(self.plan)] else None)
+        self.gaps = [t for t, c in enumerate(self.plan) if c is None]
+        self.last = len(self.plan) - 1 + DELAYS[-1]
         self.own = own
         self.s = s
         self.send, self.recv = sems
@@ -272,29 +292,29 @@
         s = self.s
         rows, width = s["r0"].shape[-2:]
         half = rows // 2
-        q = j % RING
+        q0, q1, q2, q3 = (j % RINGS[k] for k in ("r0", "r1", "r2", "r3"))
         if phase == 0:
             out = []
             for k, p in enumerate(self.cores):
                 cols = pl.ds(pl.multiple_of(p[1] * width, width), width)
-                out.append(self.copy(j, k, self.own(j).at[:, :, :, :, cols], s["r0"].at[q, k], p))
+                out.append(self.copy(j, k, self.own(j).at[:, :, :, :, cols], s["r0"].at[q0, k], p))
             return out
         n = B - 1
         if phase == 1:
-            total = s["r0"].at[q, 0]
+            total = s["r0"].at[q0, 0]
             return [
-                self.copy(j, n, total.at[:, :, 1 - x, :half], s["r1"].at[q, 0], self.across_x),
-                self.copy(j, n + 1, total.at[:, 1 - y, :, half:], s["r1"].at[q, 1], self.across_y),
+                self.copy(j, n, total.at[:, :, 1 - x, :half], s["r1"].at[q1, 0], self.across_x),
+                self.copy(j, n + 1, total.at[:, 1 - y, :, half:], s["r1"].at[q1, 1], self.across_y),
             ]
         if phase == 2:
             return [
-                self.copy(j, n + 2, s["r1"].at[q, 0, :, 1 - y], s["r2"].at[q, :, :half], self.across_y),
-                self.copy(j, n + 3, s["r1"].at[q, 1, :, 1 - x], s["r2"].at[q, :, half:], self.across_x),
+                self.copy(j, n + 2, s["r1"].at[q1, 0, :, 1 - y], s["r2"].at[q2, :, :half], self.across_y),
+                self.copy(j, n + 3, s["r1"].at[q1, 1, :, 1 - x], s["r2"].at[q2, :, half:], self.across_x),
             ]
         n += 4
         if phase == 3:
             return [
-                self.copy(j, n + k, s["r2"].at[q, p[0] // 4], s["r3"].at[q, k], p)
+                self.copy(j, n + k, s["r2"].at[q2, p[0] // 4], s["r3"].at[q3, k], p)
                 for k, p in enumerate(self.across_z)
             ]
         n += H - 1
@@ -312,68 +332,88 @@
         s, x, y, z, H = self.s, self.x, self.y, self.z, self.H
         rows, width = s["r0"].shape[-2:]
         half = rows // 2
-        q = j % RING
+        q0, q1, q2, q3 = (j % RINGS[k] for k in ("r0", "r1", "r2", "r3"))
         cols = pl.ds(pl.multiple_of(self.c * width, width), width)
         if phase == 0:
             own = self.own(j)
 
-            def add(i, _):
-                h, b = i // 4, i % 4
-                t = own[h, b // 2, b % 2, :, cols].astype(f32)
-                for k in range(self.B - 1):
-                    t = t + s["r0"][q, k, h, b // 2, b % 2].astype(f32)
-                s["r0"][q, 0, h, b // 2, b % 2] = t.astype(bf16)
+            def add(h, _):
+                t = own[h, :, :, :, cols]
+                if self.B == 2:
+                    t = t + s["r0"][q0, 0, h]
+                else:
+                    t = t.astype(f32)
+                    for k in range(self.B - 1):
+                        t = t + s["r0"][q0, k, h].astype(f32)
+                s["r0"][q0, 0, h] = t.astype(bf16)
                 return _
 
-            lax.fori_loop(0, 4 * H, add, 0)
+            lax.fori_loop(0, H, add, 0)
         elif phase == 1:
 
             def add(h, _):
-                for i in range(2):
-                    a = s["r1"][q, 0, h, i].astype(f32) + s["r0"][q, 0, h, i, x, :half].astype(f32)
-                    s["r1"][q, 0, h, i] = a.astype(bf16)
-                    b = s["r1"][q, 1, h, i].astype(f32) + s["r0"][q, 0, h, y, i, half:].astype(f32)
-                    s["r1"][q, 1, h, i] = b.astype(bf16)
+                s["r1"][q1, 0, h] = s["r1"][q1, 0, h] + s["r0"][q0, 0, h, :, x, :half]
+                s["r1"][q1, 1, h] = s["r1"][q1, 1, h] + s["r0"][q0, 0, h, y, :, half:]
                 return _
 
             lax.fori_loop(0, H, add, 0)
         elif phase == 2:
-
-            def add(h, _):
-                a = s["r2"][q, h, :half].astype(f32) + s["r1"][q, 0, h, y].astype(f32)
-                s["r2"][q, h, :half] = a.astype(bf16)
-                b = s["r2"][q, h, half:].astype(f32) + s["r1"][q, 1, h, x].astype(f32)
-                s["r2"][q, h, half:] = b.astype(bf16)
-                return _
-
-            lax.fori_loop(0, H, add, 0)
+            s["r2"][q2, :, :half] = s["r2"][q2, :, :half] + s["r1"][q1, 0, :, y]
+            s["r2"][q2, :, half:] = s["r2"][q2, :, half:] + s["r1"][q1, 1, :, x]
         elif phase == 3:
-            t = s["r2"][q, z].astype(f32)
+            t = s["r2"][q2, z].astype(f32)
             for k in range(H - 1):
-                t = t + s["r3"][q, k].astype(f32)
+                t = t + s["r3"][q3, k].astype(f32)
             s["out"][j, :, cols] = t
 
     @staticmethod
     def scratch(groups, batch, chunks, rows, cols):
         H, w = groups // 4, cols // batch
         return dict(
-            r0=pltpu.VMEM((RING, batch - 1, H, 2, 2, rows, w), bf16),
-            r1=pltpu.VMEM((RING, 2, H, 2, rows // 2, w), bf16),
-            r2=pltpu.VMEM((RING, H, rows, w), bf16),
-            r3=pltpu.VMEM((RING, H - 1, rows, w), bf16),
+            r0=pltpu.VMEM((RINGS["r0"], batch - 1, H, 2, 2, rows, w), bf16),
+            r1=pltpu.VMEM((RINGS["r1"], 2, H, 2, rows // 2, w), bf16),
+            r2=pltpu.VMEM((RINGS["r2"], H, rows, w), bf16),
+            r3=pltpu.VMEM((RINGS["r3"], H - 1, rows, w), bf16),
             out=pltpu.VMEM((chunks, rows, cols), f32),
         )
 
-    def advance(self, step):
-        static = isinstance(step, int)
+    def tick(self, t, first=None, final=None):
+        static = isinstance(t, int)
+        if static:
+            first = final = t
+        n = len(self.plan)
         for phase in range(5, -1, -1):
-            j = step - phase
-            if static and not 0 <= j < self.chunks:
+            lo, hi = first - DELAYS[phase], final - DELAYS[phase]
+            j = t - DELAYS[phase]
+            if hi < 0 or lo >= n or (static and self.plan[j] is None):
                 continue
-            if phase > 0:
-                self.finish(j, phase - 1)
-            if phase < 5:
-                self.start(j, phase)
+
+            def act(phase=phase, j=j):
+                c = self.plan[j] if static else j
+                if not static:
+                    for g in self.gaps:
+                        if g < lo:
+                            c = c - 1
+                        elif g <= hi:
+                            c = c - jnp.where(j > g, 1, 0)
+                if phase > 0:
+                    self.finish(c, phase - 1)
+                if phase < 5:
+                    self.start(c, phase)
+
+            conds = []
+            if lo < 0:
+                conds.append(j >= 0)
+            if hi >= n:
+                conds.append(j < n)
+            conds += [j != g for g in self.gaps if lo <= g <= hi]
+            if static or not conds:
+                act()
+            else:
+                ok = conds[0]
+                for c in conds[1:]:
+                    ok = jnp.logical_and(ok, c)
+                pl.when(ok)(act)
 
 
 class Small:
@@ -430,7 +470,11 @@
     H, rows = groups // 4, d // groups
     chunk = lambda strip: strip // per
     n_own = own.shape[0]
-    ex = Exchange(groups, batch, lambda j: own.at[j % n_own], dict(r0=r0, r1=r1, r2=r2, r3=r3, out=out), (send, recv), n_chunks)
+    pairs = d // 128
+    n_half = pairs // 2
+    ready = [4, 6, 8, 10, 10] + [10] * n_half + [13] * (1 + n_half) + [16]
+    ex = Exchange(groups, batch, lambda j: own.at[j % n_own], dict(r0=r0, r1=r1, r2=r2, r3=r3, out=out), (send, recv),
+                  [n // per for n in ready], n_chunks)
     sums = Small(ex, (ssum, rsum), total=total, mine=mine)
     gather_early = Small(ex, (sear, rear), seen=early)
     gather_late = Small(ex, (slat, rlat), seen=late)
@@ -446,9 +490,8 @@
     load_w = [load(11 + k, half(w_hbm, k), ebuf.at[k // 2, k % 2]) for k in range(3)]
     load_x = load(14, x_hbm, dat)
     load_e = lambda p, slot: pltpu.make_async_copy(e_hbm.at[pl.ds(2 * p, 2)], ebuf.at[slot], eld.at[slot])
-    for t in loads:
+    for t in loads[:3]:
         t.start()
-    load_e(0, 0).start()
 
     for k in range(4 * d // STRIP):
         etmp[k : k + 1, :] = dmodb_ref[:, k * STRIP : (k + 1) * STRIP]
@@ -464,16 +507,8 @@
     ex.barrier()
     gather_early.start(0)
 
-    done = [0]
-
-    def service(ready, most):
-        n = max(0, min(ready - done[0], most))
-        for _ in range(n):
-            ex.advance(done[0])
-            done[0] += 1
-
     def column_sums(value, row, k):
-        mine[0, row + k : row + k + 1, :] = jnp.sum(value.astype(f32), axis=0, keepdims=True)
+        mine[0, pl.ds(row + k, 1), :] = jnp.sum(value.astype(f32), axis=0, keepdims=True)
 
     def wgrad_into(left, block_rows, rights, place, zs):
         parts = block_rows // rows
@@ -488,24 +523,31 @@
                         strip = place(k, part)
                         lo = b * block_rows + part * rows
                         off = (strip % per) * STRIP
-                        own[chunk(strip) % n_own, i * zs + b // 4, (b // 2) % 2, b % 2, :, off : off + STRIP] = r[lo : lo + rows]
+                        cols = pl.ds(off if isinstance(off, int) else pl.multiple_of(off, STRIP), STRIP)
+                        own[chunk(strip) % n_own, i * zs + b // 4, (b // 2) % 2, b % 2, :, cols] = r[lo : lo + rows]
             return _
 
         lax.fori_loop(0, H // zs, body, 0)
 
     for k in (0, 1, 2):
         loads[k].wait()
+    for k in (3, 4, 5, 6, 7):
+        loads[k].start()
     wide = lambda ref: lambda lo, n: ref[lo // d, :, pl.ds(pl.multiple_of(lo % d, 128), n)]
     flat = lambda ref: lambda lo, n: ref[:, pl.ds(pl.multiple_of(lo, 128), n)]
-    cut = lambda ref, k: lambda: ref[:, k * STRIP : (k + 1) * STRIP]
+    strip_at = lambda k: pl.ds(k * STRIP if isinstance(k, int) else pl.multiple_of(k * STRIP, STRIP), STRIP)
+    cut = lambda ref, k: lambda: ref[:, strip_at(k)]
     wgrad_into(wide(ebuf.at[1]), 2 * rows, [cut(dbr, k) for k in range(2)], lambda k, part: 2 * k + part, 2)
     for k in range(2):
         column_sums(cut(dbr, k)(), 12, k)
     gather_early.finish(0)
     gather_early.start(1)
-    service(4 // per, 1)
+    ex.tick(0)
     for k in (3, 4, 5):
         loads[k].wait()
+    for k in (8, 9):
+        loads[k].start()
+    load_e(0, 0).start()
     for h in range(2):
         wgrad_into(flat(h2), rows, [cut(dsb.at[h], k) for k in range(2)], lambda k, part: 4 + 2 * h + k, 2)
         for k in range(2):
@@ -513,7 +555,7 @@
         if h == 0:
             gather_early.finish(1)
             gather_early.start(2)
-        service((6 + 2 * h) // per, 1)
+        ex.tick(1 + h)
     load_h1.start()
     for k in (6, 7):
         loads[k].wait()
@@ -523,13 +565,13 @@
     gather_early.finish(2)
     gather_early.start(3)
     load_x.start()
-    service(10 // per, 2)
+    ex.tick(3)
+    ex.tick(4)
     for k in (8, 9):
         loads[k].wait()
     gather_early.finish(3)
     lane = lax.broadcasted_iota(jnp.int32, (1, 128), 1)
     even = even_lanes(slots)
-    pairs = d // 128
     at_once = 256
 
     def attention(p, slot):
@@ -558,12 +600,8 @@
         qkv[:, kc] = turn(dk.T, cos, sin, even).astype(bf16)
         qkv[:, vc] = dv.T.astype(bf16)
 
-    for part in range(2):
-        base = done[0]
-        assert base >= 5
-        ready = (10 if part == 0 else 13) // per
-        n_half = pairs // 2
-        n_serve = max(0, min(ready - base, n_half))
+    def half_of_heads(part, carry):
+        base = 5 + part * (n_half + 1)
 
         def body(i, carry):
             p = part * n_half + i
@@ -575,41 +613,50 @@
                 load_e(p + 1, 1 - slot).start()
 
             attention(p, slot)
-            if n_serve:
-
-                @pl.when(i < n_serve)
-                def _():
-                    ex.advance(base + i)
-
+            ex.tick(base + i, 5, 5 + 2 * n_half)
             return carry
 
         lax.fori_loop(0, n_half, body, 0)
-        done[0] += n_serve
-        if part == 0:
+
+        @pl.when(part == 0)
+        def _():
             load_h1.wait()
-        else:
+
+        @pl.when(part == 1)
+        def _():
             for t in load_w:
                 t.start()
-        order = (0, 1, 2) if part == 0 else (2, 0, 1)
-        rights = [cut(qkv, 2 * k + part) for k in order]
+
+        rights = [cut(qkv, 2 * k + part) for k in range(3)]
         wgrad_into(flat(h2), rows, rights, lambda k, _: 10 + 3 * part + k, 2)
-        for k, r in zip(order, rights):
+        for k, r in enumerate(rights):
             column_sums(r(), 2 * k + part, 0)
-        service((13 if part == 0 else 16) // per, 1)
+        ex.tick(base + n_half, 5 + n_half, 6 + 2 * n_half)
+        return carry
+
+    lax.fori_loop(0, 2, half_of_heads, 0)
     sums.start(0)
     tile = dmid.shape[1]
     tiles = slots // tile
-    load_d = lambda i, slot: pltpu.make_async_copy(dmid_hbm.at[pl.ds(i * tile, tile)], dmid.at[slot], dld.at[slot])
-    store_f = lambda i, slot: pltpu.make_async_copy(fg.at[slot], fg_hbm.at[pl.ds(i * tile, tile)], fst.at[slot])
+    row_tile = lambda i: pl.ds(pl.multiple_of(i * tile, tile), tile)
+    load_d = lambda i, slot: pltpu.make_async_copy(dmid_hbm.at[row_tile(i)], dmid.at[slot], dld.at[slot])
+    store_f = lambda i, slot: pltpu.make_async_copy(fg.at[slot], fg_hbm.at[row_tile(i)], fst.at[slot])
     load_d(0, 0).start()
     load_x.wait()
     for t in load_w:
         t.wait()
-    for i in range(tiles):
+    dmoda_ref[...] = jnp.zeros_like(dmoda_ref)
+    t0 = 7 + 2 * n_half
+
+    def front(i, carry):
         slot = i % 2
-        if i + 1 < tiles:
+
+        @pl.when(i + 1 < tiles)
+        def _():
             load_d(i + 1, 1 - slot).start()
-        rws = pl.ds(i * tile, tile)
+
+        ex.tick(t0 + 2 * i, t0, t0 + 2 * tiles - 2)
+        rws = row_tile(i)
         dh = (
             mm(qkv[rws, :d], ebuf[0, 0], NT) + mm(qkv[rws, d : 2 * d], ebuf[0, 1], NT) + mm(qkv[rws, 2 * d :], ebuf[1, 0], NT)
         )
@@ -617,44 +664,53 @@
         cen = x - jnp.mean(x, axis=1, keepdims=True)
         r = lax.rsqrt(jnp.mean(cen * cen, axis=1, keepdims=True) + EPS)
         n1 = cen * r
-        psc = jnp.sum(dh * n1, axis=0, keepdims=True)
-        psh = jnp.sum(dh, axis=0, keepdims=True)
-        if i == 0:
-            dmoda_ref[:, :d] = psh
-            dmoda_ref[:, d:] = psc
-        else:
-            dmoda_ref[:, :d] += psh
-            dmoda_ref[:, d:] += psc
+        dmoda_ref[:, :d] += jnp.sum(dh, axis=0, keepdims=True)
+        dmoda_ref[:, d:] += jnp.sum(dh * n1, axis=0, keepdims=True)
         dn = dh * (1.0 + mod_ref[:, d : 2 * d])
         load_d(i, slot).wait()
-        if i >= 2:
+
+        @pl.when(i >= 2)
+        def _():
             store_f(i - 2, slot).wait()
+
         fg[slot] = dmid[slot] + r * (
             dn - jnp.mean(dn, axis=1, keepdims=True) - n1 * jnp.mean(dn * n1, axis=1, keepdims=True)
         )
         store_f(i, slot).start()
-        if i < 3:
-            sums.finish(i)
-            sums.start(i + 1)
-        service(n_chunks + 5, 1)
+        for phase in range(3):
+
+            @pl.when(i == phase)
+            def _():
+                sums.finish(phase)
+                sums.start(phase + 1)
+
+        ex.tick(t0 + 2 * i + 1, t0 + 1, t0 + 2 * tiles - 1)
+        return carry
+
+    lax.fori_loop(0, tiles, front, 0)
     for k in range(2 * d // 128):
         ltmp[k : k + 1, :] = dmoda_ref[:, k * 128 : (k + 1) * 128]
     late[ex.z, ex.y, ex.x, ex.c] = ltmp[...].astype(bf16)
     gather_late.start(0)
     sums.finish(3)
+    t = t0 + 2 * tiles
     for phase in range(4):
-        service(n_chunks + 5, 1)
+        if t <= ex.last:
+            ex.tick(t)
+            t += 1
         gather_late.finish(phase)
         if phase < 3:
             gather_late.start(phase + 1)
     bias_out[...] = mine[4]
     for i in range(max(0, tiles - 2), tiles):
         store_f(i, i % 2).wait()
-    service(n_chunks + 5, n_chunks + 5)
+    while t <= ex.last:
+        ex.tick(t)
+        t += 1
     dst = [dwo.at[part, :, k * STRIP : (k + 1) * STRIP] for k in range(2) for part in range(2)]
     dst += [uwo.at[:, k * STRIP : (k + 1) * STRIP] for k in range(4)]
     dst += [owo.at[:, k * STRIP : (k + 1) * STRIP] for k in range(2)]
-    dst += [qwo.at[:, k * STRIP : (k + 1) * STRIP] for k in (0, 2, 4, 5, 1, 3)]
+    dst += [qwo.at[:, k * STRIP : (k + 1) * STRIP] for k in (0, 2, 4, 1, 3, 5)]
     stores = []
     for strip, a in enumerate(dst):
         off = (strip % per) * STRIP
@@ -746,10 +802,9 @@
     def body(frames, te, lengths, mod_w, mod_b, qkv_w, qkv_b, out_w, out_b, up_w, up_b, down_w, down_b, cot):
         x, ct = frames[0], cot[0]
         slots, d = x.shape
-        cos, sin = rot_tables(slots, d // HEADS)
         row = lambda b: b.reshape(1, -1)
         mod = modulation(te, mod_w, row(mod_b))
-        h1, qkv = project_qkv(x, mod, qkv_w, row(qkv_b), cos, sin)
+        h1, qkv, cos, sin = project_qkv(x, mod, qkv_w, row(qkv_b), rot_tables(slots, d // HEADS))
         mixed, e, linv = attend(lengths, qkv)
         out, h2, act, dbr, dup, dat, dmix, dmid, dmod_b = middle_part(
             lengths, mixed, x, ct, mod, linv, out_w, row(out_b), up_w, row(up_b), down_w, row(down_b)

time: 257 us -> 242 us (0.942); the launches traced: 252 us -> 241 us
  Pallas kernels: 230 us -> 220 us
    pallas_call x1, Pallas kernels: 134 us -> 124 us  [backward(): pl.pallas_call(lambda *a: back_kernel(groups, batch, per, n_chunks, *a),...]
where the time goes in v3:
time: 242 us; the launch traced here: 241 us
  Pallas kernels  220 us (91%)
  local copies, waits for them, and re-layouts  17.9 us (7%)
    pallas_call x1, Pallas kernels, backward(): pl.pallas_call(lambda *a: back_kernel(groups, batch, per, n_chunks, *a),...  124 us
    pallas_call x1, Pallas kernels, middle_part(): pl.pallas_call(middle_kernel, grid_spec=pltpu.PrefetchScalarGridSpec(num_...  38.8 us
    pallas_call x1, Pallas kernels, attend(): pl.pallas_call(lambda *a: attend_kernel(*a, rows_at_once=rows_at_once), g...  27.7 us
    pallas_call x1, Pallas kernels, project_qkv(): pl.pallas_call(qkv_kernel, grid=(slots // tile,), in_specs=[row(d), full(...  12.7 us
    unnamed x28, local copies, waits for them, and re-layouts  10.4 us
    pallas_call x1, Pallas kernels, mods(): pl.pallas_call(mods_kernel, grid=(wide // d,), in_specs=[full((n, rows)),...  9.16 us
    pallas_call x1, Pallas kernels, modulation(): pl.pallas_call(mod_kernel, grid=(n // blk,), in_specs=[full((1, d)), pl.B...  7.56 us

profile of v3, /device:TPU:0, one launch (start us, length us, event | category | flops | bytes accessed | tf_op | source)
XLA Modules:
  0.0 241.5 jit_solution(9592115212597340559)
XLA Ops:
  1.3 1.3 reshape.82.b_ref
  2.6 7.6 %modulation.1.mod_ref.a_15_ = f32[1,6144]{1,0:T(1,128)} custom-call(bf16[1,1024]{1,0:T(2,128)(2,1)} %te_ref.3, bf16[1024,6144]{1,0:T(8,128)(2,1)} %w_ref.5, bf16[1,6144]{1,0:T(2,128)(2,1)} %reshape.82.b_ref), custom_call_target="tpu_custom_call" | custom-call | tf_op jit(solution)/shard_map/modulation/pallas_call | solution.py:65
  10.2 0.0 copy-done.6
  10.2 0.6 reshape.83.b_ref
  10.8 12.7 %project_qkv.1 = (bf16[1024,1024]{1,0:T(8,128)(2,1)}, bf16[1024,3072]{1,0:T(8,128)(2,1)}, f32[1024,128]{1,0:T(8,128)}, f32[1024,128]{1,0:T(8,128)}) custom-call(bf16[1024,1024]{1,0:T(8,128)(2,1)} %bitcast.15, f32[1,6144]{1,0:T(1,128)} %modulation.1.mod_ref.a_15_, bf16[1024,3072]{1,0:T(8,128)(2,1)} %a_10_.1, bf16[1,3072]{1,0:T(2,128)(2,1)} %reshape.83.b_ref, ...), custom_call_target="tpu_custom_call" | custom-call | tf_op jit(solution)/shard_map/project_qkv/pallas_call | solution.py:106
  23.5 0.0 copy-start.7
  23.5 0.0 copy-start.9
  23.5 27.7 %attend.1 = (bf16[1024,1024]{1,0:T(8,128)(2,1)}, bf16[16,1024,1024]{2,1,0:T(8,128)(2,1)}, f32[1024,1024]{1,0:T(8,128)}) custom-call(s32[1]{0:T(128)S(6)} %copy.41.a_0_.len_ref, bf16[1024,3072]{1,0:T(8,128)(2,1)} %get-tuple-element.41.a_1_.a_2_.a_3_.a_7_, bf16[1024,3072]{1,0:T(8,128)(2,1)} %get-tuple-element.41.a_1_.a_2_.a_3_.a_7_, ...), custom_call_target="tpu_custom_call" | custom-call | tf_op jit(solution)/shard_map/attend/pallas_call | solution.py:148
  51.2 0.0 copy-done.8
  51.2 0.6 reshape.84.ob_ref
  51.8 0.6 reshape.85.ub_ref
  52.4 0.6 reshape.86.db_ref
  53.0 38.8 %middle_part.1 = (bf16[1024,1024]{1,0:T(8,128)(2,1)}, bf16[1024,1024]{1,0:T(8,128)(2,1)}, bf16[1024,2048]{1,0:T(8,128)(2,1)}, bf16[1024,1024]{1,0:T(8,128)(2,1)}...) custom-call(s32[1]{0:T(128)S(6)} %copy.41.a_0_.len_ref, ...), custom_call_target="tpu_custom_call" | custom-call | tf_op jit(solution)/shard_map/middle_part/pallas_call | solution.py:228
  91.8 0.0 copy-start.4
  91.8 124.1 %backward.1 = (f32[2,64,1024]{2,1,0:T(8,128)}, f32[64,2048]{1,0:T(8,128)}, f32[64,1024]{1,0:T(8,128)}, f32[64,3072]{1,0:T(8,128)}, f32[16,512]{1,0:T(8,128)}, /*...) custom-call(bf16[1024,2048]{1,0:T(8,128)(2,1)} %get-tuple-element.45, ...), custom_call_target="tpu_custom_call" | custom-call | tf_op jit(solution)/shard_map/backward/pallas_call | solution.py:740
  215.9 1.3 copy.31
  217.3 0.7 constant_dynamic-slice_fusion.em_ref
  218.0 0.9 copy.35
  218.9 0.8 pad_maximum_fusion.dm_ref
  219.7 0.0 copy-done.4
  219.7 0.7 convert.6
  220.4 0.6 pad_maximum_fusion.1.own_ref
  221.1 9.2 %mods.1 = (f32[64,6144]{1,0:T(8,128)}, f32[1,6144]{1,0:T(1,128)}, f32[1,1024]{1,0:T(1,128)}) custom-call(bf16[32,64]{1,0:T(8,128)(2,1)} %constant_dynamic-slice_fusion.em_ref, bf16[32,6144]{1,0:T(8,128)(2,1)} %pad_maximum_fusion.dm_ref, bf16[1,6144]{1,0:T(2,128)(2,1)} %pad_maximum_fusion.1.own_ref, bf16[1024,6144]{1,0:T(8,128)(2,1)} %w_ref.5, ...), custom_call_target="tpu_custom_call" | custom-call | tf_op jit(solution)/shard_map/mods/pallas_call | solution.py:788
  230.2 1.3 dynamic-slice_reduce_fusion
  231.5 0.6 dynamic_slice.23
  232.2 0.6 fusion
  232.7 0.6 dynamic_slice.25
  233.3 4.9 %copy.42 = f32[1,1024,1024]{2,1,0:T(8,128)} copy(f32[1,1024,1024]{2,1,0:T(8,128)} %bitcast.18) | data formatting | bytes 8388608
  238.3 0.9 copy.43
  239.2 0.7 copy.44
  239.9 0.8 copy.45
  240.7 0.8 copy.46
  (17 shorter events, 0.1 us)
Async XLA Ops:
  2.6 7.6 %copy-start.6 = (bf16[3072]{0:T(1024)(128)(2,1)S(1)}, bf16[3072]{0:T(1024)(128)(2,1)}, u32[]{:S(2)}) copy-start(bf16[3072]{0:T(1024)(128)(2,1)} %param.24) | copy-start | bytes 18436
  23.5 27.8 %copy-start.8 = (bf16[1024]{0:T(1024)(128)(2,1)S(1)}, bf16[1024]{0:T(1024)(128)(2,1)}, u32[]{:S(2)}) copy-start(bf16[1024]{0:T(1024)(128)(2,1)} %param.26) | copy-start | bytes 6148
  23.5 28.3 %copy-start.7 = (bf16[2048]{0:T(1024)(128)(2,1)S(1)}, bf16[2048]{0:T(1024)(128)(2,1)}, u32[]{:S(2)}) copy-start(bf16[2048]{0:T(1024)(128)(2,1)} %param.28) | copy-start | bytes 12292
  23.5 28.9 %copy-start.9 = (bf16[1024]{0:T(1024)(128)(2,1)S(1)}, bf16[1024]{0:T(1024)(128)(2,1)}, u32[]{:S(2)}) copy-start(bf16[1024]{0:T(1024)(128)(2,1)} %param.30) | copy-start | bytes 6148
  91.8 127.9 %copy-start.4 = (f32[1,4096]{1,0:T(1,128)S(1)}, f32[1,4096]{1,0:T(1,128)}, u32[]{:S(2)}) copy-start(f32[1,4096]{1,0:T(1,128)} %get-tuple-element.56.a_16_) | copy-start | bytes 49156
  221.1 10.4 %copy-start.5 = (f32[16,512]{1,0:T(8,128)S(1)}, f32[16,512]{1,0:T(8,128)}, u32[]{:S(2)}) copy-start(f32[16,512]{1,0:T(8,128)} %get-tuple-element.65) | copy-start | bytes 98308
  233.3 4.9 %copy-start = (f32[64,3072]{1,0:T(8,128)S(1)}, f32[64,3072]{1,0:T(8,128)}, u32[]{:S(2)}) copy-start(f32[64,3072]{1,0:T(8,128)} %get-tuple-element.89) | copy-start | bytes 2359300
  233.3 5.8 %copy-start.3 = (f32[64,1024]{1,0:T(8,128)S(1)}, f32[64,1024]{1,0:T(8,128)}, u32[]{:S(2)}) copy-start(f32[64,1024]{1,0:T(8,128)} %get-tuple-element.91) | copy-start | bytes 786436
  233.3 6.5 %copy-start.2 = (f32[64,2048]{1,0:T(8,128)S(1)}, f32[64,2048]{1,0:T(8,128)}, u32[]{:S(2)}) copy-start(f32[64,2048]{1,0:T(8,128)} %get-tuple-element.93) | copy-start | bytes 1572868
  233.3 7.3 %copy-start.1 = (f32[2,64,1024]{2,1,0:T(8,128)S(1)}, f32[2,64,1024]{2,1,0:T(8,128)}, u32[]{:S(2)}) copy-start(f32[2,64,1024]{2,1,0:T(8,128)} %get-tuple-element.68) | copy-start | bytes 1572868

commit v4 on v3

--- a/solution.py
+++ b/solution.py
@@ -460,19 +460,19 @@
 
 
 def back_kernel(groups, batch, per, n_chunks, *refs):
-    (act_hbm, dbr_hbm, h2_hbm, dup_hbm, mixed_hbm, dat_hbm, dmix_hbm, qkv_hbm, e_hbm, h1_hbm, w_hbm, x_hbm, dmid_hbm,
+    (act_hbm, dbr_hbm, h2_hbm, dup_hbm, mixed_hbm, dat_hbm, dmix_hbm, qkv_hbm, e_hbm, h1_hbm, w_hbm, x_hbm, dmid_hbm, mw_hbm,
      cos_ref, sin_ref, mod_ref, dmodb_ref, te_ref,
-     dwo, uwo, owo, qwo, bias_out, early_out, late_out, fg_hbm, dmoda_ref,
+     dwo, uwo, owo, qwo, bias_out, early_out, late_out, fg_hbm, tg_ref,
      own, r0, r1, r2, r3, out, total, mine, early, late, etmp, ltmp,
-     ebuf, dsb, qkv, mixed, dmix, dbr, h2, dat, dmid, fg,
-     send, recv, ssum, rsum, sear, rear, slat, rlat, ld, eld, dld, fst, ost) = refs
+     ebuf, dsb, qkv, mixed, dmix, dbr, h2, dat, dmid, fg, dmoda_ref,
+     send, recv, ssum, rsum, sear, rear, slat, rlat, ld, eld, dld, fst, ost, mld) = refs
     slots, d = mixed.shape
     H, rows = groups // 4, d // groups
     chunk = lambda strip: strip // per
     n_own = own.shape[0]
     pairs = d // 128
-    n_half = pairs // 2
-    ready = [4, 6, 8, 10, 10] + [10] * n_half + [13] * (1 + n_half) + [16]
+    first, second = pairs // 2, pairs - 1
+    ready = [4, 6, 8, 10, 10] + [10] * first + [13] * (second - first + 1) + [15] * (1 + pairs - second) + [16]
     ex = Exchange(groups, batch, lambda j: own.at[j % n_own], dict(r0=r0, r1=r1, r2=r2, r3=r3, out=out), (send, recv),
                   [n // per for n in ready], n_chunks)
     sums = Small(ex, (ssum, rsum), total=total, mine=mine)
@@ -489,6 +489,8 @@
     load_h1 = load(10, h1_hbm, h2)
     load_w = [load(11 + k, half(w_hbm, k), ebuf.at[k // 2, k % 2]) for k in range(3)]
     load_x = load(14, x_hbm, dat)
+    free = [mixed, dmix, dbr, dsb.at[0], dsb.at[1], ebuf.at[1, 1]]
+    load_m = [pltpu.make_async_copy(half(mw_hbm, k), free[k], mld.at[k]) for k in range(6)]
     load_e = lambda p, slot: pltpu.make_async_copy(e_hbm.at[pl.ds(2 * p, 2)], ebuf.at[slot], eld.at[slot])
     for t in loads[:3]:
         t.start()
@@ -587,7 +589,7 @@
                 t = dmix[rws, qc]
                 t = jnp.where(own_lanes, t, jnp.zeros_like(t))
                 inner = jnp.sum(t.astype(f32) * mixed[rws, qc].astype(f32), axis=1, keepdims=True)
-                ds = (ebuf[slot, h, rws, :].astype(f32) * (mm(t, v, NT) - inner)).astype(bf16)
+                ds = ebuf[slot, h, rws, :] * (mm(t, v, NT) - inner).astype(bf16)
                 dsb[h, rws, :] = ds
                 parts.append(mm(ds, k, NN))
             dqs.append(jnp.concatenate(parts, axis=0))
@@ -600,41 +602,65 @@
         qkv[:, kc] = turn(dk.T, cos, sin, even).astype(bf16)
         qkv[:, vc] = dv.T.astype(bf16)
 
-    def half_of_heads(part, carry):
-        base = 5 + part * (n_half + 1)
+    def qkv_grad(rights, places):
+        zs = 2
 
         def body(i, carry):
-            p = part * n_half + i
-            slot = p % 2
-            load_e(p, slot).wait()
-
-            @pl.when(p + 1 < pairs)
-            def _():
-                load_e(p + 1, 1 - slot).start()
-
-            attention(p, slot)
-            ex.tick(base + i, 5, 5 + 2 * n_half)
+            n = zs * 4 * rows
+            lt = h2[:, pl.ds(pl.multiple_of(i * n, 128), n)].T
+            for right, where in zip(rights, places):
+                r = mm(lt, right(), NN).astype(bf16)
+                for c, (strip, at) in enumerate(where):
+                    lo = (strip % per) * STRIP + at * 128
+                    for b in range(4 * zs):
+                        own[chunk(strip) % n_own, i * zs + b // 4, (b // 2) % 2, b % 2, :, lo : lo + 128] = (
+                            r[b * rows : (b + 1) * rows, c * 128 : (c + 1) * 128]
+                        )
             return carry
 
-        lax.fori_loop(0, n_half, body, 0)
-
-        @pl.when(part == 0)
+        lax.fori_loop(0, H // zs, body, 0)
+
+    span = lambda k, lo, hi: lambda: qkv[:, k * d + lo * 128 : k * d + hi * 128]
+    late_cols = [(k, p) for k in range(3) for p in range(first, second)] + [(k, p) for k in range(3) for p in range(second, pairs)]
+    late_place = {kp: (13 + n // 4, n % 4) for n, kp in enumerate(late_cols)}
+    t1 = 5 + first
+
+    def heads(p, carry):
+        slot = p % 2
+        load_e(p, slot).wait()
+
+        @pl.when(p + 1 < pairs)
+        def _():
+            load_e(p + 1, 1 - slot).start()
+
+        attention(p, slot)
+        ex.tick(5 + p + jnp.where(p >= first, 1, 0) + jnp.where(p >= second, 1, 0), 5, 6 + pairs)
+
+        @pl.when(p == first - 1)
         def _():
             load_h1.wait()
-
-        @pl.when(part == 1)
+            qkv_grad([cut(qkv, 2 * k) for k in range(3)], [[(10 + k, c) for c in range(4)] for k in range(3)])
+            for k in range(3):
+                column_sums(cut(qkv, 2 * k)(), 2 * k, 0)
+            ex.tick(t1)
+
+        @pl.when(p == second - 1)
         def _():
-            for t in load_w:
-                t.start()
-
-        rights = [cut(qkv, 2 * k + part) for k in range(3)]
-        wgrad_into(flat(h2), rows, rights, lambda k, _: 10 + 3 * part + k, 2)
-        for k, r in enumerate(rights):
-            column_sums(r(), 2 * k + part, 0)
-        ex.tick(base + n_half, 5 + n_half, 6 + 2 * n_half)
+            qkv_grad([span(k, first, second) for k in range(3)],
+                     [[late_place[k, q] for q in range(first, second)] for k in range(3)])
+            ex.tick(1 + 5 + second)
+
         return carry
 
-    lax.fori_loop(0, 2, half_of_heads, 0)
+    lax.fori_loop(0, pairs, heads, 0)
+    for t in load_w:
+        t.start()
+    qkv_grad([lambda: jnp.concatenate([span(k, second, pairs)() for k in range(3)], axis=1)],
+             [[late_place[k, q] for k in range(3) for q in range(second, pairs)]])
+    t0 = 8 + pairs
+    ex.tick(t0 - 1)
+    for k in range(3):
+        column_sums(cut(qkv, 2 * k + 1)(), 2 * k + 1, 0)
     sums.start(0)
     tile = dmid.shape[1]
     tiles = slots // tile
@@ -645,9 +671,9 @@
     load_x.wait()
     for t in load_w:
         t.wait()
+    for t in load_m:
+        t.start()
     dmoda_ref[...] = jnp.zeros_like(dmoda_ref)
-    t0 = 7 + 2 * n_half
-
     def front(i, carry):
         slot = i % 2
 
@@ -655,11 +681,11 @@
         def _():
             load_d(i + 1, 1 - slot).start()
 
-        ex.tick(t0 + 2 * i, t0, t0 + 2 * tiles - 2)
         rws = row_tile(i)
         dh = (
             mm(qkv[rws, :d], ebuf[0, 0], NT) + mm(qkv[rws, d : 2 * d], ebuf[0, 1], NT) + mm(qkv[rws, 2 * d :], ebuf[1, 0], NT)
         )
+        ex.tick(t0 + 2 * i, t0, t0 + 2 * tiles - 2)
         x = dat[rws, :].astype(f32)
         cen = x - jnp.mean(x, axis=1, keepdims=True)
         r = lax.rsqrt(jnp.mean(cen * cen, axis=1, keepdims=True) + EPS)
@@ -693,37 +719,62 @@
     late[ex.z, ex.y, ex.x, ex.c] = ltmp[...].astype(bf16)
     gather_late.start(0)
     sums.finish(3)
+
+    def through_mod(k):
+        load_m[k].wait()
+        v = dmoda_ref[:, k * d : (k + 1) * d] if k < 2 else dmodb_ref[:, (k - 2) * d : (k - 1) * d]
+        v = jnp.broadcast_to(v, (8, d)).astype(bf16)
+        tg_ref[...] += mm(v, free[k][...], NT)[:1]
+
+    pieces = [(2 * k + part, 0, dwo.at[part, :, k * STRIP : (k + 1) * STRIP]) for k in range(2) for part in range(2)]
+    pieces += [(4 + k, 0, uwo.at[:, k * STRIP : (k + 1) * STRIP]) for k in range(4)]
+    pieces += [(8 + k, 0, owo.at[:, k * STRIP : (k + 1) * STRIP]) for k in range(2)]
+    pieces += [(10 + k, 0, qwo.at[:, k * d : k * d + STRIP]) for k in range(3)]
+    for (k, p), (strip, at) in late_place.items():
+        pieces.append((strip, at * 128, qwo.at[:, k * d + p * 128 : k * d + (p + 1) * 128]))
+    stores = [pltpu.make_async_copy(early, early_out, ost.at[0])]
+    for n, (strip, off, dst) in enumerate(pieces):
+        off += (strip % per) * STRIP
+        stores.append(pltpu.make_async_copy(out.at[chunk(strip), :, off : off + dst.shape[1]], dst, ost.at[n + 1]))
+
+    def start_stores():
+        for c in stores:
+            c.start()
+
+    tg_ref[...] = jnp.zeros_like(tg_ref)
     t = t0 + 2 * tiles
+    stored = t > ex.last
+    if stored:
+        start_stores()
     for phase in range(4):
+        through_mod(phase)
         if t <= ex.last:
             ex.tick(t)
             t += 1
         gather_late.finish(phase)
         if phase < 3:
             gather_late.start(phase + 1)
-    bias_out[...] = mine[4]
+    through_mod(4)
+    through_mod(5)
+    for k in range(mine.shape[1]):
+        for c in range(STRIP // 128):
+            at = k * (STRIP // 128) + c
+            bias_out[at : at + 1, :] = mine[4, k : k + 1, c * 128 : (c + 1) * 128]
     for i in range(max(0, tiles - 2), tiles):
         store_f(i, i % 2).wait()
     while t <= ex.last:
         ex.tick(t)
         t += 1
-    dst = [dwo.at[part, :, k * STRIP : (k + 1) * STRIP] for k in range(2) for part in range(2)]
-    dst += [uwo.at[:, k * STRIP : (k + 1) * STRIP] for k in range(4)]
-    dst += [owo.at[:, k * STRIP : (k + 1) * STRIP] for k in range(2)]
-    dst += [qwo.at[:, k * STRIP : (k + 1) * STRIP] for k in (0, 2, 4, 1, 3, 5)]
-    stores = []
-    for strip, a in enumerate(dst):
-        off = (strip % per) * STRIP
-        stores.append(pltpu.make_async_copy(out.at[chunk(strip), :, off : off + STRIP], a, ost.at[strip]))
-    stores.append(pltpu.make_async_copy(early, early_out, ost.at[16]))
-    stores.append(pltpu.make_async_copy(late, late_out, ost.at[17]))
-    for t in stores:
-        t.start()
-    for t in stores:
-        t.wait()
-
-
-def backward(groups, batch, act, dbr, h2, dup, mixed, dat, dmix, qkv, e, h1, w, x, dmid, cos, sin, mod, dmodb, te):
+    if not stored:
+        start_stores()
+    late_store = pltpu.make_async_copy(late, late_out, ost.at[len(stores)])
+    late_store.start()
+    for c in stores:
+        c.wait()
+    late_store.wait()
+
+
+def backward(groups, batch, act, dbr, h2, dup, mixed, dat, dmix, qkv, e, h1, w, x, dmid, mw, cos, sin, mod, dmodb, te):
     slots, d = mixed.shape
     H, rows = groups // 4, d // groups
     per = max(1, 128 * batch // STRIP)
@@ -739,61 +790,73 @@
     seen = (H, 2, 2, batch)
     return pl.pallas_call(
         lambda *a: back_kernel(groups, batch, per, n_chunks, *a),
-        in_specs=[hbm] * 13 + [vm] * 5,
+        in_specs=[hbm] * 14 + [vm] * 5,
         out_specs=[hbm] * 4 + [vm, hbm, hbm, hbm, vm],
         out_shape=[S((2, rows, d), f32), S((rows, 2 * d), f32), S((rows, d), f32), S((rows, 3 * d), f32),
-                   S((16, STRIP), f32), S(seen + (16, STRIP), bf16), S(seen + (16, 128), bf16),
-                   S((slots, d), f32), S((1, 2 * d), f32)],
+                   S((16 * STRIP // 128, 128), f32), S(seen + (16, STRIP), bf16), S(seen + (16, 128), bf16),
+                   S((slots, d), f32), S((1, d), f32)],
         scratch_shapes=[V((-(-10 // per), H, 2, 2, rows, per * STRIP), bf16),
                         sc["r0"], sc["r1"], sc["r2"], sc["r3"], sc["out"],
                         V((nsm, 16, STRIP), f32), V((5, 16, STRIP), f32), V(seen + (16, STRIP), bf16), V(seen + (16, 128), bf16),
                         V((16, STRIP), f32), V((16, 128), f32),
                         V((2, 2, slots, slots), bf16), V((2, slots, slots), bf16), V((slots, 3 * d), bf16), V((slots, d), bf16),
                         V((slots, d), bf16), V((slots, d), bf16), V((slots, d), bf16), V((slots, d), bf16),
-                        V((2, tile, d), f32), V((2, tile, d), f32),
+                        V((2, tile, d), f32), V((2, tile, d), f32), V((1, 2 * d), f32),
                         dma((n_chunks, ns)), dma((n_chunks, ns)), dma((nsm,)), dma((nsm,)), dma((nsm,)), dma((nsm,)),
-                        dma((nsm,)), dma((nsm,)), dma((15,)), dma((2,)), dma((2,)), dma((2,)), dma((18,))],
+                        dma((nsm,)), dma((nsm,)), dma((15,)), dma((2,)), dma((2,)), dma((2,)), dma((27,)), dma((6,))],
         compiler_params=pltpu.CompilerParams(vmem_limit_bytes=67_000_000, collective_id=0, has_side_effects=True),
         name="backward",
-    )(act, dbr, h2, dup, mixed, dat, dmix, qkv, e, h1, w, x, dmid, cos, sin, mod, dmodb, te)
-
-
-def mods_kernel(em_ref, dm_ref, own_ref, w_ref, te_ref, wg_ref, bg_ref, tg_ref):
-    i = pl.program_id(0)
-    dm = dm_ref[...]
-    wg_ref[...] = mm(em_ref[...], dm, TN)
-    bg_ref[...] = jnp.sum(dm.astype(f32), axis=0, keepdims=True)
-    part = mm(jnp.broadcast_to(own_ref[...], (8, own_ref.shape[1])), w_ref[...], NT)[:1]
-
-    @pl.when(i == 0)
-    def _():
-        tg_ref[...] = part
-
-    @pl.when(i > 0)
-    def _():
-        tg_ref[...] += part
-
-    @pl.when(i == pl.num_programs(0) - 1)
-    def _():
-        t = te_ref[...].astype(f32)
-        s = jax.nn.sigmoid(t)
-        tg_ref[...] = tg_ref[...] * (s * (1.0 + t * (1.0 - s)))
-
-
-def mods(em, dm, own, w, te):
-    n, rows = em.shape
-    d, wide = w.shape
-    col = lambda r: pl.BlockSpec((r, d), lambda i: (0, i))
+    )(act, dbr, h2, dup, mixed, dat, dmix, qkv, e, h1, w, x, dmid, mw, cos, sin, mod, dmodb, te)
+
+
+def finish_kernel(early_ref, late_ref, bias_ref, tg_ref, te_ref, wg_ref, tout_ref, mb_ref, qb_ref, ob_ref, ub_ref, db_ref, flat):
+    rows, d = wg_ref.shape[0], wg_ref.shape[1] // 6
+    g = lax.axis_index("groups")
+    e, late = early_ref[...], late_ref[...]
+    n = e.shape[0] // 16
+    at, off = 4 * d // STRIP + (g * rows) // STRIP, (g * rows) % STRIP
+    pick = lax.broadcasted_iota(jnp.int32, (STRIP, 128), 0) - lax.broadcasted_iota(jnp.int32, (STRIP, 128), 1) == off
+    em = mm(e, jnp.where(pick, 1.0, 0.0).astype(bf16), NN).reshape(n, 16, 128)
+    em = jnp.where(lax.broadcasted_iota(jnp.int32, em.shape, 1) == at, em, 0.0)
+    em = jnp.broadcast_to(jnp.sum(em, axis=1, keepdims=True), em.shape).reshape(n * 16, 128).T[:rows]
+    row = lax.broadcasted_iota(jnp.int32, em.shape, 1) % 16
+    for r in range(16):
+        left = jnp.where(row == r, em, 0.0).astype(bf16)
+        wg_ref[:, r * 128 : (r + 1) * 128] = mm(left, late, NN)
+        if r < 4 * d // STRIP:
+            lo = 2 * d + r * STRIP
+            wg_ref[:, lo : lo + STRIP] = mm(left, e, NN)
+    flat[:16, :] = jnp.sum(late.astype(f32).reshape(n, 16, 128), axis=0)
+    es = jnp.sum(e.astype(f32).reshape(n, 16, STRIP), axis=0)
+    for r in range(4 * d // STRIP):
+        for c in range(STRIP // 128):
+            k = 16 + r * (STRIP // 128) + c
+            flat[k : k + 1, :] = es[r : r + 1, c * 128 : (c + 1) * 128]
+    flat[48:, :] = jnp.zeros((flat.shape[0] - 48, 128), f32)
+    lane = lax.broadcasted_iota(jnp.int32, (1, 128), 1)
+    for ref, src, first in ((mb_ref, flat, 0), (qb_ref, bias_ref, 0), (ob_ref, bias_ref, 3 * d), (ub_ref, bias_ref, 4 * d), (db_ref, bias_ref, 6 * d)):
+        width = ref.shape[1]
+        at, off = first // 128 + (g * width) // 128, (g * width) % 128
+        for k in range(-(-width // 128)):
+            turned = [pltpu.roll(src[pl.ds(at + k + i, 1), :], (128 - off) % 128, 1) for i in range(2)]
+            v = jnp.where(lane < 128 - off, turned[0], turned[1])
+            w = min(128, width - k * 128)
+            ref[:, k * 128 : k * 128 + w] = v[:, :w]
+    t = te_ref[...].astype(f32)
+    s = jax.nn.sigmoid(t)
+    tout_ref[...] = tg_ref[...] * (s * (1.0 + t * (1.0 - s)))
+
+
+def finish(early, late, bias, tg, te, rows):
+    d = te.shape[1]
     S = jax.ShapeDtypeStruct
     return pl.pallas_call(
-        mods_kernel,
-        grid=(wide // d,),
-        in_specs=[full((n, rows)), col(n), col(1), col(d), full((1, d))],
-        out_specs=[col(rows), col(1), pl.BlockSpec((1, d), lambda i: (0, 0))],
-        out_shape=[S((rows, wide), f32), S((1, wide), f32), S((1, d), f32)],
+        finish_kernel,
+        out_shape=[S((rows, 6 * d), f32), S((1, d), f32)] + [S((1, k * rows), f32) for k in (6, 3, 1, 2, 1)],
+        scratch_shapes=[pltpu.VMEM((56, 128), f32)],
         compiler_params=params(),
-        name="mods",
-    )(em, dm, own, w, te)
+        name="finish",
+    )(early, late, bias, tg, te)
 
 
 def solution(mesh):
@@ -809,20 +872,12 @@
         out, h2, act, dbr, dup, dat, dmix, dmid, dmod_b = middle_part(
             lengths, mixed, x, ct, mod, linv, out_w, row(out_b), up_w, row(up_b), down_w, row(down_b)
         )
-        dws, uws, ows, qws, bs, early, late, fg, dmod_a = backward(
-            groups, batch, act, dbr, h2, dup, mixed, dat, dmix, qkv, e, h1, qkv_w, x, dmid, cos, sin, mod, dmod_b, te
+        dws, uws, ows, qws, bs, early, late, fg, tg = backward(
+            groups, batch, act, dbr, h2, dup, mixed, dat, dmix, qkv, e, h1, qkv_w, x, dmid, mod_w, cos, sin, mod, dmod_b, te
         )
         rows, n = d // groups, groups * batch
-        early, late = early.reshape(n, 16 * STRIP), late.reshape(n, 2 * d)
-        g = lax.axis_index("groups")
-        em = lax.dynamic_slice_in_dim(early, 4 * d + g * rows, rows, 1)
-        dm = jnp.concatenate([late, early[:, : 4 * d]], axis=1)
-        own = jnp.concatenate([dmod_a, dmod_b], axis=1).astype(bf16)
-        mod_wg, mod_bg, time_grad = mods(em, dm, own, mod_w, te)
-        bs = bs.reshape(16 * STRIP)
-        cut = lambda v, off, n: lax.dynamic_slice_in_dim(v, off + g * n, n)
-        return (out[None], fg[None], time_grad, mod_wg, cut(mod_bg[0], 0, 6 * rows), qws, cut(bs, 0, 3 * rows),
-                ows, cut(bs, 3 * d, rows), uws, cut(bs, 4 * d, 2 * rows), dws.reshape(2 * rows, d), cut(bs, 6 * d, rows))
+        mod_wg, time_grad, mb, qb, ob, ub, db = finish(early.reshape(n * 16, STRIP), late.reshape(n * 16, 128), bs, tg, te, rows)
+        return (out[None], fg[None], time_grad, mod_wg, mb[0], qws, qb[0], ows, ob[0], uws, ub[0], dws.reshape(2 * rows, d), db[0])
 
     split = P(("groups", "batch"))
     own = P("groups")

time: 242 us -> 228 us (0.942)
  Pallas kernels: 220 us -> 213 us
  local copies, waits for them, and re-layouts: 17.9 us -> 11.9 us
    pallas_call x1, Pallas kernels: 9.16 us -> 3.98 us  [finish(): pl.pallas_call(finish_kernel, out_shape=[S((rows, 6 * d), f32), S((1, d),...]
    dynamic_slice x5 -> x0, local copies, waits for them, and re-layouts: 3.76 us -> none  [the longest x4 3.08 us: body(): cut = lambda v, off, n: lax.dynamic_slice_in_dim(v, off + g * n, n)]
    unnamed x28 -> x21, local copies, waits for them, and re-layouts: 10.4 us -> 8.14 us
where the time goes in v4:
time: 228 us
  Pallas kernels  213 us (93%)
  local copies, waits for them, and re-layouts  11.9 us (5%)
    pallas_call x1, Pallas kernels, backward(): pl.pallas_call(lambda *a: back_kernel(groups, batch, per, n_chunks, *a),...  122 us
    pallas_call x1, Pallas kernels, middle_part(): pl.pallas_call(middle_kernel, grid_spec=pltpu.PrefetchScalarGridSpec(num_...  38.8 us
    pallas_call x1, Pallas kernels, attend(): pl.pallas_call(lambda *a: attend_kernel(*a, rows_at_once=rows_at_once), g...  27.7 us
    pallas_call x1, Pallas kernels, project_qkv(): pl.pallas_call(qkv_kernel, grid=(slots // tile,), in_specs=[row(d), full(...  12.7 us
    unnamed x21, local copies, waits for them, and re-layouts  8.14 us
    pallas_call x1, Pallas kernels, modulation(): pl.pallas_call(mod_kernel, grid=(n // blk,), in_specs=[full((1, d)), pl.B...  7.56 us

profile of v4, /device:TPU:0, one launch (start us, length us, event | category | flops | bytes accessed | tf_op | source)
XLA Modules:
  0.0 227.7 jit_solution(7089081585538705006)
XLA Ops:
  1.3 1.3 reshape.50.b_ref
  2.6 0.0 copy-start.4
  2.6 7.6 %modulation.1.mod_ref.a_16_ = f32[1,6144]{1,0:T(1,128)} custom-call(bf16[1,1024]{1,0:T(2,128)(2,1)} %te_ref.3, bf16[1024,6144]{1,0:T(8,128)(2,1)} %a_13_.1, bf16[1,6144]{1,0:T(2,128)(2,1)} %reshape.50.b_ref), custom_call_target="tpu_custom_call" | custom-call | tf_op jit(solution)/shard_map/modulation/pallas_call | solution.py:65
  10.2 0.0 copy-done.4
  10.2 0.6 reshape.51.b_ref
  10.8 12.7 %project_qkv.1 = (bf16[1024,1024]{1,0:T(8,128)(2,1)}, bf16[1024,3072]{1,0:T(8,128)(2,1)}, f32[1024,128]{1,0:T(8,128)}, f32[1024,128]{1,0:T(8,128)}) custom-call(bf16[1024,1024]{1,0:T(8,128)(2,1)} %bitcast.11, f32[1,6144]{1,0:T(1,128)} %modulation.1.mod_ref.a_16_, bf16[1024,3072]{1,0:T(8,128)(2,1)} %a_10_.1, bf16[1,3072]{1,0:T(2,128)(2,1)} %reshape.51.b_ref, ...), custom_call_target="tpu_custom_call" | custom-call | tf_op jit(solution)/shard_map/project_qkv/pallas_call | solution.py:106
  23.5 0.0 copy-start.6
  23.5 0.0 copy-start.5
  23.5 0.0 copy-start.7
  23.5 27.7 %attend.1 = (bf16[1024,1024]{1,0:T(8,128)(2,1)}, bf16[16,1024,1024]{2,1,0:T(8,128)(2,1)}, f32[1024,1024]{1,0:T(8,128)}) custom-call(s32[1]{0:T(128)S(6)} %copy.36.a_0_.len_ref, bf16[1024,3072]{1,0:T(8,128)(2,1)} %get-tuple-element.45.a_1_.a_2_.a_3_.a_7_, bf16[1024,3072]{1,0:T(8,128)(2,1)} %get-tuple-element.45.a_1_.a_2_.a_3_.a_7_, ...), custom_call_target="tpu_custom_call" | custom-call | tf_op jit(solution)/shard_map/attend/pallas_call | solution.py:148
  51.2 0.0 copy-done.6
  51.2 0.6 reshape.52.ob_ref
  51.8 0.0 copy-done.5
  51.8 0.6 reshape.53.ub_ref
  52.4 0.0 copy-done.7
  52.5 0.6 reshape.54.db_ref
  53.0 38.8 %middle_part.1 = (bf16[1024,1024]{1,0:T(8,128)(2,1)}, bf16[1024,1024]{1,0:T(8,128)(2,1)}, bf16[1024,2048]{1,0:T(8,128)(2,1)}, bf16[1024,1024]{1,0:T(8,128)(2,1)}...) custom-call(s32[1]{0:T(128)S(6)} %copy.36.a_0_.len_ref, ...), custom_call_target="tpu_custom_call" | custom-call | tf_op jit(solution)/shard_map/middle_part/pallas_call | solution.py:228
  91.9 122.5 %backward.1 = (f32[2,64,1024]{2,1,0:T(8,128)}, f32[64,2048]{1,0:T(8,128)}, f32[64,1024]{1,0:T(8,128)}, f32[64,3072]{1,0:T(8,128)}, f32[64,128]{1,0:T(8,128)}, /*...) custom-call(bf16[1024,2048]{1,0:T(8,128)(2,1)} %get-tuple-element.49, ...), custom_call_target="tpu_custom_call" | custom-call | tf_op jit(solution)/shard_map/backward/pallas_call | solution.py:791
  214.3 4.0 %finish.1 = (f32[64,6144]{1,0:T(8,128)}, f32[1,1024]{1,0:T(1,128)}, f32[1,384]{1,0:T(1,128)}, f32[1,192]{1,0:T(1,128)}, f32[1,64]{1,0:T(1,128)}, /*index=5*/f32[1,128]{1,0:T(1,128)}, f32[1,64]{1,0:T(1,128)}) custom-call(bf16[512,512]{1,0:T(8,128)(2,1)} %bitcast.17, bf16[512,128]{1,0:T(8,128)(2,1)} %bitcast.18, f32[64,128]{1,0:T(8,128)} %get-tuple-element.64.bias_ref, ...), custom_call_target="tpu_custom_call" | custom-call | tf_op jit(solution)/shard_map/finish/pallas_call | solution.py:853
  218.3 1.3 reduce
  219.6 0.0 copy-start
  219.6 0.0 copy-start.2
  219.6 0.0 copy-start.1
  219.6 4.9 %copy.37 = f32[1,1024,1024]{2,1,0:T(8,128)} copy(f32[1,1024,1024]{2,1,0:T(8,128)} %bitcast.14) | data formatting | bytes 8388608
  224.5 0.0 copy-done
  224.5 0.9 copy.38
  225.4 0.0 copy-done.3
  225.4 0.7 copy.39
  226.1 0.0 copy-done.2
  226.1 0.8 copy.40
  226.9 0.0 copy-done.1
  226.9 0.8 copy.41
  (1 shorter events, 0.0 us)
Async XLA Ops:
  2.6 7.6 %copy-start.4 = (bf16[3072]{0:T(1024)(128)(2,1)S(1)}, bf16[3072]{0:T(1024)(128)(2,1)}, u32[]{:S(2)}) copy-start(bf16[3072]{0:T(1024)(128)(2,1)} %param.24) | copy-start | bytes 18436
  23.5 27.7 %copy-start.6 = (bf16[1024]{0:T(1024)(128)(2,1)S(1)}, bf16[1024]{0:T(1024)(128)(2,1)}, u32[]{:S(2)}) copy-start(bf16[1024]{0:T(1024)(128)(2,1)} %param.26) | copy-start | bytes 6148
  23.5 28.3 %copy-start.5 = (bf16[2048]{0:T(1024)(128)(2,1)S(1)}, bf16[2048]{0:T(1024)(128)(2,1)}, u32[]{:S(2)}) copy-start(bf16[2048]{0:T(1024)(128)(2,1)} %param.28) | copy-start | bytes 12292
  23.5 28.9 %copy-start.7 = (bf16[1024]{0:T(1024)(128)(2,1)S(1)}, bf16[1024]{0:T(1024)(128)(2,1)}, u32[]{:S(2)}) copy-start(bf16[1024]{0:T(1024)(128)(2,1)} %param.30) | copy-start | bytes 6148
  219.6 4.9 %copy-start = (f32[64,3072]{1,0:T(8,128)S(1)}, f32[64,3072]{1,0:T(8,128)}, u32[]{:S(2)}) copy-start(f32[64,3072]{1,0:T(8,128)} %get-tuple-element.95) | copy-start | bytes 2359300
  219.6 5.8 %copy-start.3 = (f32[64,1024]{1,0:T(8,128)S(1)}, f32[64,1024]{1,0:T(8,128)}, u32[]{:S(2)}) copy-start(f32[64,1024]{1,0:T(8,128)} %get-tuple-element.97) | copy-start | bytes 786436
  219.6 6.5 %copy-start.2 = (f32[64,2048]{1,0:T(8,128)S(1)}, f32[64,2048]{1,0:T(8,128)}, u32[]{:S(2)}) copy-start(f32[64,2048]{1,0:T(8,128)} %get-tuple-element.99) | copy-start | bytes 1572868
  219.6 7.3 %copy-start.1 = (f32[2,64,1024]{2,1,0:T(8,128)S(1)}, f32[2,64,1024]{2,1,0:T(8,128)}, u32[]{:S(2)}) copy-start(f32[2,64,1024]{2,1,0:T(8,128)} %get-tuple-element.75) | copy-start | bytes 1572868

commit v5 on v4

--- a/solution.py
+++ b/solution.py
@@ -245,8 +245,8 @@
 
 MESH = pl.DeviceIdType.MESH
 STRIP = 512
-RINGS = dict(r0=4, r1=6, r2=6, r3=4)
-DELAYS = (0, 1, 3, 5, 7, 8)
+RINGS = dict(r0=4, r1=6, r2=7, r3=6)
+DELAYS = (0, 1, 3, 5, 8, 9)
 
 
 class Exchange:
@@ -487,13 +487,13 @@
         load(6, mixed_hbm, mixed), load(7, dat_hbm, dat), load(8, qkv_hbm, qkv), load(9, dmix_hbm, dmix),
     ]
     load_h1 = load(10, h1_hbm, h2)
-    load_w = [load(11 + k, half(w_hbm, k), ebuf.at[k // 2, k % 2]) for k in range(3)]
+    load_w = [load(11 + k, half(w_hbm, k), (ebuf.at[0, 0], ebuf.at[0, 1], dbr)[k]) for k in range(3)]
     load_x = load(14, x_hbm, dat)
-    free = [mixed, dmix, dbr, dsb.at[0], dsb.at[1], ebuf.at[1, 1]]
+    free = [mixed, dmix, ebuf.at[1, 0], dsb.at[0], dsb.at[1], ebuf.at[1, 1]]
     load_m = [pltpu.make_async_copy(half(mw_hbm, k), free[k], mld.at[k]) for k in range(6)]
     load_e = lambda p, slot: pltpu.make_async_copy(e_hbm.at[pl.ds(2 * p, 2)], ebuf.at[slot], eld.at[slot])
-    for t in loads[:3]:
-        t.start()
+    for k in (0, 2, 1):
+        loads[k].start()
 
     for k in range(4 * d // STRIP):
         etmp[k : k + 1, :] = dmodb_ref[:, k * STRIP : (k + 1) * STRIP]
@@ -512,11 +512,13 @@
     def column_sums(value, row, k):
         mine[0, pl.ds(row + k, 1), :] = jnp.sum(value.astype(f32), axis=0, keepdims=True)
 
-    def wgrad_into(left, block_rows, rights, place, zs):
+    def wgrad_into(left, block_rows, rights, place, zs, before=None):
         parts = block_rows // rows
 
         def body(i, _):
             n = zs * 4 * block_rows
+            if before is not None:
+                before(i, n)
             lt = left(i * n, n).T
             for k, right in enumerate(rights):
                 r = mm(lt, right(), NN).astype(bf16)
@@ -531,7 +533,7 @@
 
         lax.fori_loop(0, H // zs, body, 0)
 
-    for k in (0, 1, 2):
+    for k in (0, 2):
         loads[k].wait()
     for k in (3, 4, 5, 6, 7):
         loads[k].start()
@@ -539,7 +541,13 @@
     flat = lambda ref: lambda lo, n: ref[:, pl.ds(pl.multiple_of(lo, 128), n)]
     strip_at = lambda k: pl.ds(k * STRIP if isinstance(k, int) else pl.multiple_of(k * STRIP, STRIP), STRIP)
     cut = lambda ref, k: lambda: ref[:, strip_at(k)]
-    wgrad_into(wide(ebuf.at[1]), 2 * rows, [cut(dbr, k) for k in range(2)], lambda k, part: 2 * k + part, 2)
+
+    def second_half(i, n):
+        @pl.when(i * n == d)
+        def _():
+            loads[1].wait()
+
+    wgrad_into(wide(ebuf.at[1]), 2 * rows, [cut(dbr, k) for k in range(2)], lambda k, part: 2 * k + part, 2, second_half)
     for k in range(2):
         column_sums(cut(dbr, k)(), 12, k)
     gather_early.finish(0)
@@ -646,6 +654,8 @@
 
         @pl.when(p == second - 1)
         def _():
+            for c in load_w:
+                c.start()
             qkv_grad([span(k, first, second) for k in range(3)],
                      [[late_place[k, q] for q in range(first, second)] for k in range(3)])
             ex.tick(1 + 5 + second)
@@ -653,7 +663,8 @@
         return carry
 
     lax.fori_loop(0, pairs, heads, 0)
-    for t in load_w:
+    assert second % 2 == 1
+    for t in load_m:
         t.start()
     qkv_grad([lambda: jnp.concatenate([span(k, second, pairs)() for k in range(3)], axis=1)],
              [[late_place[k, q] for k in range(3) for q in range(second, pairs)]])
@@ -671,8 +682,6 @@
     load_x.wait()
     for t in load_w:
         t.wait()
-    for t in load_m:
-        t.start()
     dmoda_ref[...] = jnp.zeros_like(dmoda_ref)
     def front(i, carry):
         slot = i % 2
@@ -683,7 +692,7 @@
 
         rws = row_tile(i)
         dh = (
-            mm(qkv[rws, :d], ebuf[0, 0], NT) + mm(qkv[rws, d : 2 * d], ebuf[0, 1], NT) + mm(qkv[rws, 2 * d :], ebuf[1, 0], NT)
+            mm(qkv[rws, :d], ebuf[0, 0], NT) + mm(qkv[rws, d : 2 * d], ebuf[0, 1], NT) + mm(qkv[rws, 2 * d :], dbr[...], NT)
         )
         ex.tick(t0 + 2 * i, t0, t0 + 2 * tiles - 2)
         x = dat[rws, :].astype(f32)
@@ -751,6 +760,9 @@
         if t <= ex.last:
             ex.tick(t)
             t += 1
+            if t > ex.last:
+                start_stores()
+                stored = True
         gather_late.finish(phase)
         if phase < 3:
             gather_late.start(phase + 1)
@@ -809,8 +821,20 @@
     )(act, dbr, h2, dup, mixed, dat, dmix, qkv, e, h1, w, x, dmid, mw, cos, sin, mod, dmodb, te)
 
 
-def finish_kernel(early_ref, late_ref, bias_ref, tg_ref, te_ref, wg_ref, tout_ref, mb_ref, qb_ref, ob_ref, ub_ref, db_ref, flat):
+def finish_kernel(
+    early_ref, late_ref, bias_ref, tg_ref, te_ref, dw_in, uw_in, ow_in, qw_in, fg_in,
+    wg_hbm, tout_ref, mb_ref, qb_ref, ob_ref, ub_ref, db_ref, dw_out, uw_out, ow_out, qw_out, fg_out,
+    flat, wg_ref, dw, uw, ow, qw, fg, isem, osem,
+):
     rows, d = wg_ref.shape[0], wg_ref.shape[1] // 6
+    tile = fg.shape[0] // 8
+    cuts = [pl.ds(k * tile, tile) for k in range(8)]
+    through = [(dw_in, dw, dw_out), (uw_in, uw, uw_out), (ow_in, ow, ow_out), (qw_in, qw, qw_out)]
+    through += [(fg_in.at[c], fg.at[c], fg_out.at[c]) for c in cuts]
+    ins = [pltpu.make_async_copy(a, v, isem.at[k]) for k, (a, v, _) in enumerate(through)]
+    outs = [pltpu.make_async_copy(v, b, osem.at[k]) for k, (_, v, b) in enumerate(through)]
+    for c in ins:
+        c.start()
     g = lax.axis_index("groups")
     e, late = early_ref[...], late_ref[...]
     n = e.shape[0] // 16
@@ -826,6 +850,11 @@
         if r < 4 * d // STRIP:
             lo = 2 * d + r * STRIP
             wg_ref[:, lo : lo + STRIP] = mm(left, e, NN)
+    store_wg = pltpu.make_async_copy(wg_ref, wg_hbm, osem.at[len(outs)])
+    store_wg.start()
+    for a, b in zip(ins, outs):
+        a.wait()
+        b.start()
     flat[:16, :] = jnp.sum(late.astype(f32).reshape(n, 16, 128), axis=0)
     es = jnp.sum(e.astype(f32).reshape(n, 16, STRIP), axis=0)
     for r in range(4 * d // STRIP):
@@ -845,18 +874,28 @@
     t = te_ref[...].astype(f32)
     s = jax.nn.sigmoid(t)
     tout_ref[...] = tg_ref[...] * (s * (1.0 + t * (1.0 - s)))
-
-
-def finish(early, late, bias, tg, te, rows):
-    d = te.shape[1]
+    for c in outs:
+        c.wait()
+    store_wg.wait()
+
+
+def finish(early, late, bias, tg, te, *results):
+    rows, d = results[2].shape
     S = jax.ShapeDtypeStruct
+    hbm, vm = pl.BlockSpec(memory_space=pl.ANY), pl.BlockSpec(memory_space=pltpu.VMEM)
+    n = len(results)
     return pl.pallas_call(
         finish_kernel,
-        out_shape=[S((rows, 6 * d), f32), S((1, d), f32)] + [S((1, k * rows), f32) for k in (6, 3, 1, 2, 1)],
-        scratch_shapes=[pltpu.VMEM((56, 128), f32)],
+        in_specs=[vm] * 5 + [hbm] * n,
+        out_specs=[hbm] + [vm] * 6 + [hbm] * n,
+        out_shape=[S((rows, 6 * d), f32), S((1, d), f32)] + [S((1, k * rows), f32) for k in (6, 3, 1, 2, 1)]
+        + [S(r.shape, f32) for r in results],
+        scratch_shapes=[pltpu.VMEM((56, 128), f32), pltpu.VMEM((rows, 6 * d), f32)]
+        + [pltpu.VMEM(r.shape, f32) for r in results]
+        + [pltpu.SemaphoreType.DMA((n + 7,)), pltpu.SemaphoreType.DMA((n + 8,))],
         compiler_params=params(),
         name="finish",
-    )(early, late, bias, tg, te)
+    )(early, late, bias, tg, te, *results)
 
 
 def solution(mesh):
@@ -876,7 +915,9 @@
             groups, batch, act, dbr, h2, dup, mixed, dat, dmix, qkv, e, h1, qkv_w, x, dmid, mod_w, cos, sin, mod, dmod_b, te
         )
         rows, n = d // groups, groups * batch
-        mod_wg, time_grad, mb, qb, ob, ub, db = finish(early.reshape(n * 16, STRIP), late.reshape(n * 16, 128), bs, tg, te, rows)
+        mod_wg, time_grad, mb, qb, ob, ub, db, dws, uws, ows, qws, fg = finish(
+            early.reshape(n * 16, STRIP), late.reshape(n * 16, 128), bs, tg, te, dws, uws, ows, qws, fg
+        )
         return (out[None], fg[None], time_grad, mod_wg, mb[0], qws, qb[0], ows, ob[0], uws, ub[0], dws.reshape(2 * rows, d), db[0])
 
     split = P(("groups", "batch"))

time: 228 us -> 221 us (0.969)
  local copies, waits for them, and re-layouts: 11.9 us -> 3.76 us
    unnamed x21 -> x8, local copies, waits for them, and re-layouts: 8.14 us -> 0.02 us
    pallas_call x1, Pallas kernels: 3.98 us -> 6.78 us  [finish(): pl.pallas_call(finish_kernel, in_specs=[vm] * 5 + [hbm] * n, out_specs=[h...]
where the time goes in v5:
time: 221 us
  Pallas kernels  214 us (97%)
  local copies, waits for them, and re-layouts  3.76 us (2%)
    pallas_call x1, Pallas kernels, backward(): pl.pallas_call(lambda *a: back_kernel(groups, batch, per, n_chunks, *a),...  121 us
    pallas_call x1, Pallas kernels, middle_part(): pl.pallas_call(middle_kernel, grid_spec=pltpu.PrefetchScalarGridSpec(num_...  38.8 us
    pallas_call x1, Pallas kernels, attend(): pl.pallas_call(lambda *a: attend_kernel(*a, rows_at_once=rows_at_once), g...  27.7 us
    pallas_call x1, Pallas kernels, project_qkv(): pl.pallas_call(qkv_kernel, grid=(slots // tile,), in_specs=[row(d), full(...  12.7 us
    pallas_call x1, Pallas kernels, modulation(): pl.pallas_call(mod_kernel, grid=(n // blk,), in_specs=[full((1, d)), pl.B...  7.56 us
    pallas_call x1, Pallas kernels, finish(): pl.pallas_call(finish_kernel, in_specs=[vm] * 5 + [hbm] * n, out_specs=[h...  6.78 us

profile of v5, /device:TPU:0, one launch (start us, length us, event | category | flops | bytes accessed | tf_op | source)
XLA Modules:
  0.0 220.8 jit_solution(18293219984981447302)
XLA Ops:
  1.3 1.3 reshape.50.b_ref
  2.6 0.0 copy-start
  2.6 7.6 %modulation.1.mod_ref.a_16_ = f32[1,6144]{1,0:T(1,128)} custom-call(bf16[1,1024]{1,0:T(2,128)(2,1)} %te_ref.3, bf16[1024,6144]{1,0:T(8,128)(2,1)} %a_13_.1, bf16[1,6144]{1,0:T(2,128)(2,1)} %reshape.50.b_ref), custom_call_target="tpu_custom_call" | custom-call | tf_op jit(solution)/shard_map/modulation/pallas_call | solution.py:65
  10.2 0.0 copy-done
  10.2 0.6 reshape.51.b_ref
  10.8 12.7 %project_qkv.1 = (bf16[1024,1024]{1,0:T(8,128)(2,1)}, bf16[1024,3072]{1,0:T(8,128)(2,1)}, f32[1024,128]{1,0:T(8,128)}, f32[1024,128]{1,0:T(8,128)}) custom-call(bf16[1024,1024]{1,0:T(8,128)(2,1)} %bitcast.11, f32[1,6144]{1,0:T(1,128)} %modulation.1.mod_ref.a_16_, bf16[1024,3072]{1,0:T(8,128)(2,1)} %a_10_.1, bf16[1,3072]{1,0:T(2,128)(2,1)} %reshape.51.b_ref, ...), custom_call_target="tpu_custom_call" | custom-call | tf_op jit(solution)/shard_map/project_qkv/pallas_call | solution.py:106
  23.5 0.0 copy-start.2
  23.5 0.0 copy-start.1
  23.5 0.0 copy-start.3
  23.5 27.7 %attend.1 = (bf16[1024,1024]{1,0:T(8,128)(2,1)}, bf16[16,1024,1024]{2,1,0:T(8,128)(2,1)}, f32[1024,1024]{1,0:T(8,128)}) custom-call(s32[1]{0:T(128)S(6)} %copy.31.a_0_.len_ref, bf16[1024,3072]{1,0:T(8,128)(2,1)} %get-tuple-element.50.a_1_.a_2_.a_3_.a_7_, bf16[1024,3072]{1,0:T(8,128)(2,1)} %get-tuple-element.50.a_1_.a_2_.a_3_.a_7_, ...), custom_call_target="tpu_custom_call" | custom-call | tf_op jit(solution)/shard_map/attend/pallas_call | solution.py:148
  51.2 0.0 copy-done.2
  51.2 0.6 reshape.52.ob_ref
  51.8 0.0 copy-done.1
  51.8 0.6 reshape.53.ub_ref
  52.4 0.0 copy-done.3
  52.4 0.6 reshape.54.db_ref
  53.0 38.8 %middle_part.1 = (bf16[1024,1024]{1,0:T(8,128)(2,1)}, bf16[1024,1024]{1,0:T(8,128)(2,1)}, bf16[1024,2048]{1,0:T(8,128)(2,1)}, bf16[1024,1024]{1,0:T(8,128)(2,1)}...) custom-call(s32[1]{0:T(128)S(6)} %copy.31.a_0_.len_ref, ...), custom_call_target="tpu_custom_call" | custom-call | tf_op jit(solution)/shard_map/middle_part/pallas_call | solution.py:228
  91.9 120.9 %backward.1 = (f32[2,64,1024]{2,1,0:T(8,128)}, f32[64,2048]{1,0:T(8,128)}, f32[64,1024]{1,0:T(8,128)}, f32[64,3072]{1,0:T(8,128)}, f32[64,128]{1,0:T(8,128)}, /*...) custom-call(bf16[1024,2048]{1,0:T(8,128)(2,1)} %get-tuple-element.54, ...), custom_call_target="tpu_custom_call" | custom-call | tf_op jit(solution)/shard_map/backward/pallas_call | solution.py:803
  212.8 6.8 %finish.1 = (f32[64,6144]{1,0:T(8,128)}, f32[1,1024]{1,0:T(1,128)}, f32[1,384]{1,0:T(1,128)}, f32[1,192]{1,0:T(1,128)}, f32[1,64]{1,0:T(1,128)}, /*index=5*/f32[...) custom-call(bf16[512,512]{1,0:T(8,128)(2,1)} %bitcast.15, ...), custom_call_target="tpu_custom_call" | custom-call | tf_op jit(solution)/shard_map/finish/pallas_call | solution.py:887
  219.5 1.2 reduce
Async XLA Ops:
  2.6 7.6 %copy-start = (bf16[3072]{0:T(1024)(128)(2,1)S(1)}, bf16[3072]{0:T(1024)(128)(2,1)}, u32[]{:S(2)}) copy-start(bf16[3072]{0:T(1024)(128)(2,1)} %param.24) | copy-start | bytes 18436
  23.5 27.7 %copy-start.2 = (bf16[1024]{0:T(1024)(128)(2,1)S(1)}, bf16[1024]{0:T(1024)(128)(2,1)}, u32[]{:S(2)}) copy-start(bf16[1024]{0:T(1024)(128)(2,1)} %param.26) | copy-start | bytes 6148
  23.5 28.3 %copy-start.1 = (bf16[2048]{0:T(1024)(128)(2,1)S(1)}, bf16[2048]{0:T(1024)(128)(2,1)}, u32[]{:S(2)}) copy-start(bf16[2048]{0:T(1024)(128)(2,1)} %param.28) | copy-start | bytes 12292
  23.5 28.9 %copy-start.3 = (bf16[1024]{0:T(1024)(128)(2,1)S(1)}, bf16[1024]{0:T(1024)(128)(2,1)}, u32[]{:S(2)}) copy-start(bf16[1024]{0:T(1024)(128)(2,1)} %param.30) | copy-start | bytes 6148

commit v6 on v5

--- a/solution.py
+++ b/solution.py
@@ -50,6 +50,10 @@
 
 def full(shape):
     return pl.BlockSpec(shape, lambda *_: (0,) * len(shape), pipeline_mode=pl.Buffered(1))
+
+
+def part(b, n, k):
+    return pl.BlockSpec((1, n), lambda *_: (0, k), pipeline_mode=pl.Buffered(1))
 
 
 def mod_kernel(te_ref, w_ref, b_ref, out_ref):
@@ -106,7 +110,7 @@
     return pl.pallas_call(
         qkv_kernel,
         grid=(slots // tile,),
-        in_specs=[row(d), full(mod.shape), full(w.shape), full(b.shape)]
+        in_specs=[row(d), full(mod.shape), full(w.shape), part(b, 3 * d, 0)]
         + [pl.BlockSpec((tile // BLOCK, 128), lambda i: (i, 0))] * 2 + [full((BLOCK, 128))] * 2,
         out_specs=[row(d), row(3 * d), row(128), row(128)],
         out_shape=[jax.ShapeDtypeStruct((slots, d), bf16), jax.ShapeDtypeStruct((slots, 3 * d), bf16),
@@ -220,7 +224,7 @@
         dmod_ref[...] += part
 
 
-def middle_part(length, mixed, x, cot, mod, linv, ow, ob, uw, ub, dw, db, tile=256):
+def middle_part(length, mixed, x, cot, mod, linv, ow, uw, dw, b, tile=256):
     slots, d = x.shape
     ff = uw.shape[1]
     row = lambda n: pl.BlockSpec((tile, n), lambda i, n_: (i, 0))
@@ -230,8 +234,8 @@
         grid_spec=pltpu.PrefetchScalarGridSpec(
             num_scalar_prefetch=1,
             grid=(slots // tile,),
-            in_specs=[row(d), row(d), row(d), full(mod.shape), row(d), full(ow.shape), full(ob.shape),
-                      full(uw.shape), full(ub.shape), full(dw.shape), full(db.shape)],
+            in_specs=[row(d), row(d), row(d), full(mod.shape), row(d), full(ow.shape), part(b, d, 3),
+                      full(uw.shape), part(b, 2 * d, 2), full(dw.shape), part(b, d, 6)],
             out_specs=[row(d), row(d), row(ff), row(d), row(ff), row(d), row(d), row(d),
                        pl.BlockSpec((1, 4 * d), lambda i, n_: (0, 0))],
         ),
@@ -240,7 +244,7 @@
                    S((1, 4 * d), f32)],
         compiler_params=params(),
         name="middle_part",
-    )(length, mixed, x, cot, mod, linv, ow, ob, uw, ub, dw, db)
+    )(length, mixed, x, cot, mod, linv, ow, b, uw, b, dw, b)
 
 
 MESH = pl.DeviceIdType.MESH
@@ -905,11 +909,12 @@
         x, ct = frames[0], cot[0]
         slots, d = x.shape
         row = lambda b: b.reshape(1, -1)
+        biases = row(jnp.concatenate([qkv_b, out_b, up_b, down_b]))
         mod = modulation(te, mod_w, row(mod_b))
-        h1, qkv, cos, sin = project_qkv(x, mod, qkv_w, row(qkv_b), rot_tables(slots, d // HEADS))
+        h1, qkv, cos, sin = project_qkv(x, mod, qkv_w, biases, rot_tables(slots, d // HEADS))
         mixed, e, linv = attend(lengths, qkv)
         out, h2, act, dbr, dup, dat, dmix, dmid, dmod_b = middle_part(
-            lengths, mixed, x, ct, mod, linv, out_w, row(out_b), up_w, row(up_b), down_w, row(down_b)
+            lengths, mixed, x, ct, mod, linv, out_w, up_w, down_w, biases
         )
         dws, uws, ows, qws, bs, early, late, fg, tg = backward(
             groups, batch, act, dbr, h2, dup, mixed, dat, dmix, qkv, e, h1, qkv_w, x, dmid, mod_w, cos, sin, mod, dmod_b, te

time: 221 us -> 219 us (level)
  no operation moved by 1% of the time
where the time goes in v6:
time: 219 us
  Pallas kernels  214 us (98%)
    pallas_call x1, Pallas kernels, backward(): pl.pallas_call(lambda *a: back_kernel(groups, batch, per, n_chunks, *a),...  121 us
    pallas_call x1, Pallas kernels, middle_part(): pl.pallas_call(middle_kernel, grid_spec=pltpu.PrefetchScalarGridSpec(num_...  38.7 us
    pallas_call x1, Pallas kernels, attend(): pl.pallas_call(lambda *a: attend_kernel(*a, rows_at_once=rows_at_once), g...  27.7 us
    pallas_call x1, Pallas kernels, project_qkv(): pl.pallas_call(qkv_kernel, grid=(slots // tile,), in_specs=[row(d), full(...  12.7 us
    pallas_call x1, Pallas kernels, modulation(): pl.pallas_call(mod_kernel, grid=(n // blk,), in_specs=[full((1, d)), pl.B...  7.6 us
    pallas_call x1, Pallas kernels, finish(): pl.pallas_call(finish_kernel, in_specs=[vm] * 5 + [hbm] * n, out_specs=[h...  6.78 us

profile of v6, /device:TPU:0, one launch (start us, length us, event | category | flops | bytes accessed | tf_op | source)
XLA Modules:
  0.0 219.0 jit_solution(16318129921132854691)
XLA Ops:
  1.3 1.3 reshape.41.b_ref
  2.6 0.0 copy-start
  2.6 0.0 copy-start.1
  2.6 0.0 copy-start.2
  2.6 0.0 copy-start.3
  2.6 7.6 %modulation.1.mod_ref.a_16_ = f32[1,6144]{1,0:T(1,128)} custom-call(bf16[1,1024]{1,0:T(2,128)(2,1)} %te_ref.3, bf16[1024,6144]{1,0:T(8,128)(2,1)} %a_13_.1, bf16[1,6144]{1,0:T(2,128)(2,1)} %reshape.41.b_ref), custom_call_target="tpu_custom_call" | custom-call | tf_op jit(solution)/shard_map/modulation/pallas_call | solution.py:69
  10.2 0.0 copy-done
  10.2 0.0 copy-done.1
  10.2 0.0 copy-done.2
  10.3 0.0 copy-done.3
  10.3 0.6 reshape.42.b_ref.ob_ref.ub_ref.db_ref
  10.9 12.7 %project_qkv.1 = (bf16[1024,1024]{1,0:T(8,128)(2,1)}, bf16[1024,3072]{1,0:T(8,128)(2,1)}, f32[1024,128]{1,0:T(8,128)}, f32[1024,128]{1,0:T(8,128)}) custom-call(bf16[1024,1024]{1,0:T(8,128)(2,1)} %bitcast.11, f32[1,6144]{1,0:T(1,128)} %modulation.1.mod_ref.a_16_, bf16[1024,3072]{1,0:T(8,128)(2,1)} %a_10_.1, ...), custom_call_target="tpu_custom_call" | custom-call | tf_op jit(solution)/shard_map/project_qkv/pallas_call | solution.py:110
  23.6 27.7 %attend.1 = (bf16[1024,1024]{1,0:T(8,128)(2,1)}, bf16[16,1024,1024]{2,1,0:T(8,128)(2,1)}, f32[1024,1024]{1,0:T(8,128)}) custom-call(s32[1]{0:T(128)S(6)} %copy.31.a_0_.len_ref, bf16[1024,3072]{1,0:T(8,128)(2,1)} %get-tuple-element.50.a_1_.a_2_.a_3_.a_7_, bf16[1024,3072]{1,0:T(8,128)(2,1)} %get-tuple-element.50.a_1_.a_2_.a_3_.a_7_, ...), custom_call_target="tpu_custom_call" | custom-call | tf_op jit(solution)/shard_map/attend/pallas_call | solution.py:152
  51.3 38.7 %middle_part.1 = (bf16[1024,1024]{1,0:T(8,128)(2,1)}, bf16[1024,1024]{1,0:T(8,128)(2,1)}, bf16[1024,2048]{1,0:T(8,128)(2,1)}, bf16[1024,1024]{1,0:T(8,128)(2,1)}...) custom-call(s32[1]{0:T(128)S(6)} %copy.31.a_0_.len_ref, ...), custom_call_target="tpu_custom_call" | custom-call | tf_op jit(solution)/shard_map/middle_part/pallas_call | solution.py:232
  90.1 120.9 %backward.1 = (f32[2,64,1024]{2,1,0:T(8,128)}, f32[64,2048]{1,0:T(8,128)}, f32[64,1024]{1,0:T(8,128)}, f32[64,3072]{1,0:T(8,128)}, f32[64,128]{1,0:T(8,128)}, /*...) custom-call(bf16[1024,2048]{1,0:T(8,128)(2,1)} %get-tuple-element.54, ...), custom_call_target="tpu_custom_call" | custom-call | tf_op jit(solution)/shard_map/backward/pallas_call | solution.py:807
  210.9 6.8 %finish.1 = (f32[64,6144]{1,0:T(8,128)}, f32[1,1024]{1,0:T(1,128)}, f32[1,384]{1,0:T(1,128)}, f32[1,192]{1,0:T(1,128)}, f32[1,64]{1,0:T(1,128)}, /*index=5*/f32[...) custom-call(bf16[512,512]{1,0:T(8,128)(2,1)} %bitcast.15, ...), custom_call_target="tpu_custom_call" | custom-call | tf_op jit(solution)/shard_map/finish/pallas_call | solution.py:891
  217.7 1.3 reduce
  (1 shorter events, 0.0 us)
Async XLA Ops:
  2.6 7.6 %copy-start = (bf16[3072]{0:T(1024)(128)(2,1)S(1)}, bf16[3072]{0:T(1024)(128)(2,1)}, u32[]{:S(2)}) copy-start(bf16[3072]{0:T(1024)(128)(2,1)} %param.24) | copy-start | bytes 18436
  2.6 7.6 %copy-start.1 = (bf16[2048]{0:T(1024)(128)(2,1)S(1)}, bf16[2048]{0:T(1024)(128)(2,1)}, u32[]{:S(2)}) copy-start(bf16[2048]{0:T(1024)(128)(2,1)} %param.28) | copy-start | bytes 12292
  2.6 7.6 %copy-start.2 = (bf16[1024]{0:T(1024)(128)(2,1)S(1)}, bf16[1024]{0:T(1024)(128)(2,1)}, u32[]{:S(2)}) copy-start(bf16[1024]{0:T(1024)(128)(2,1)} %param.30) | copy-start | bytes 6148
  2.6 7.6 %copy-start.3 = (bf16[1024]{0:T(1024)(128)(2,1)S(1)}, bf16[1024]{0:T(1024)(128)(2,1)}, u32[]{:S(2)}) copy-start(bf16[1024]{0:T(1024)(128)(2,1)} %param.26) | copy-start | bytes 6148
